TPU v7x, 128 devices: a whole 4x4x4 slice. The times are simulated.
128 devices in a mesh: space: 16 (over z, x), bins: 8 (over y, core).
Axes of the slice: x: 4, y: 4, z: 4, core: 2. Of those that a mesh axis runs over, the one named last changes fastest.
Arguments:
- spectrum: bfloat16 [1152, 384, 256], P('bins', 'space'), may hold values from 0.099609375 to 2
- group_speed: float32 [2, 1152], P(None, 'bins'), may hold values from -0.3 to 0.3
- stokes_kernel: bfloat16 [1152, 128], P('bins'), may hold values from -0.1875 to 0.1875
- pair_bins: int32 [3, 4608], replicated, may hold values from 0 to 1151
- pair_coef: float32 [4608], replicated, may hold values from -3 to 3
- currents: float32 [256, 384, 128], P(('space', 'bins')), may hold values from -6 to 6
- col_map: int32 [128], replicated, may hold values from 0 to 127, each once
- wave_wet: int32 [384, 256], P('space'), may hold values 0 or 1
- ocean_wet: int32 [256, 384], P(('space', 'bins')), may hold values 0 or 1
Outputs:
- new_spectrum: bfloat16 [1152, 384, 256], P(None, ('space', 'bins'))
- new_currents: float32 [256, 384, 128], P(('space', 'bins'))
All inputs are finite; a program needn't handle non-finite values. No bound on the sum of `wave_wet` or of `ocean_wet` on one device may be relied on, other than what follows from the above.
Results may differ from a plain program's by a relative error of at most 0.0052.
Values may be sent and summed in bfloat16 or wider, within the bound.
No kernel may reach another device: no remote copies, remote signals or barrier semaphores. Data moves between devices by JAX's collectives and lax.ppermute only.
A program may use at most 64 MiB of HBM per device.

v0:
```python
import jax
import jax.numpy as jnp
from jax import lax
from jax.sharding import PartitionSpec as P

DT_OCEAN = 0.5
CORIOLIS = 0.8
MIXING = 0.4
CURRENT_SCALE = 0.15
DT_SOURCE = 0.5


def copy_for_each(x, axis):
    copies = jnp.broadcast_to(x, (lax.axis_size(axis), *x.shape))
    return lax.all_to_all(copies, axis, split_axis=0, concat_axis=0, tiled=True)


def joined_along(parts, dim):
    dims = list(parts.shape[1:])
    dims[dim] *= parts.shape[0]
    return jnp.moveaxis(parts, 0, dim).reshape(dims)


def collect(x, axis, dim):
    parts = copy_for_each(x, axis)
    return joined_along(parts, dim)


def shifted(value, axis, steps):
    count = lax.axis_size(axis)
    first, last = (max(0, -steps), min(count, count - steps))
    return lax.ppermute(value, axis, [(source, source + steps) for source in range(first, last)])


def levels_laplacian(field):
    upper = jnp.concatenate([field[..., :1], field[..., :-1]], axis=-1)
    lower = jnp.concatenate([field[..., 1:], field[..., -1:]], axis=-1)
    return upper + lower - 2.0 * field


def ocean_step(currents, drift, wet, levels):
    east = currents[..., :levels]
    north = currents[..., levels:]
    east_drift = drift[..., :levels]
    north_drift = drift[..., levels:]
    new_east = east + DT_OCEAN * (
        CORIOLIS * (north + north_drift) + MIXING * levels_laplacian(east)
    )
    new_north = north + DT_OCEAN * (
        -CORIOLIS * (east + east_drift) + MIXING * levels_laplacian(north)
    )
    return wet[..., None].astype(jnp.float32) * jnp.concatenate([new_east, new_north], axis=-1)


def fluxes(energy, speeds, cur):
    speed_x = speeds[0][:, None, None] + cur[0][None]
    speed_y = speeds[1][:, None, None] + cur[1][None]
    plus_x = jnp.maximum(speed_x, 0.0) * energy
    minus_x = jnp.minimum(speed_x, 0.0) * energy
    plus_y = jnp.maximum(speed_y, 0.0) * energy
    minus_y = jnp.minimum(speed_y, 0.0) * energy
    return (plus_x, minus_x, plus_y, minus_y)


def combine(energy, flux_set, below, above, wet):
    plus_x, minus_x, plus_y, minus_y = flux_set
    plus_x_prev = jnp.concatenate([below[:, None, :], plus_x[:, :-1, :]], axis=1)
    minus_x_next = jnp.concatenate([minus_x[:, 1:, :], above[:, None, :]], axis=1)
    plus_y_prev = jnp.pad(plus_y[:, :, :-1], ((0, 0), (0, 0), (1, 0)))
    minus_y_next = jnp.pad(minus_y[:, :, 1:], ((0, 0), (0, 0), (0, 1)))
    moved = energy.astype(jnp.float32) - plus_x + plus_x_prev - minus_x_next + minus_x
    moved = moved - plus_y + plus_y_prev - minus_y_next + minus_y
    return (wet.astype(jnp.float32)[None] * moved).astype(jnp.bfloat16)


def per_device(
    spectrum,
    group_speed,
    stokes_kernel,
    pair_bins,
    pair_coef,
    currents,
    col_map,
    wave_wet,
    ocean_wet,
):
    local_bins, tile_rows, columns = spectrum.shape
    space_count = lax.axis_size("space")
    bins_count = lax.axis_size("bins")
    groups = space_count * bins_count
    group_cols = columns // groups
    levels = stokes_kernel.shape[1] // 2
    slot_col = (
        col_map[:, None] * group_cols + jnp.arange(group_cols, dtype=jnp.int32)[None, :]
    ).reshape(-1)
    inverse = jnp.argsort(slot_col)
    pair_total = pair_bins.shape[1]
    block_pairs = pair_total // 4
    first_bins = pair_bins[0].reshape(4, block_pairs)
    second_bins = pair_bins[1].reshape(4, block_pairs)
    target_bins = pair_bins[2].reshape(4, block_pairs)
    coef_blocks = pair_coef.reshape(4, block_pairs)
    partial_value = jnp.einsum(
        "kxc,kl->cxl", spectrum, stokes_kernel, preferred_element_type=jnp.float32
    )
    routed = jnp.take(partial_value, slot_col, axis=0)
    arrived = lax.all_to_all(
        routed.astype(jnp.bfloat16), ("space", "bins"), split_axis=0, concat_axis=1, tiled=True
    ).astype(routed.dtype)
    drift = jnp.sum(
        arrived.reshape(group_cols, space_count, bins_count, tile_rows, 2 * levels), axis=2
    )
    drift = drift.reshape(group_cols, space_count * tile_rows, 2 * levels)
    new_currents = ocean_step(currents, drift, ocean_wet, levels)
    surface = jnp.stack([new_currents[:, :, 0], new_currents[:, :, levels]])
    routed_rows = lax.all_to_all(
        surface, ("space", "bins"), split_axis=2, concat_axis=1, tiled=True
    )
    slotted = collect(routed_rows, "bins", 2)
    cur = CURRENT_SCALE * jnp.tanh(jnp.transpose(jnp.take(slotted, inverse, axis=1), (0, 2, 1)))
    flux_set = fluxes(spectrum, group_speed, cur)
    below = shifted(flux_set[0][:, -1, :].astype(jnp.bfloat16), "space", 1).astype(jnp.float32)
    above = shifted(flux_set[1][:, 0, :].astype(jnp.bfloat16), "space", -1).astype(jnp.float32)
    advected = combine(spectrum, flux_set, below, above, wave_wet)
    whole = lax.all_to_all(advected, "bins", split_axis=1, concat_axis=0, tiled=True)
    all_bins, some_rows, some_cols = whole.shape
    flat = whole.reshape(all_bins, some_rows * some_cols)
    bin_ids = jnp.arange(all_bins, dtype=jnp.int32)

    def one_block(total, tables):
        first_ids, second_ids, target_ids, coefs = tables
        first = jnp.take(flat, first_ids, axis=0).astype(jnp.float32)
        second = jnp.take(flat, second_ids, axis=0).astype(jnp.float32)
        products = (coefs[:, None] * first * second).astype(jnp.bfloat16)
        onehot = (bin_ids[:, None] == target_ids[None, :]).astype(jnp.bfloat16)
        return (total + jnp.dot(onehot, products, preferred_element_type=jnp.float32), None)

    start = jnp.zeros((all_bins, some_rows * some_cols), jnp.float32)
    source, _ = lax.scan(one_block, start, (first_bins, second_bins, target_bins, coef_blocks))
    updated = (flat.astype(jnp.float32) + DT_SOURCE * source).astype(jnp.bfloat16)
    new_spectrum = updated.reshape(all_bins, some_rows, some_cols)
    return (new_spectrum, new_currents)


def solution(mesh):
    placed = (
        P("bins", "space", None),
        P(None, "bins"),
        P("bins", None),
        P(),
        P(),
        P(("space", "bins"), None, None),
        P(),
        P("space", None),
        P(("space", "bins"), None),
    )
    return jax.shard_map(
        per_device,
        mesh=mesh,
        in_specs=placed,
        out_specs=(P(None, ("space", "bins"), None), P(("space", "bins"), None, None)),
        check_vma=False,
    )
```

profile of v0, /device:TPU:1, one launch (start us, length us, event | category | flops | bytes accessed | tf_op | source)
XLA Modules:
  0.0 199.9 jit_solution(397441468630240345)
XLA Ops:
  0.6 0.7 broadcast_multiply_fusion
  1.3 0.1 iota_add_fusion
  1.4 0.1 add.150
  1.5 0.1 add.154
  1.7 2.1 %convolution_bitcast_fusion = bf16[256,24,128]{0,2,1:T(8,128)(2,1)S(1)} fusion(bf16[144,24,256]{2,1,0:T(8,128)(2,1)} %param.13, bf16[144,128]{1,0:T(8,128)(2,1)S(1)} %copy-done), kind=kOutput, calls=%fused_computation.48 | convolution fusion | flops 226492416 | bytes 3379200 | tf_op jit(solution)/shard_map/kxc,kl->cxl/dot_general | solution.py:103
  3.8 1.1 copy.59
  5.0 1.0 gather_fusion.2
  6.0 1.8 select_convert_fusion
  7.8 11.5 %all-to-all-start = ((bf16[256,24,128]{2,1,0:T(8,128)(2,1)}), bf16[256,24,128]{2,1,0:T(8,128)(2,1)S(1)}, u32[]{:S(2)}, u32[]{:S(2)}) async-start(bf16[256,24,128]{2,1,0:T(8,128)(2,1)} %select_convert_fusion), calls=%async_computation | async-start | bytes 3145728 | tf_op jit(solution)/shard_map/all_to_all | solution.py:107
  19.3 3.2 %sort.17 = (s32[256]{0:T(256)}, s32[256]{0:T(256)S(1)}) sort(s32[256]{0:T(256)S(1)} %add.150, s32[256]{0:T(256)S(1)} %iota.11), dimensions={0}, to_apply=%region_0.0 | sort | flops 2048 | bytes 4096 | tf_op jit(solution)/shard_map/jit(argsort)/sort | solution.py:96
  22.5 1.1 fusion.37
  23.6 1.5 fusion.38
  25.1 18.5 %all-to-all-done = bf16[256,24,128]{2,1,0:T(8,128)(2,1)S(1)} async-done(((bf16[256,24,128]{2,1,0:T(8,128)(2,1)}), bf16[256,24,128]{2,1,0:T(8,128)(2,1)S(1)}, u32[]{:S(2)}, u32[]{:S(2)}) %all-to-all-start) | async-done | bytes 1572896 | tf_op jit(solution)/shard_map/all_to_all | solution.py:107
  43.7 0.2 bitcast_convert_fusion
  43.9 0.2 bitcast_reduce_fusion
  44.2 0.5 copy-done.4
  44.7 0.1 copy-done.5
  44.8 0.1 copy-done.6
  44.9 0.1 copy-done.7
  45.0 0.1 copy-done.8
  45.1 0.7 fusion.29
  45.9 0.3 maximum_multiply_fusion
  46.2 0.4 slice_reduce_fusion.1
  46.6 0.9 copy.61
  47.5 4.8 %all-to-all-start.1 = ((f32[2,2,384]{1,0,2:T(2,128)}), f32[2,2,384]{1,0,2:T(2,128)S(1)}, u32[]{:S(2)}, u32[]{:S(2)}) async-start(f32[2,2,384]{1,0,2:T(2,128)} %copy.61), calls=%async_computation.1 | async-start | bytes 786432 | tf_op jit(solution)/shard_map/all_to_all | solution.py:116
  52.4 12.3 %all-to-all-done.1 = f32[2,2,384]{1,0,2:T(2,128)S(1)} async-done(((f32[2,2,384]{1,0,2:T(2,128)}), f32[2,2,384]{1,0,2:T(2,128)S(1)}, u32[]{:S(2)}, u32[]{:S(2)}) %all-to-all-start.1) | async-done | bytes 6176 | tf_op jit(solution)/shard_map/all_to_all | solution.py:116
  64.7 0.3 all_to_all.38
  65.0 0.6 broadcast_in_dim.59
  65.6 4.2 %all-to-all-start.2 = ((f32[8,2,256,3]{2,1,3,0:T(2,128)}), f32[8,2,256,3]{2,1,3,0:T(2,128)S(1)}, u32[]{:S(2)}, u32[]{:S(2)}) async-start(f32[8,2,256,3]{2,1,3,0:T(2,128)} %broadcast_in_dim.59), calls=%async_computation.2 | async-start | bytes 98304 | tf_op jit(solution)/shard_map/all_to_all | solution.py:15
  69.9 4.8 %all-to-all-done.2 = f32[8,2,256,3]{2,1,3,0:T(2,128)S(1)} async-done(((f32[8,2,256,3]{2,1,3,0:T(2,128)}), f32[8,2,256,3]{2,1,3,0:T(2,128)S(1)}, u32[]{:S(2)}, u32[]{:S(2)}) %all-to-all-start.2) | async-done | bytes 49184 | tf_op jit(solution)/shard_map/all_to_all | solution.py:15
  74.6 0.2 copy.64
  74.8 1.0 gather_fusion.3
  75.8 0.3 multiply_bitcast_fusion
  76.1 0.2 fusion.39
  76.4 0.1 copy.66
  76.5 2.1 %convert_multiply_fusion.1 = (f32[144,24,256]{2,0,1:T(8,128)S(1)}, f32[144,24,256]{2,0,1:T(8,128)S(1)}, f32[144,24,256]{2,0,1:T(8,128)S(1)}, f32[144,24,256]{2,0,1:T(8,128)S(1)}) fusion(f32[24,256]{1,0:T(8,128)S(1)} %copy.66, f32[144]{0:T(256)S(1)} %bitcast.65, bf16[144,24,256]{2,1,0:T(8,128)(2,1)S(1)} %copy-done.2, f32[24,256]{1,0:T(8,128)S(1)} %copy.65, ...), kind=kLoop, calls=%fused_computation.28 | loop fusion | flops 9732096 | bytes 15975552 | tf_op jit(solution)/shard_map/mul | solution.py:60
  78.6 1.3 collective-permute-start.1
  80.0 0.2 slice.132
  80.2 0.2 slice.133
  80.4 1.0 slice.137
  81.4 4.2 %collective-permute-start = (bf16[144,256]{1,0:T(8,128)(2,1)S(1)}, bf16[144,256]{1,0:T(8,128)(2,1)S(1)}, u32[]{:S(2)}, u32[]{:S(2)}) collective-permute-start(bf16[144,256]{1,0:T(8,128)(2,1)S(1)} %fusion.34), channel_id=1, source_target_pairs={{0,8},{8,16},{16,24},{24,32},{32,40},{40,48},{48,56},{56,64},{64,7... | collective-permute-start | bytes 221192 | tf_op jit(solution)/shard_map/ppermute | solution.py:32
  85.6 1.2 collective-permute-done
  86.8 4.0 %fusion.20 = bf16[144,24,256]{2,0,1:T(8,128)(2,1)} fusion(f32[144,23,256]{2,0,1:T(8,128)S(1)} %slice.132, f32[144,1,256]{2,0,1:T(8,128)S(1)} %bitcast_convert_fusion.2, f32[144,1,256]{2,0,1:T(8,128)S(1)} %bitcast_convert_fusion.1, f32[144,23,256]{2,0,1:T(8,128)S(1)} %slice.133, f32[144,24,255]{2,0,1:T(8,128)S(1)} %slice.137, ...), kind=kLoop, calls=%fused_computation.44 | loop fusion | flops 20348928 | bytes 17741952 | tf_op jit(solution)/shard_map/convert_element_type | solution.py:73
  90.8 5.5 %all-to-all-start.3 = ((bf16[144,24,256]{2,0,1:T(8,128)(2,1)}), bf16[144,24,256]{2,0,1:T(8,128)(2,1)S(1)}, u32[]{:S(2)}, u32[]{:S(2)}) async-start(bf16[144,24,256]{2,0,1:T(8,128)(2,1)} %fusion.20), calls=%async_computation.3 | async-start | bytes 3538944 | tf_op jit(solution)/shard_map/all_to_all | solution.py:125
  96.3 0.1 slice_reduce_fusion.2
  96.5 22.5 %all-to-all-done.3 = bf16[144,24,256]{2,0,1:T(8,128)(2,1)S(1)} async-done(((bf16[144,24,256]{2,0,1:T(8,128)(2,1)}), bf16[144,24,256]{2,0,1:T(8,128)(2,1)S(1)}, u32[]{:S(2)}, u32[]{:S(2)}) %all-to-all-start.3) | async-done | bytes 1769504 | tf_op jit(solution)/shard_map/all_to_all | solution.py:125
  119.0 1.2 copy.67
  120.3 0.5 copy.72
  120.7 70.5 %while.11 = (s32[]{:T(128)}, f32[1152,768]{1,0:T(8,128)}, s32[4,1152]{1,0:T(4,128)S(1)}, f32[4,1152]{1,0:T(4,128)S(1)}, s32[4,1152]{1,0:T(4,128)S(1)}, /*index=5...) while((s32[]{:T(128)}, f32[1152,768]{1,0:T(8,128)}, ...), condition=%wide.region_3.5_spmd.clone, body=%wide.region_2.4_spmd.clone.sunk | while | flops 2047746304 | bytes 17807988 | solution.py:139
  120.8 4.8 %gather_fusion = bf16[1152,768]{1,0:T(8,128)(2,1)} fusion(bf16[1152,768]{1,0:T(8,128)(2,1)S(1)} %get-tuple-element.193, s32[2048]{0:T(1024)S(1)} %pad_clamp_fusion.6), kind=kCustom, calls=%fused_computation.1.clone.clone.1 | custom fusion | bytes 3543552 | tf_op jit(solution)/shard_map/while/body/eval_jaxpr/jit(_take)/gather | solution.py:133
  125.6 4.8 %gather_fusion.1 = bf16[1152,768]{1,0:T(8,128)(2,1)} fusion(bf16[1152,768]{1,0:T(8,128)(2,1)S(1)} %get-tuple-element.193, s32[2048]{0:T(1024)S(1)} %pad_clamp_fusion.7), kind=kCustom, calls=%fused_computation.clone.clone.1 | custom fusion | bytes 3543552 | tf_op jit(solution)/shard_map/while/body/eval_jaxpr/jit(_take)/gather | solution.py:132
  130.5 7.0 %fusion.42 = f32[1152,768]{1,0:T(8,128)} fusion(f32[1152,768]{1,0:T(8,128)} %get-tuple-element.180, s32[1152]{0:T(1024)S(1)} %dynamic-slice_reduce_fusion.7, bf16[1152,768]{1,0:T(8,128)(2,1)} %gather_fusion, bf16[1152,768]{1,0:T(8,128)(2,1)} %gather_fusion.1, f32[1152]{0:T(1024)S(1)} %dynamic-slice_reduce_fusion.9, ...), kind=kOutput, calls=%fused_computation.7.clone.1 | convolution fusion | flops 2047721472 | bytes 10628353 | tf_op jit(solution)/shard_map/while/body/eval_jaxpr/dot_general | solution.py:136
  137.6 4.8 %gather_fusion = bf16[1152,768]{1,0:T(8,128)(2,1)} fusion(bf16[1152,768]{1,0:T(8,128)(2,1)S(1)} %get-tuple-element.193, s32[2048]{0:T(1024)S(1)} %pad_clamp_fusion.6), kind=kCustom, calls=%fused_computation.1.clone.clone.1 | custom fusion | bytes 3543552 | tf_op jit(solution)/shard_map/while/body/eval_jaxpr/jit(_take)/gather | solution.py:133
  142.5 4.8 %gather_fusion.1 = bf16[1152,768]{1,0:T(8,128)(2,1)} fusion(bf16[1152,768]{1,0:T(8,128)(2,1)S(1)} %get-tuple-element.193, s32[2048]{0:T(1024)S(1)} %pad_clamp_fusion.7), kind=kCustom, calls=%fused_computation.clone.clone.1 | custom fusion | bytes 3543552 | tf_op jit(solution)/shard_map/while/body/eval_jaxpr/jit(_take)/gather | solution.py:132
  147.4 8.1 %fusion.42 = f32[1152,768]{1,0:T(8,128)} fusion(f32[1152,768]{1,0:T(8,128)} %get-tuple-element.180, s32[1152]{0:T(1024)S(1)} %dynamic-slice_reduce_fusion.7, bf16[1152,768]{1,0:T(8,128)(2,1)} %gather_fusion, bf16[1152,768]{1,0:T(8,128)(2,1)} %gather_fusion.1, f32[1152]{0:T(1024)S(1)} %dynamic-slice_reduce_fusion.9, ...), kind=kOutput, calls=%fused_computation.7.clone.1 | convolution fusion | flops 2047721472 | bytes 10628353 | tf_op jit(solution)/shard_map/while/body/eval_jaxpr/dot_general | solution.py:136
  155.5 4.8 %gather_fusion = bf16[1152,768]{1,0:T(8,128)(2,1)} fusion(bf16[1152,768]{1,0:T(8,128)(2,1)S(1)} %get-tuple-element.193, s32[2048]{0:T(1024)S(1)} %pad_clamp_fusion.6), kind=kCustom, calls=%fused_computation.1.clone.clone.1 | custom fusion | bytes 3543552 | tf_op jit(solution)/shard_map/while/body/eval_jaxpr/jit(_take)/gather | solution.py:133
  160.3 4.8 %gather_fusion.1 = bf16[1152,768]{1,0:T(8,128)(2,1)} fusion(bf16[1152,768]{1,0:T(8,128)(2,1)S(1)} %get-tuple-element.193, s32[2048]{0:T(1024)S(1)} %pad_clamp_fusion.7), kind=kCustom, calls=%fused_computation.clone.clone.1 | custom fusion | bytes 3543552 | tf_op jit(solution)/shard_map/while/body/eval_jaxpr/jit(_take)/gather | solution.py:132
  165.3 8.1 %fusion.42 = f32[1152,768]{1,0:T(8,128)} fusion(f32[1152,768]{1,0:T(8,128)} %get-tuple-element.180, s32[1152]{0:T(1024)S(1)} %dynamic-slice_reduce_fusion.7, bf16[1152,768]{1,0:T(8,128)(2,1)} %gather_fusion, bf16[1152,768]{1,0:T(8,128)(2,1)} %gather_fusion.1, f32[1152]{0:T(1024)S(1)} %dynamic-slice_reduce_fusion.9, ...), kind=kOutput, calls=%fused_computation.7.clone.1 | convolution fusion | flops 2047721472 | bytes 10628353 | tf_op jit(solution)/shard_map/while/body/eval_jaxpr/dot_general | solution.py:136
  173.4 4.8 %gather_fusion = bf16[1152,768]{1,0:T(8,128)(2,1)} fusion(bf16[1152,768]{1,0:T(8,128)(2,1)S(1)} %get-tuple-element.193, s32[2048]{0:T(1024)S(1)} %pad_clamp_fusion.6), kind=kCustom, calls=%fused_computation.1.clone.clone.1 | custom fusion | bytes 3543552 | tf_op jit(solution)/shard_map/while/body/eval_jaxpr/jit(_take)/gather | solution.py:133
  178.2 4.8 %gather_fusion.1 = bf16[1152,768]{1,0:T(8,128)(2,1)} fusion(bf16[1152,768]{1,0:T(8,128)(2,1)S(1)} %get-tuple-element.193, s32[2048]{0:T(1024)S(1)} %pad_clamp_fusion.7), kind=kCustom, calls=%fused_computation.clone.clone.1 | custom fusion | bytes 3543552 | tf_op jit(solution)/shard_map/while/body/eval_jaxpr/jit(_take)/gather | solution.py:132
  183.1 8.1 %fusion.42 = f32[1152,768]{1,0:T(8,128)} fusion(f32[1152,768]{1,0:T(8,128)} %get-tuple-element.180, s32[1152]{0:T(1024)S(1)} %dynamic-slice_reduce_fusion.7, bf16[1152,768]{1,0:T(8,128)(2,1)} %gather_fusion, bf16[1152,768]{1,0:T(8,128)(2,1)} %gather_fusion.1, f32[1152]{0:T(1024)S(1)} %dynamic-slice_reduce_fusion.9, ...), kind=kOutput, calls=%fused_computation.7.clone.1 | convolution fusion | flops 2047721472 | bytes 10628353 | tf_op jit(solution)/shard_map/while/body/eval_jaxpr/dot_general | solution.py:136
  191.2 3.7 %add_convert_fusion = bf16[1152,768]{1,0:T(8,128)(2,1)} fusion(f32[1152,768]{1,0:T(8,128)} %get-tuple-element.47, bf16[1152,768]{1,0:T(8,128)(2,1)S(1)} %get-tuple-element.197), kind=kLoop, calls=%fused_computation.45 | loop fusion | flops 3538944 | bytes 7077888 | tf_op jit(solution)/shard_map/convert_element_type | solution.py:140
  194.9 2.7 %copy.68 = bf16[1152,768]{0,1:T(8,128)(2,1)S(1)} copy(bf16[1152,768]{1,0:T(8,128)(2,1)} %add_convert_fusion) | data formatting | bytes 3538944 | tf_op jit(solution)/shard_map/convert_element_type | solution.py:140
  197.7 2.2 %copy.69 = bf16[1152,3,256]{2,0,1:T(8,128)(2,1)} copy(bf16[1152,3,256]{0,2,1:T(8,128)(2,1)S(1)} %bitcast.55) | data formatting | bytes 3538944
  (83 shorter events, 0.8 us)
Async XLA Ops:
  0.6 1.1 copy-start
  6.0 13.3 %copy-start.12 = (s32[2,384]{1,0:T(2,128)S(1)}, s32[2,384]{1,0:T(2,128)}, u32[]{:S(2)}) copy-start(s32[2,384]{1,0:T(2,128)} %param.21) | copy-start | bytes 9220
  6.0 16.5 %copy-start.13 = (f32[2,144]{1,0:T(2,128)S(1)}, f32[2,144]{1,0:T(2,128)}, u32[]{:S(2)}) copy-start(f32[2,144]{1,0:T(2,128)} %param.14) | copy-start | bytes 3460
  6.0 16.5 %copy-start.1 = (f32[2,384,128]{2,1,0:T(8,128)S(1)}, f32[2,384,128]{2,1,0:T(8,128)}, u32[]{:S(2)}) copy-start(f32[2,384,128]{2,1,0:T(8,128)} %param.18) | copy-start | bytes 1179652
  7.8 35.9 %all-to-all-start = ((bf16[256,24,128]{2,1,0:T(8,128)(2,1)}), bf16[256,24,128]{2,1,0:T(8,128)(2,1)S(1)}, u32[]{:S(2)}, u32[]{:S(2)}) async-start(bf16[256,24,128]{2,1,0:T(8,128)(2,1)} %select_convert_fusion), calls=%async_computation | async-start | bytes 3145728 | tf_op jit(solution)/shard_map/all_to_all | solution.py:107
  43.7 1.0 copy-start.4
  43.7 1.1 copy-start.5
  43.7 1.2 copy-start.6
  43.7 1.3 copy-start.7
  43.7 1.5 copy-start.8
  45.8 24.0 %copy-start.10 = (s32[24,256]{1,0:T(8,128)S(1)}, s32[24,256]{1,0:T(8,128)}, u32[]{:S(2)}) copy-start(s32[24,256]{1,0:T(8,128)} %param.20) | copy-start | bytes 73732
  45.9 30.6 %copy-start.2 = (bf16[144,24,256]{2,1,0:T(8,128)(2,1)S(1)}, bf16[144,24,256]{2,1,0:T(8,128)(2,1)}, u32[]{:S(2)}) copy-start(bf16[144,24,256]{2,1,0:T(8,128)(2,1)} %param.13) | copy-start | bytes 5308420
  46.1 32.5 %copy-start.3 = (f32[2,384,128]{2,1,0:T(8,128)}, f32[2,384,128]{2,1,0:T(8,128)S(1)}, u32[]{:S(2)}) copy-start(f32[2,384,128]{2,1,0:T(8,128)S(1)} %maximum_multiply_fusion) | copy-start | bytes 1179652
  47.5 17.1 %all-to-all-start.1 = ((f32[2,2,384]{1,0,2:T(2,128)}), f32[2,2,384]{1,0,2:T(2,128)S(1)}, u32[]{:S(2)}, u32[]{:S(2)}) async-start(f32[2,2,384]{1,0,2:T(2,128)} %copy.61), calls=%async_computation.1 | async-start | bytes 786432 | tf_op jit(solution)/shard_map/all_to_all | solution.py:116
  65.6 9.0 %all-to-all-start.2 = ((f32[8,2,256,3]{2,1,3,0:T(2,128)}), f32[8,2,256,3]{2,1,3,0:T(2,128)S(1)}, u32[]{:S(2)}, u32[]{:S(2)}) async-start(f32[8,2,256,3]{2,1,3,0:T(2,128)} %broadcast_in_dim.59), calls=%async_computation.2 | async-start | bytes 98304 | tf_op jit(solution)/shard_map/all_to_all | solution.py:15
  78.6 6.9 %collective-permute-start.1 = (bf16[144,256]{1,0:T(8,128)(2,1)S(1)}, bf16[144,256]{1,0:T(8,128)(2,1)S(1)}, u32[]{:S(2)}, u32[]{:S(2)}) collective-permute-start(bf16[144,256]{1,0:T(8,128)(2,1)S(1)} %fusion.35), channel_id=1, source_target_pairs={{8,0},{16,8},{24,16},{32,24},{40,32},{48,40},{56,48},{64,56},{72,6... | collective-permute-start | bytes 221192 | tf_op jit(solution)/shard_map/ppermute | solution.py:32
  81.4 5.4 %collective-permute-start = (bf16[144,256]{1,0:T(8,128)(2,1)S(1)}, bf16[144,256]{1,0:T(8,128)(2,1)S(1)}, u32[]{:S(2)}, u32[]{:S(2)}) collective-permute-start(bf16[144,256]{1,0:T(8,128)(2,1)S(1)} %fusion.34), channel_id=1, source_target_pairs={{0,8},{8,16},{16,24},{24,32},{32,40},{40,48},{48,56},{56,64},{64,7... | collective-permute-start | bytes 221192 | tf_op jit(solution)/shard_map/ppermute | solution.py:32
  90.8 5.5 %copy-start.9 = (s32[3,4608]{1,0:T(4,128)S(1)}, s32[3,4608]{1,0:T(4,128)}, u32[]{:S(2)}) copy-start(s32[3,4608]{1,0:T(4,128)} %param.16) | copy-start | bytes 165892
  90.8 5.7 %copy-start.11 = (f32[4608]{0:T(1024)S(1)}, f32[4608]{0:T(1024)}, u32[]{:S(2)}) copy-start(f32[4608]{0:T(1024)} %param.17) | copy-start | bytes 55300
  90.8 28.2 %all-to-all-start.3 = ((bf16[144,24,256]{2,0,1:T(8,128)(2,1)}), bf16[144,24,256]{2,0,1:T(8,128)(2,1)S(1)}, u32[]{:S(2)}, u32[]{:S(2)}) async-start(bf16[144,24,256]{2,0,1:T(8,128)(2,1)} %fusion.20), calls=%async_computation.3 | async-start | bytes 3538944 | tf_op jit(solution)/shard_map/all_to_all | solution.py:125
where the time goes:
time: 203 us; the launch traced here: 200 us
  waiting for transfers between devices  59.3 us (29%)
  local copies, waits for them, and re-layouts  57 us (28%)
  matrix products  33.4 us (16%)
  starting transfers between devices  31.5 us (16%)
  other arithmetic  17.5 us (9%)
    dot_general x4, matrix products, one_block(): jnp.dot(onehot, products, preferred_element_type=jnp.float32)  31.3 us
    all_to_all x1, waiting for transfers between devices, per_device(): lax.all_to_all(advected, 'bins', split_axis=1, concat_axis=0, tiled=True)  22.5 us
    gather x4, local copies, waits for them, and re-layouts, one_block(): second = jnp.take(flat, second_ids, axis=0).astype(jnp.float32)  19.3 us
    gather x4, local copies, waits for them, and re-layouts, one_block(): first = jnp.take(flat, first_ids, axis=0).astype(jnp.float32)  19.3 us
    all_to_all x1, waiting for transfers between devices, per_device(): lax.all_to_all(routed.astype(jnp.bfloat16), ('space', 'bins'), split_axis...  18.5 us
    all_to_all x1, waiting for transfers between devices, per_device(): lax.all_to_all(surface, ('space', 'bins'), split_axis=2, concat_axis=1, t...  12.3 us
    all_to_all x1, starting transfers between devices, per_device(): lax.all_to_all(routed.astype(jnp.bfloat16), ('space', 'bins'), split_axis...  11.5 us
    all_to_all x1, starting transfers between devices, per_device(): lax.all_to_all(advected, 'bins', split_axis=1, concat_axis=0, tiled=True)  5.51 us
  transfers between devices with their start and end apart: 6, of which 5 were waited for; matrix products, arithmetic and copies ran while one was open for 4% of the time, Pallas kernels for 0%

commit v1 on v0

v1 whole, which is shorter than its diff:
```python
import functools

import jax
import jax.numpy as jnp
from jax import lax
from jax.experimental import pallas as pl
from jax.experimental.pallas import tpu as pltpu
from jax.sharding import PartitionSpec as P

DT_OCEAN = 0.5
CORIOLIS = 0.8
MIXING = 0.4
CURRENT_SCALE = 0.15
DT_SOURCE = 0.5

LANES = 128
ACCS = 4
UNROLL = 32
BLOCK = 16
ROW_GAP = 400
SPEED_LANE = 32
HIGHEST = lax.Precision.HIGHEST
VMEM = pltpu.VMEM
SMEM = pltpu.SMEM


def in_vmem():
    return pl.BlockSpec(memory_space=VMEM)


def in_smem():
    return pl.BlockSpec(memory_space=SMEM)


def call(body, out_shape, ins, outs, scratch, flops, moved, args, name):
    return pl.pallas_call(
        body,
        out_shape=out_shape,
        in_specs=ins,
        out_specs=outs,
        scratch_shapes=scratch,
        name=name,
        compiler_params=pltpu.CompilerParams(vmem_limit_bytes=58 * 2**20),
        cost_estimate=pl.CostEstimate(flops=flops, bytes_accessed=moved, transcendentals=0),
    )(*args)


def wet_columns(wet_ref):
    wet = wet_ref[...].astype(jnp.float32)
    rows = wet.shape[1]
    return jnp.concatenate([wet, jnp.zeros((6, rows), jnp.float32)], axis=0).T


def surface_kernel(currents_ref, wet_ref, speed_ref, out_ref, rows_ref):
    rows = currents_ref.shape[1]
    half = LANES // 2
    lane = lax.broadcasted_iota(jnp.int32, (rows, LANES), 1)
    wet = wet_columns(wet_ref)
    sign = jnp.where(lane < half, CORIOLIS, -CORIOLIS)
    kept = (lane == 0) | (lane == 1) | (lane == half)
    rows_ref[...] = jnp.zeros_like(rows_ref)
    for slot in range(2):
        x = currents_ref[slot]
        cross = sign * pltpu.roll(x, half, 1)
        below = pltpu.roll(x, LANES - 1, 1)
        column = wet[:, slot : slot + 1]
        value = column * (x + DT_OCEAN * (cross + MIXING * (below - x)))
        value = jnp.where(lane == 1, column, value)
        rows_ref[pl.ds(slot * ROW_GAP + 8, rows), :] = jnp.where(kept, value, 0.0)
    total = jnp.broadcast_to(speed_ref[...], (LANES, LANES))
    for slot in range(2):
        for row in range(5):
            part = rows_ref[pl.ds(slot * ROW_GAP + 7 + row, LANES, stride=3), :]
            shift = 2 * (slot * 5 + row)
            total = total + (pltpu.roll(part, shift, 1) if shift else part)
    out_ref[...] = total


def columns_of(map_ref):
    row = jnp.broadcast_to(map_ref[...].astype(jnp.float32), (LANES, LANES))
    column = row.T
    return jnp.concatenate([column, column], axis=1)


def chosen(column, slot):
    index = lax.broadcasted_iota(jnp.int32, column.shape, 1).astype(jnp.float32)
    return (2.0 * column + float(slot)) == index


def tables_kernel(recv_ref, map_ref, surface_ref, speeds_ref):
    recv = recv_ref[...]
    turned = recv.T
    column = columns_of(map_ref)
    parts = []
    for slot in range(2):
        pick = chosen(column, slot).astype(jnp.float32)
        parts.append(jnp.dot(turned, pick, precision=HIGHEST, preferred_element_type=jnp.float32))
    surface_ref[...] = jnp.zeros_like(surface_ref)
    surface_ref[0:10, :] = parts[0][0:10] + parts[1][10:20]
    surface_ref[16:26, :] = parts[0][64:74] + parts[1][74:84]
    bins = speeds_ref.shape[1]
    lane = lax.broadcasted_iota(jnp.int32, (bins, LANES), 1)
    index = lax.broadcasted_iota(jnp.int32, (bins, LANES), 0)
    first = ((lane & 7) * 16 + (lane >> 3)) * 9
    own = (index >= first) & (index < first + 9)
    rows = jnp.dot(
        own.astype(jnp.float32), recv, precision=HIGHEST, preferred_element_type=jnp.float32
    )
    place = index - ((index * 7282) >> 16) * 9
    ones = jnp.ones((LANES, LANES), jnp.float32)
    for part in range(2):
        value = jnp.where(lane == place + (SPEED_LANE + 9 * part), rows, 0.0)
        speeds_ref[part] = jnp.dot(
            value, ones, precision=HIGHEST, preferred_element_type=jnp.float32
        )


def drift_kernel(whole_ref, map_ref, routed_ref, near_ref, weights_ref, rows_ref):
    sources, _, local_bins, _ = whole_ref.shape
    bins = sources * local_bins
    turned = whole_ref[:, 6].reshape(bins, LANES).T
    weights_ref[0:16, :] = turned[0:16]
    weights_ref[16:32, :] = turned[64:80]
    column = columns_of(map_ref)
    picks = [chosen(column, slot).astype(jnp.float32).astype(jnp.bfloat16) for slot in range(2)]
    rows_ref[...] = jnp.zeros_like(rows_ref)
    near_ref[...] = jnp.zeros_like(near_ref)
    for row in range(3):
        parts = [jnp.zeros((LANES, LANES), jnp.float32) for _ in range(2)]
        for half in range(2):
            cells = whole_ref[:, 2 * row + half].reshape(bins, LANES)
            drift = jnp.dot(turned, cells, preferred_element_type=jnp.float32)
            lanes = slice(half * LANES, (half + 1) * LANES)
            near_ref[row : row + 1, lanes] = drift[0:1]
            near_ref[8 + row : 9 + row, lanes] = drift[64:65]
            narrow = drift.astype(jnp.bfloat16)
            for slot in range(2):
                parts[slot] = parts[slot] + lax.dot_general(
                    picks[slot][:, lanes],
                    narrow,
                    (((1,), (1,)), ((), ())),
                    preferred_element_type=jnp.float32,
                )
        for slot in range(2):
            rows_ref[pl.ds(slot * 3 + row, LANES, stride=8), :] = parts[slot]
    routed_ref[...] = rows_ref[...].astype(jnp.bfloat16)


def wave_kernel(
    pair_ref,
    coef_ref,
    whole_ref,
    below_ref,
    above_ref,
    speeds_ref,
    surface_ref,
    near_ref,
    weights_ref,
    wet_ref,
    out_ref,
    field_ref,
    cur_ref,
    *acc_refs,
):
    sources, _, local_bins, _ = whole_ref.shape
    bins = sources * local_bins
    pairs = coef_ref.shape[0]
    steps = local_bins // BLOCK

    weights = weights_ref[...]
    for side, ref in enumerate((below_ref, above_ref)):
        for half in range(2):
            cells = ref[:, half].reshape(bins, LANES)
            drift = jnp.dot(weights, cells, preferred_element_type=jnp.float32)
            lanes = slice(half * LANES, (half + 1) * LANES)
            cur_ref[24 + side : 25 + side, lanes] = drift[0:1]
            cur_ref[32 + side : 33 + side, lanes] = drift[16:17]
    for row in range(5):
        if row in (0, 4):
            side = 0 if row == 0 else 1
            east = cur_ref[24 + side : 25 + side, :]
            north = cur_ref[32 + side : 33 + side, :]
        else:
            east = near_ref[row - 1 : row, :]
            north = near_ref[8 + row - 1 : 8 + row, :]
        fixed_east = surface_ref[2 * row : 2 * row + 1, :]
        wet = surface_ref[2 * row + 1 : 2 * row + 2, :]
        fixed_north = surface_ref[16 + 2 * row : 17 + 2 * row, :]
        factor = (DT_OCEAN * CORIOLIS) * wet
        cur_ref[row : row + 1, :] = CURRENT_SCALE * jnp.tanh(fixed_east + factor * north)
        cur_ref[8 + row : 9 + row, :] = CURRENT_SCALE * jnp.tanh(fixed_north - factor * east)
    for row in range(3):
        cur_ref[16 + row : 17 + row, :] = wet_ref[row : row + 1, :].astype(jnp.float32)

    lane = lax.broadcasted_iota(jnp.int32, (BLOCK, LANES), 1)
    at_first = lane == 0
    at_last = lane == LANES - 1

    def advect(step, carry):
        source = step // steps
        start = pl.multiple_of((step - source * steps) * BLOCK, BLOCK)
        first = source * local_bins + start
        span = pl.ds(start, BLOCK)
        speed_x = speeds_ref[0, pl.ds(pl.multiple_of(first, BLOCK), BLOCK), :]
        speed_y = speeds_ref[1, pl.ds(pl.multiple_of(first, BLOCK), BLOCK), :]

        def cells(ref, chunk):
            return ref[source, chunk, span, :].astype(jnp.float32)

        def row_flux(energy, row, half):
            current = cur_ref[row : row + 1, half * LANES : (half + 1) * LANES]
            return (speed_x + current) * energy

        energy = [[cells(whole_ref, 2 * row + half) for half in range(2)] for row in range(3)]
        for half in range(2):
            flux = [row_flux(cells(below_ref, half), 0, half)]
            flux += [row_flux(energy[row][half], row + 1, half) for row in range(3)]
            flux += [row_flux(cells(above_ref, half), 4, half)]
            for row in range(3):
                energy[row][half] = (
                    energy[row][half],
                    energy[row][half]
                    - jnp.abs(flux[row + 1])
                    + jnp.maximum(flux[row], 0.0)
                    - jnp.minimum(flux[row + 2], 0.0),
                )
        for row in range(3):
            forward = []
            backward = []
            moved = []
            for half in range(2):
                old, value = energy[row][half]
                current = cur_ref[9 + row : 10 + row, half * LANES : (half + 1) * LANES]
                side = (speed_y + current) * old
                moved.append(value - jnp.abs(side))
                forward.append(pltpu.roll(jnp.maximum(side, 0.0), 1, 1))
                backward.append(pltpu.roll(jnp.minimum(side, 0.0), LANES - 1, 1))
            left = [
                jnp.where(at_first, 0.0, forward[0]),
                jnp.where(at_first, forward[0], forward[1]),
            ]
            right = [
                jnp.where(at_last, backward[1], backward[0]),
                jnp.where(at_last, 0.0, backward[1]),
            ]
            for half in range(2):
                wet = cur_ref[16 + row : 17 + row, half * LANES : (half + 1) * LANES]
                result = wet * (moved[half] + left[half] - right[half])
                rows = pl.ds(first * 8 + (2 * row + half), BLOCK, stride=8)
                field_ref[rows, :] = result
                acc_refs[0][rows, :] = result
        zeros = jnp.zeros((BLOCK * 8, LANES), jnp.float32)
        for ref in acc_refs[1:]:
            ref[pl.ds(pl.multiple_of(first * 8, BLOCK * 8), BLOCK * 8), :] = zeros
        return carry

    lax.fori_loop(0, sources * steps, advect, 0)

    def interact(step, carry):
        start = pl.multiple_of(step * UNROLL, UNROLL)
        firsts = pair_ref.at[pl.ds(start, UNROLL)]
        seconds = pair_ref.at[pl.ds(pairs + start, UNROLL)]
        targets = pair_ref.at[pl.ds(2 * pairs + start, UNROLL)]
        coefs = coef_ref.at[pl.ds(start, UNROLL)]
        for item in range(UNROLL):
            first = pl.ds(pl.multiple_of(firsts[item], 8), 8)
            second = pl.ds(pl.multiple_of(seconds[item], 8), 8)
            target = pl.ds(pl.multiple_of(targets[item], 8), 8)
            ref = acc_refs[item % ACCS]
            product = coefs[item] * (field_ref[first, :] * field_ref[second, :])
            ref[target, :] = ref[target, :] + product
        return carry

    lax.fori_loop(0, pairs // UNROLL, interact, 0)

    def finish(step, carry):
        first = pl.multiple_of(step * BLOCK, BLOCK)
        for row in range(3):
            for half in range(2):
                rows = pl.ds(first * 8 + (2 * row + half), BLOCK, stride=8)
                total = acc_refs[0][rows, :]
                for ref in acc_refs[1:]:
                    total = total + ref[rows, :]
                out_ref[row, pl.ds(first, BLOCK), half * LANES : (half + 1) * LANES] = (
                    total.astype(jnp.bfloat16)
                )
        return carry

    lax.fori_loop(0, bins // BLOCK, finish, 0)


def ocean_kernel(currents_ref, recv_ref, wet_ref, out_ref, wide_ref, rows_ref):
    rows = currents_ref.shape[1]
    half = LANES // 2
    lane = lax.broadcasted_iota(jnp.int32, (rows, LANES), 1)
    place = lane & (half - 1)
    sign = jnp.where(lane < half, CORIOLIS, -CORIOLIS)
    wet = wet_columns(wet_ref)
    wide_ref[...] = recv_ref[...].astype(jnp.float32)
    for slot in range(2):
        for row in range(3):
            rows_ref[pl.ds(row, LANES, stride=3), :] = wide_ref[
                pl.ds(slot * 3 + row, LANES, stride=8), :
            ]
        x = currents_ref[slot]
        upper = jnp.where(place == 0, x, pltpu.roll(x, 1, 1))
        lower = jnp.where(place == half - 1, x, pltpu.roll(x, LANES - 1, 1))
        cross = sign * pltpu.roll(x + rows_ref[...], half, 1)
        mixed = upper + lower - 2.0 * x
        out_ref[slot] = wet[:, slot : slot + 1] * (x + DT_OCEAN * (cross + MIXING * mixed))


def per_device(
    spectrum,
    group_speed,
    stokes_kernel,
    pair_bins,
    pair_coef,
    currents,
    col_map,
    wave_wet,
    ocean_wet,
):
    local_bins, tile_rows, columns = spectrum.shape
    space_count = lax.axis_size("space")
    bins_count = lax.axis_size("bins")
    devices = space_count * bins_count
    rows = tile_rows // bins_count
    bins = local_bins * bins_count
    pairs = pair_bins.shape[1]
    both = ("space", "bins")
    f32 = jnp.float32
    bf16 = jnp.bfloat16
    space_at = lax.axis_index("space")
    bins_at = lax.axis_index("bins")

    cells = spectrum.reshape(local_bins, bins_count, rows, 2, LANES)
    cells = jnp.transpose(cells, (1, 2, 3, 0, 4)).reshape(bins_count, 6, local_bins, LANES)
    kernel_copies = jnp.broadcast_to(
        stokes_kernel[None, None], (bins_count, 1, local_bins, LANES)
    )
    whole = lax.all_to_all(
        jnp.concatenate([cells, kernel_copies], axis=1),
        "bins",
        split_axis=0,
        concat_axis=0,
        tiled=True,
    )

    piece = local_bins // space_count
    speeds = lax.dynamic_slice(group_speed, (0, space_at * piece), (2, piece)).reshape(1, -1)
    speeds = jnp.pad(speeds, ((0, 0), (SPEED_LANE, LANES - SPEED_LANE - 2 * piece)))
    surface = call(
        surface_kernel,
        jax.ShapeDtypeStruct((devices, LANES), f32),
        [in_vmem()] * 3,
        in_vmem(),
        [VMEM((2 * ROW_GAP, LANES), f32)],
        4_000_000,
        500_000,
        (currents, ocean_wet, speeds),
        "surface",
    )
    arrived = lax.all_to_all(surface, both, split_axis=0, concat_axis=0, tiled=True)
    map_row = col_map.reshape(1, -1)
    surface_rows, speed_rows = call(
        tables_kernel,
        (
            jax.ShapeDtypeStruct((32, columns), f32),
            jax.ShapeDtypeStruct((2, bins, LANES), f32),
        ),
        [in_vmem()] * 2,
        (in_vmem(), in_vmem()),
        [],
        600_000_000,
        1_300_000,
        (arrived, map_row),
        "tables",
    )

    ahead = [(at, at + 1) for at in range(devices - 1)]
    back = [(at + 1, at) for at in range(devices - 1)]
    below = lax.ppermute(whole[:, 4:6], both, ahead)
    above = lax.ppermute(whole[:, 0:2], both, back)

    routed, near, weights = call(
        drift_kernel,
        (
            jax.ShapeDtypeStruct((devices * 8, LANES), bf16),
            jax.ShapeDtypeStruct((16, columns), f32),
            jax.ShapeDtypeStruct((32, bins), bf16),
        ),
        [in_vmem()] * 2,
        (in_vmem(),) * 3,
        [VMEM((devices * 8, LANES), f32)],
        300_000_000,
        2_500_000,
        (whole, map_row),
        "drift",
    )
    routed = lax.all_to_all(
        routed.reshape(devices, 8, LANES), both, split_axis=0, concat_axis=0, tiled=True
    ).reshape(devices * 8, LANES)

    own_wet = lax.dynamic_slice(wave_wet, (bins_at * rows, 0), (rows, columns))
    new_spectrum = call(
        wave_kernel,
        jax.ShapeDtypeStruct((rows, bins, columns), bf16),
        [in_smem()] * 2 + [in_vmem()] * 8,
        in_vmem(),
        [VMEM((bins * 8, LANES), f32), VMEM((40, columns), f32)]
        + [VMEM((bins * 8, LANES), f32)] * ACCS,
        40_000_000,
        8_000_000,
        (
            pair_bins.reshape(-1) * 8,
            pair_coef * DT_SOURCE,
            whole,
            below,
            above,
            speed_rows,
            surface_rows,
            near,
            weights,
            own_wet,
        ),
        "waves",
    )
    new_currents = call(
        ocean_kernel,
        jax.ShapeDtypeStruct(currents.shape, f32),
        [in_vmem()] * 3,
        in_vmem(),
        [VMEM((devices * 8, LANES), f32), VMEM((currents.shape[1], LANES), f32)],
        4_000_000,
        1_500_000,
        (currents, routed, ocean_wet),
        "ocean",
    )
    return (jnp.transpose(new_spectrum, (1, 0, 2)), new_currents)


def solution(mesh):
    placed = (
        P("bins", "space", None),
        P(None, "bins"),
        P("bins", None),
        P(),
        P(),
        P(("space", "bins"), None, None),
        P(),
        P("space", None),
        P(("space", "bins"), None),
    )
    return jax.shard_map(
        per_device,
        mesh=mesh,
        in_specs=placed,
        out_specs=(P(None, ("space", "bins"), None), P(("space", "bins"), None, None)),
        check_vma=False,
    )
```

time: 203 us -> 110 us (0.54); the launches traced: 200 us -> 109 us
  local copies, waits for them, and re-layouts: 57 us -> 9.23 us
  Pallas kernels: 0 us -> 37.5 us
  matrix products: 33.4 us -> 0 us
  waiting for transfers between devices: 59.3 us -> 29.3 us
  other arithmetic: 17.5 us -> 2.13 us
    gather x10 -> x0, local copies, waits for them, and re-layouts: 40.5 us -> none  [the longest x4 19.3 us: one_block(): second = jnp.take(flat, second_ids, axis=0).astype(jnp.float32)]
    pallas_call x0 -> x5, Pallas kernels: none -> 37.5 us  [call(): pl.pallas_call(body, out_shape=out_shape, in_specs=ins, out_specs=outs, s...]
    dot_general x5 -> x0, matrix products: 33.4 us -> none  [the longest x4 31.3 us: one_block(): jnp.dot(onehot, products, preferred_element_type=jnp.float32)]
    all_to_all x4 -> x3, waiting for transfers between devices: 58.1 us -> 29.3 us  [the longest x1 22.8 us: per_device(): lax.all_to_all(jnp.concatenate([cells, kernel_copies], axis=1), 'bins', s...]
    convert_element_type x6 -> x0, other arithmetic: 9.78 us -> none  [the longest x2 4.02 us: combine(): return (wet.astype(jnp.float32)[None] * moved).astype(jnp.bfloat16)]
    reshape x2 -> x3, local copies, waits for them, and re-layouts: 0.17 us -> 4.15 us  [the longest x2 4.07 us: per_device(): cells = spectrum.reshape(local_bins, bins_count, rows, 2, LANES)]
    slice x9 -> x1, local copies, waits for them, and re-layouts: 4.78 us -> 1.11 us  [per_device(): above = lax.ppermute(whole[:, 0:2], both, back)]
    sort x1 -> x0, other arithmetic: 3.17 us -> none  [per_device(): inverse = jnp.argsort(slot_col)]
  transfers between devices with their start and end apart: 6 -> 5, of which waited for: 5 -> 2; matrix products, arithmetic and copies ran while one was open for 4% -> 3% of each run, Pallas kernels for 0% -> 11%
where the time goes in v1:
time: 110 us; the launch traced here: 109 us
  Pallas kernels  37.5 us (34%)
  starting transfers between devices  30.3 us (28%)
  waiting for transfers between devices  29.3 us (27%)
  local copies, waits for them, and re-layouts  9.23 us (8%)
  other arithmetic  2.13 us (2%)
    pallas_call x5, Pallas kernels, call(): pl.pallas_call(body, out_shape=out_shape, in_specs=ins, out_specs=outs, s...  37.5 us
    all_to_all x1, waiting for transfers between devices, per_device(): lax.all_to_all(jnp.concatenate([cells, kernel_copies], axis=1), 'bins', s...  22.8 us
    all_to_all x1, starting transfers between devices, per_device(): lax.all_to_all(routed.reshape(devices, 8, LANES), both, split_axis=0, con...  9.86 us
    all_to_all x1, starting transfers between devices, per_device(): lax.all_to_all(surface, both, split_axis=0, concat_axis=0, tiled=True)  8.94 us
    all_to_all x1, waiting for transfers between devices, per_device(): lax.all_to_all(routed.reshape(devices, 8, LANES), both, split_axis=0, con...  6.44 us
    all_to_all x1, starting transfers between devices, per_device(): lax.all_to_all(jnp.concatenate([cells, kernel_copies], axis=1), 'bins', s...  6.09 us
    reshape x2, local copies, waits for them, and re-layouts, per_device(): cells = spectrum.reshape(local_bins, bins_count, rows, 2, LANES)  4.07 us
    ppermute x1, starting transfers between devices, per_device(): below = lax.ppermute(whole[:, 4:6], both, ahead)  3.53 us
  transfers between devices with their start and end apart: 5, of which 2 were waited for; matrix products, arithmetic and copies ran while one was open for 3% of the time, Pallas kernels for 11%

profile of v1, /device:TPU:1, one launch (start us, length us, event | category | flops | bytes accessed | tf_op | source)
XLA Modules:
  0.0 109.3 jit_solution(2763932845118040980)
XLA Ops:
  0.6 0.0 copy-start
  0.6 3.6 %reshape.30 = bf16[144,8,3,2,128]{4,3,2,1,0:T(2,128)(2,1)S(1)} reshape(bf16[144,24,256]{2,1,0:T(8,128)(2,1)} %param.9) | data formatting | bytes 3538944 | tf_op jit(solution)/shard_map/reshape | solution.py:337
  4.3 0.0 copy-start.7
  4.3 0.5 copy.12
  4.7 0.3 copy-done.7
  5.1 1.5 %pad_maximum_fusion = bf16[8,7,144,128]{3,2,1,0:T(8,128)(2,1)} fusion(bf16[8,1,144,128]{3,2,1,0:T(8,128)(2,1)S(1)} %broadcast_in_dim.2, bf16[8,6,144,128]{3,2,1,0:T(8,128)(2,1)S(1)} %bitcast.11), kind=kLoop, calls=%fused_computation | loop fusion | flops 1032192 | bytes 4128768 | tf_op jit(solution)/shard_map/concatenate | solution.py:343
  6.6 0.0 copy-start.9
  6.6 6.1 %all-to-all-start = ((bf16[8,7,144,128]{3,2,1,0:T(8,128)(2,1)}), bf16[8,7,144,128]{3,2,1,0:T(8,128)(2,1)S(1)}, u32[]{:S(2)}, u32[]{:S(2)}) async-start(bf16[8,7,144,128]{3,2,1,0:T(8,128)(2,1)} %pad_maximum_fusion), calls=%async_computation | async-start | bytes 4128768 | tf_op jit(solution)/shard_map/all_to_all | solution.py:342
  12.7 0.0 copy-start.5
  12.7 0.0 copy-done.9
  12.7 0.1 constant_dynamic-slice_fusion.1
  12.8 0.1 reshape.32
  12.8 0.6 pad.4.speed_ref
  13.4 2.3 %surface.1 = f32[128,128]{1,0:T(8,128)} custom-call(f32[2,384,128]{2,1,0:T(8,128)} %currents_ref.3, s32[2,384]{1,0:T(2,128)} %wet_ref.3, f32[1,128]{1,0:T(1,128)} %pad.4.speed_ref), custom_call_target="tpu_custom_call" | custom-call | flops 4000000 | bytes 500000 | tf_op jit(solution)/shard_map/surface/pallas_call | solution.py:36
  15.7 22.8 %all-to-all-done.whole_ref = bf16[8,7,144,128]{3,2,1,0:T(8,128)(2,1)S(1)} async-done(((bf16[8,7,144,128]{3,2,1,0:T(8,128)(2,1)}), bf16[8,7,144,128]{3,2,1,0:T(8,128)(2,1)S(1)}, u32[]{:S(2)}, u32[]{:S(2)}) %all-to-all-start) | async-done | bytes 2064416 | tf_op jit(solution)/shard_map/all_to_all | solution.py:342
  38.5 0.0 copy-start.1
  38.5 8.9 %all-to-all-start.1 = ((f32[128,1,128]{2,1,0:T(1,128)}), f32[128,1,128]{2,1,0:T(1,128)S(1)}, u32[]{:S(2)}, u32[]{:S(2)}) async-start(f32[128,1,128]{2,1,0:T(1,128)} %bitcast.15), calls=%async_computation.1 | async-start | bytes 131072 | tf_op jit(solution)/shard_map/all_to_all | solution.py:364
  47.5 0.0 copy-start.8
  47.5 1.1 %fusion = (bf16[8,2,144,128]{3,2,1,0:T(8,128)(2,1)}, bf16[8,2,144,128]{3,2,1,0:T(8,128)(2,1)}) fusion(bf16[8,7,144,128]{3,2,1,0:T(8,128)(2,1)S(1)} %all-to-all-done.whole_ref), kind=kLoop, calls=%fused_computation.5 | loop fusion | bytes 2359296 | tf_op jit(solution)/shard_map/slice | solution.py:384
  48.6 3.5 %collective-permute-start = (bf16[8,2,144,128]{3,2,1,0:T(8,128)(2,1)}, bf16[8,2,144,128]{3,2,1,0:T(8,128)(2,1)S(1)}, u32[]{:S(2)}, u32[]{:S(2)}) collective-permute-start(bf16[8,2,144,128]{3,2,1,0:T(8,128)(2,1)} %get-tuple-element.13), channel_id=1, source_target_pairs={{0,1},{1,2},{2,3},{3,4},{4,5},{5,6},{6,7},{7,8},{8,9},{9,10},{10,1... | collective-permute-start | bytes 1769480 | tf_op jit(solution)/shard_map/ppermute | solution.py:383
  52.1 1.9 %collective-permute-start.1 = (bf16[8,2,144,128]{3,2,1,0:T(8,128)(2,1)}, bf16[8,2,144,128]{3,2,1,0:T(8,128)(2,1)S(1)}, u32[]{:S(2)}, u32[]{:S(2)}) collective-permute-start(bf16[8,2,144,128]{3,2,1,0:T(8,128)(2,1)} %get-tuple-element.12), channel_id=1, source_target_pairs={{1,0},{2,1},{3,2},{4,3},{5,4},{6,5},{7,6},{8,7},{9,8},{10,9},{11,1... | collective-permute-start | bytes 1769480 | tf_op jit(solution)/shard_map/ppermute | solution.py:384
  54.1 0.0 copy-done.5
  54.1 0.0 copy-done
  54.1 0.6 constant_dynamic-slice_fusion.wet_ref
  54.7 0.6 mul.22.pair_ref
  55.4 0.0 copy-done.1
  55.4 3.7 %drift.1 = (bf16[1024,128]{1,0:T(8,128)(2,1)}, f32[16,256]{1,0:T(8,128)}, bf16[32,1152]{1,0:T(8,128)(2,1)}) custom-call(bf16[8,7,144,128]{3,2,1,0:T(8,128)(2,1)} %copy-done.1, s32[1,128]{1,0:T(1,128)} %bitcast.17), custom_call_target="tpu_custom_call" | custom-call | flops 300000000 | bytes 2500000 | tf_op jit(solution)/shard_map/drift/pallas_call | solution.py:36
  59.0 0.0 all-to-all-done.1
  59.0 0.0 copy-start.6
  59.0 9.9 %all-to-all-start.2 = ((bf16[128,8,128]{2,1,0:T(8,128)(2,1)}), bf16[128,8,128]{2,1,0:T(8,128)(2,1)S(1)}, u32[]{:S(2)}, u32[]{:S(2)}) async-start(bf16[128,8,128]{2,1,0:T(8,128)(2,1)} %bitcast.14), calls=%async_computation.2 | async-start | bytes 524288 | tf_op jit(solution)/shard_map/all_to_all | solution.py:401
  68.9 0.0 copy-done.8
  68.9 0.6 broadcast_multiply_fusion.1.coef_ref
  69.5 0.0 copy-done.6
  69.5 4.0 %tables.1 = (f32[32,256]{1,0:T(8,128)}, f32[2,1152,128]{2,1,0:T(8,128)}) custom-call(f32[128,128]{1,0:T(8,128)} %bitcast.16, s32[1,128]{1,0:T(1,128)} %bitcast.18), custom_call_target="tpu_custom_call" | custom-call | flops 600000000 | bytes 1300000 | tf_op jit(solution)/shard_map/tables/pallas_call | solution.py:36
  73.5 6.4 %all-to-all-done.2 = bf16[128,8,128]{2,1,0:T(8,128)(2,1)S(1)} async-done(((bf16[128,8,128]{2,1,0:T(8,128)(2,1)}), bf16[128,8,128]{2,1,0:T(8,128)(2,1)S(1)}, u32[]{:S(2)}, u32[]{:S(2)}) %all-to-all-start.2) | async-done | bytes 262176 | tf_op jit(solution)/shard_map/all_to_all | solution.py:401
  80.0 0.0 copy-start.2
  80.0 0.7 copy-done.2
  80.7 2.4 %ocean.1 = f32[2,384,128]{2,1,0:T(8,128)} custom-call(f32[2,384,128]{2,1,0:T(8,128)} %currents_ref.3, bf16[1024,128]{1,0:T(8,128)(2,1)} %bitcast.13, s32[2,384]{1,0:T(2,128)} %wet_ref.3), custom_call_target="tpu_custom_call" | custom-call | flops 4000000 | bytes 1500000 | tf_op jit(solution)/shard_map/ocean/pallas_call | solution.py:36
  83.1 0.0 collective-permute-done.below_ref
  83.1 0.0 copy-start.3
  83.1 0.0 collective-permute-done.1.above_ref
  83.1 0.0 copy-start.4
  83.1 0.8 copy-done.3
  84.0 0.2 copy-done.4
  84.1 25.1 %waves.1 = bf16[3,1152,256]{2,1,0:T(8,128)(2,1)} custom-call(s32[13824]{0:T(1024)} %mul.22.pair_ref, f32[4608]{0:T(1024)} %broadcast_multiply_fusion.1.coef_ref, bf16[8,7,144,128]{3,2,1,0:T(8,128)(2,1)} %copy-done.1, bf16[8,2,144,128]{3,2,1,0:T(8,128)(2,1)} %copy-done.3, bf16[8,2,144,128]{3,2,1,0:T(8,128)(2,1)} %copy-done.4, ...), custom_call_target="tpu_custom_call" | custom-call | flops 40000000 | bytes 8000000 | tf_op jit(solution)/shard_map/waves/pallas_call | solution.py:36
  (2 shorter events, 0.1 us)
Async XLA Ops:
  0.6 53.5 %copy-start = (s32[24,256]{1,0:T(8,128)S(1)}, s32[24,256]{1,0:T(8,128)}, u32[]{:S(2)}) copy-start(s32[24,256]{1,0:T(8,128)} %param.16) | copy-start | bytes 73732
  4.3 0.8 copy-start.7
  6.6 6.1 %copy-start.9 = (f32[2,144]{1,0:T(2,128)S(1)}, f32[2,144]{1,0:T(2,128)}, u32[]{:S(2)}) copy-start(f32[2,144]{1,0:T(2,128)} %param.10) | copy-start | bytes 3460
  6.6 31.9 %all-to-all-start = ((bf16[8,7,144,128]{3,2,1,0:T(8,128)(2,1)}), bf16[8,7,144,128]{3,2,1,0:T(8,128)(2,1)S(1)}, u32[]{:S(2)}, u32[]{:S(2)}) async-start(bf16[8,7,144,128]{3,2,1,0:T(8,128)(2,1)} %pad_maximum_fusion), calls=%async_computation | async-start | bytes 4128768 | tf_op jit(solution)/shard_map/all_to_all | solution.py:342
  12.7 41.4 %copy-start.5 = (s32[3,4608]{1,0:T(4,128)S(1)}, s32[3,4608]{1,0:T(4,128)}, u32[]{:S(2)}) copy-start(s32[3,4608]{1,0:T(4,128)} %param.12) | copy-start | bytes 165892
  38.5 16.8 %copy-start.1 = (bf16[8,7,144,128]{3,2,1,0:T(8,128)(2,1)}, bf16[8,7,144,128]{3,2,1,0:T(8,128)(2,1)S(1)}, u32[]{:S(2)}) copy-start(bf16[8,7,144,128]{3,2,1,0:T(8,128)(2,1)S(1)} %all-to-all-done.whole_ref) | copy-start | bytes 6193156
  38.5 20.5 %all-to-all-start.1 = ((f32[128,1,128]{2,1,0:T(1,128)}), f32[128,1,128]{2,1,0:T(1,128)S(1)}, u32[]{:S(2)}, u32[]{:S(2)}) async-start(f32[128,1,128]{2,1,0:T(1,128)} %bitcast.15), calls=%async_computation.1 | async-start | bytes 131072 | tf_op jit(solution)/shard_map/all_to_all | solution.py:364
  47.5 21.4 %copy-start.8 = (f32[4608]{0:T(1024)S(1)}, f32[4608]{0:T(1024)}, u32[]{:S(2)}) copy-start(f32[4608]{0:T(1024)} %param.13) | copy-start | bytes 55300
  48.6 34.5 %collective-permute-start = (bf16[8,2,144,128]{3,2,1,0:T(8,128)(2,1)}, bf16[8,2,144,128]{3,2,1,0:T(8,128)(2,1)S(1)}, u32[]{:S(2)}, u32[]{:S(2)}) collective-permute-start(bf16[8,2,144,128]{3,2,1,0:T(8,128)(2,1)} %get-tuple-element.13), channel_id=1, source_target_pairs={{0,1},{1,2},{2,3},{3,4},{4,5},{5,6},{6,7},{7,8},{8,9},{9,10},{10,1... | collective-permute-start | bytes 1769480 | tf_op jit(solution)/shard_map/ppermute | solution.py:383
  52.1 31.0 %collective-permute-start.1 = (bf16[8,2,144,128]{3,2,1,0:T(8,128)(2,1)}, bf16[8,2,144,128]{3,2,1,0:T(8,128)(2,1)S(1)}, u32[]{:S(2)}, u32[]{:S(2)}) collective-permute-start(bf16[8,2,144,128]{3,2,1,0:T(8,128)(2,1)} %get-tuple-element.12), channel_id=1, source_target_pairs={{1,0},{2,1},{3,2},{4,3},{5,4},{6,5},{7,6},{8,7},{9,8},{10,9},{11,1... | collective-permute-start | bytes 1769480 | tf_op jit(solution)/shard_map/ppermute | solution.py:384
  59.0 10.5 %copy-start.6 = (f32[128,1,128]{2,1,0:T(1,128)}, f32[128,1,128]{2,1,0:T(1,128)S(1)}, u32[]{:S(2)}) copy-start(f32[128,1,128]{2,1,0:T(1,128)S(1)} %all-to-all-done.1) | copy-start | bytes 196612
  59.0 21.0 %all-to-all-start.2 = ((bf16[128,8,128]{2,1,0:T(8,128)(2,1)}), bf16[128,8,128]{2,1,0:T(8,128)(2,1)S(1)}, u32[]{:S(2)}, u32[]{:S(2)}) async-start(bf16[128,8,128]{2,1,0:T(8,128)(2,1)} %bitcast.14), calls=%async_computation.2 | async-start | bytes 524288 | tf_op jit(solution)/shard_map/all_to_all | solution.py:401
  80.0 0.7 copy-start.2
  83.1 0.8 copy-start.3
  83.1 1.0 copy-start.4

commit v2 on v1

--- a/solution.py
+++ b/solution.py
@@ -7,6 +7,7 @@
 from jax.experimental.pallas import tpu as pltpu
 from jax.sharding import PartitionSpec as P
 
+
 DT_OCEAN = 0.5
 CORIOLIS = 0.8
 MIXING = 0.4
@@ -14,7 +15,8 @@
 DT_SOURCE = 0.5
 
 LANES = 128
-ACCS = 4
+ACCS = 2
+CHUNKS = 7
 UNROLL = 32
 BLOCK = 16
 ROW_GAP = 400
@@ -32,17 +34,52 @@
     return pl.BlockSpec(memory_space=SMEM)
 
 
-def call(body, out_shape, ins, outs, scratch, flops, moved, args, name):
+def anywhere():
+    return pl.BlockSpec(memory_space=pl.ANY)
+
+
+def call(body, out_shape, ins, outs, scratch, flops, moved, args, limit=16):
     return pl.pallas_call(
         body,
         out_shape=out_shape,
         in_specs=ins,
         out_specs=outs,
         scratch_shapes=scratch,
-        name=name,
-        compiler_params=pltpu.CompilerParams(vmem_limit_bytes=58 * 2**20),
+        compiler_params=pltpu.CompilerParams(vmem_limit_bytes=limit * 2**20),
         cost_estimate=pl.CostEstimate(flops=flops, bytes_accessed=moved, transcendentals=0),
     )(*args)
+
+
+def pack_kernel(order, ids_ref, spectrum_ref, stokes_ref, *refs):
+    count = len(order)
+    out_refs, (wide_ref, piece_ref, sems) = refs[:count], refs[count:]
+    local_bins, tile_rows, _ = spectrum_ref.shape
+    rows = tile_rows // count
+    for half in range(2):
+        lanes = slice(half * LANES, (half + 1) * LANES)
+        value = spectrum_ref[:, :, lanes].astype(jnp.float32)
+        wide_ref[half] = value.reshape(local_bins * tile_rows, LANES)
+    copies = []
+    for turn in order:
+        base = (ids_ref[0] ^ turn) * rows
+        for row in range(rows):
+            for half in range(2):
+                value = wide_ref[half, pl.ds(base + row, local_bins, stride=tile_rows), :]
+                piece_ref[turn, 2 * row + half] = value.astype(jnp.bfloat16)
+        piece_ref[turn, 6] = stokes_ref[...]
+        copies.append(
+            pltpu.make_async_copy(piece_ref.at[turn], out_refs[turn], sems.at[turn])
+        )
+        copies[-1].start()
+    for copy in copies:
+        copy.wait()
+
+
+def piece_copies(piece_refs, whole_ref, sems, own):
+    return [
+        pltpu.make_async_copy(ref, whole_ref.at[own ^ turn], sems.at[turn])
+        for turn, ref in enumerate(piece_refs)
+    ]
 
 
 def wet_columns(wet_ref):
@@ -115,9 +152,16 @@
         )
 
 
-def drift_kernel(whole_ref, map_ref, routed_ref, near_ref, weights_ref, rows_ref):
+def drift_kernel(count, ids_ref, map_ref, *refs):
+    piece_refs = refs[:count]
+    routed_ref, near_ref, weights_ref, rows_ref, whole_ref, sems = refs[count:]
+    copies = piece_copies(piece_refs, whole_ref, sems, ids_ref[0])
+    for copy in copies:
+        copy.start()
     sources, _, local_bins, _ = whole_ref.shape
     bins = sources * local_bins
+    for copy in copies:
+        copy.wait()
     turned = whole_ref[:, 6].reshape(bins, LANES).T
     weights_ref[0:16, :] = turned[0:16]
     weights_ref[16:32, :] = turned[64:80]
@@ -147,25 +191,64 @@
 
 
 def wave_kernel(
-    pair_ref,
-    coef_ref,
-    whole_ref,
-    below_ref,
-    above_ref,
-    speeds_ref,
+    count,
+    ids_ref,
+    speeds_hbm,
+    pair_hbm,
+    coef_hbm,
+    below_hbm,
+    above_hbm,
     surface_ref,
     near_ref,
     weights_ref,
     wet_ref,
-    out_ref,
-    field_ref,
-    cur_ref,
-    *acc_refs,
+    *refs,
 ):
+    piece_refs = refs[:count]
+    (
+        out_hbm,
+        whole_ref,
+        below_ref,
+        above_ref,
+        speeds_ref,
+        pair_ref,
+        coef_ref,
+        out_ref,
+        field_ref,
+        cur_ref,
+        piece_sems,
+        halo_sems,
+        table_sems,
+        out_sems,
+        *acc_refs,
+    ) = refs[count:]
     sources, _, local_bins, _ = whole_ref.shape
     bins = sources * local_bins
     pairs = coef_ref.shape[0]
     steps = local_bins // BLOCK
+
+    halo_copies = []
+    for source in range(sources):
+        for side, (src, dst) in enumerate(((below_hbm, below_ref), (above_hbm, above_ref))):
+            halo_copies.append(
+                pltpu.make_async_copy(
+                    src.at[ids_ref[1 + side] ^ source],
+                    dst.at[source],
+                    halo_sems.at[2 * source + side],
+                )
+            )
+    bulk_copies = piece_copies(piece_refs, whole_ref, piece_sems, ids_ref[0])
+    bulk_copies.append(pltpu.make_async_copy(speeds_hbm, speeds_ref, table_sems.at[0]))
+    pair_copies = [
+        pltpu.make_async_copy(pair_hbm, pair_ref, table_sems.at[1]),
+        pltpu.make_async_copy(coef_hbm, coef_ref, table_sems.at[2]),
+    ]
+    for copy in halo_copies + bulk_copies + pair_copies:
+        copy.start()
+    for ref in acc_refs[1:]:
+        ref[...] = jnp.zeros_like(ref)
+    for copy in halo_copies:
+        copy.wait()
 
     weights = weights_ref[...]
     for side, ref in enumerate((below_ref, above_ref)):
@@ -249,12 +332,13 @@
                 rows = pl.ds(first * 8 + (2 * row + half), BLOCK, stride=8)
                 field_ref[rows, :] = result
                 acc_refs[0][rows, :] = result
-        zeros = jnp.zeros((BLOCK * 8, LANES), jnp.float32)
-        for ref in acc_refs[1:]:
-            ref[pl.ds(pl.multiple_of(first * 8, BLOCK * 8), BLOCK * 8), :] = zeros
         return carry
 
+    for copy in bulk_copies:
+        copy.wait()
     lax.fori_loop(0, sources * steps, advect, 0)
+    for copy in pair_copies:
+        copy.wait()
 
     def interact(step, carry):
         start = pl.multiple_of(step * UNROLL, UNROLL)
@@ -286,7 +370,21 @@
                 )
         return carry
 
-    lax.fori_loop(0, bins // BLOCK, finish, 0)
+    parts = 4
+    out_copies = []
+    for part in range(parts):
+        span = pl.ds(part * (bins // parts), bins // parts)
+        each = bins // BLOCK // parts
+        lax.fori_loop(part * each, (part + 1) * each, finish, 0)
+        for row in range(3):
+            out_copies.append(
+                pltpu.make_async_copy(
+                    out_ref.at[row, span], out_hbm.at[row, span], out_sems.at[3 * part + row]
+                )
+            )
+            out_copies[-1].start()
+    for copy in out_copies:
+        copy.wait()
 
 
 def ocean_kernel(currents_ref, recv_ref, wet_ref, out_ref, wide_ref, rows_ref):
@@ -334,18 +432,30 @@
     space_at = lax.axis_index("space")
     bins_at = lax.axis_index("bins")
 
-    cells = spectrum.reshape(local_bins, bins_count, rows, 2, LANES)
-    cells = jnp.transpose(cells, (1, 2, 3, 0, 4)).reshape(bins_count, 6, local_bins, LANES)
-    kernel_copies = jnp.broadcast_to(
-        stokes_kernel[None, None], (bins_count, 1, local_bins, LANES)
-    )
-    whole = lax.all_to_all(
-        jnp.concatenate([cells, kernel_copies], axis=1),
-        "bins",
-        split_axis=0,
-        concat_axis=0,
-        tiled=True,
-    )
+    ids = jnp.stack(
+        [bins_at, (bins_at + bins_count - 1) % bins_count, (bins_at + 1) % bins_count]
+    ).astype(jnp.int32)
+
+    order = (4, 5, 2, 3, 6, 7, 1, 0)
+    piece_shape = (CHUNKS, local_bins, LANES)
+    sent = call(
+        functools.partial(pack_kernel, order),
+        [jax.ShapeDtypeStruct(piece_shape, bf16)] * bins_count,
+        [in_smem(), in_vmem(), in_vmem()],
+        [anywhere()] * bins_count,
+        [
+            VMEM((2, local_bins * tile_rows, LANES), f32),
+            VMEM((bins_count, *piece_shape), bf16),
+            pltpu.SemaphoreType.DMA((bins_count,)),
+        ],
+        2_000_000,
+        4_000_000,
+        (ids, spectrum, stokes_kernel),
+    )
+    pieces = [sent[0]] * bins_count
+    for turn in order[:-1]:
+        partners = [(at, at ^ turn) for at in range(bins_count)]
+        pieces[turn] = lax.ppermute(sent[turn], "bins", partners)
 
     piece = local_bins // space_count
     speeds = lax.dynamic_slice(group_speed, (0, space_at * piece), (2, piece)).reshape(1, -1)
@@ -359,7 +469,6 @@
         4_000_000,
         500_000,
         (currents, ocean_wet, speeds),
-        "surface",
     )
     arrived = lax.all_to_all(surface, both, split_axis=0, concat_axis=0, tiled=True)
     map_row = col_map.reshape(1, -1)
@@ -375,56 +484,76 @@
         600_000_000,
         1_300_000,
         (arrived, map_row),
-        "tables",
     )
 
     ahead = [(at, at + 1) for at in range(devices - 1)]
     back = [(at + 1, at) for at in range(devices - 1)]
-    below = lax.ppermute(whole[:, 4:6], both, ahead)
-    above = lax.ppermute(whole[:, 0:2], both, back)
-
+    below = lax.ppermute(jnp.stack([piece[4:6] for piece in pieces]), both, ahead)
+    above = lax.ppermute(jnp.stack([piece[0:2] for piece in pieces]), both, back)
+
+    whole_shape = (bins_count, *piece_shape)
     routed, near, weights = call(
-        drift_kernel,
+        functools.partial(drift_kernel, bins_count),
         (
             jax.ShapeDtypeStruct((devices * 8, LANES), bf16),
             jax.ShapeDtypeStruct((16, columns), f32),
             jax.ShapeDtypeStruct((32, bins), bf16),
         ),
-        [in_vmem()] * 2,
+        [in_smem(), in_vmem()] + [anywhere()] * bins_count,
         (in_vmem(),) * 3,
-        [VMEM((devices * 8, LANES), f32)],
+        [
+            VMEM((devices * 8, LANES), f32),
+            VMEM(whole_shape, bf16),
+            pltpu.SemaphoreType.DMA((bins_count,)),
+        ],
         300_000_000,
         2_500_000,
-        (whole, map_row),
-        "drift",
+        (ids, map_row, *pieces),
     )
     routed = lax.all_to_all(
         routed.reshape(devices, 8, LANES), both, split_axis=0, concat_axis=0, tiled=True
-    ).reshape(devices * 8, LANES)
+    )
+    routed = routed.reshape(devices * 8, LANES)
 
     own_wet = lax.dynamic_slice(wave_wet, (bins_at * rows, 0), (rows, columns))
+    halo_shape = (bins_count, 2, local_bins, LANES)
     new_spectrum = call(
-        wave_kernel,
+        functools.partial(wave_kernel, bins_count),
         jax.ShapeDtypeStruct((rows, bins, columns), bf16),
-        [in_smem()] * 2 + [in_vmem()] * 8,
-        in_vmem(),
-        [VMEM((bins * 8, LANES), f32), VMEM((40, columns), f32)]
+        [in_smem()] + [anywhere()] * 5 + [in_vmem()] * 4 + [anywhere()] * bins_count,
+        anywhere(),
+        [
+            VMEM(whole_shape, bf16),
+            VMEM(halo_shape, bf16),
+            VMEM(halo_shape, bf16),
+            VMEM((2, bins, LANES), f32),
+            SMEM((3 * pairs,), jnp.int32),
+            SMEM((pairs,), f32),
+            VMEM((rows, bins, columns), bf16),
+            VMEM((bins * 8, LANES), f32),
+            VMEM((40, columns), f32),
+            pltpu.SemaphoreType.DMA((bins_count,)),
+            pltpu.SemaphoreType.DMA((2 * bins_count,)),
+            pltpu.SemaphoreType.DMA((3,)),
+            pltpu.SemaphoreType.DMA((12,)),
+        ]
         + [VMEM((bins * 8, LANES), f32)] * ACCS,
         40_000_000,
         8_000_000,
         (
+            ids,
+            speed_rows,
             pair_bins.reshape(-1) * 8,
             pair_coef * DT_SOURCE,
-            whole,
             below,
             above,
-            speed_rows,
             surface_rows,
             near,
             weights,
             own_wet,
+            *pieces,
         ),
-        "waves",
+        26,
     )
     new_currents = call(
         ocean_kernel,
@@ -435,7 +564,6 @@
         4_000_000,
         1_500_000,
         (currents, routed, ocean_wet),
-        "ocean",
     )
     return (jnp.transpose(new_spectrum, (1, 0, 2)), new_currents)
 
@@ -452,6 +580,7 @@
         P("space", None),
         P(("space", "bins"), None),
     )
+
     return jax.shard_map(
         per_device,
         mesh=mesh,

time: 110 us -> 115 us (1.045)
  waiting for transfers between devices: 29.3 us -> 19.7 us
  local copies, waits for them, and re-layouts: 9.23 us -> 15.5 us
  starting transfers between devices: 30.3 us -> 36 us
  Pallas kernels: 37.5 us -> 41 us
    all_to_all x1 -> x0, waiting for transfers between devices: 22.8 us -> none  [per_device(): lax.all_to_all(jnp.concatenate([cells, kernel_copies], axis=1), 'bins', s...]
    ppermute x2 -> x9, waiting for transfers between devices: 0.01 us -> 13.8 us  [the longest x7 13.8 us: per_device(): pieces[turn] = lax.ppermute(sent[turn], 'bins', partners)]
    unnamed x20 -> x43, local copies, waits for them, and re-layouts: 2.03 us -> 14.6 us
    ppermute x2 -> x9, starting transfers between devices: 5.45 us -> 14.7 us  [the longest x7 10.4 us: per_device(): pieces[turn] = lax.ppermute(sent[turn], 'bins', partners)]
    all_to_all x1 -> x0, starting transfers between devices: 6.09 us -> none  [per_device(): lax.all_to_all(jnp.concatenate([cells, kernel_copies], axis=1), 'bins', s...]
    reshape x2 -> x0, local copies, waits for them, and re-layouts: 4.07 us -> none  [per_device(): cells = spectrum.reshape(local_bins, bins_count, rows, 2, LANES)]
    pallas_call x5 -> x6, Pallas kernels: 37.5 us -> 41 us  [call(): pl.pallas_call(body, out_shape=out_shape, in_specs=ins, out_specs=outs, s...]
    concatenate x1 -> x0, other arithmetic: 1.51 us -> none  [per_device(): jnp.concatenate([cells, kernel_copies], axis=1)]
  transfers between devices with their start and end apart: 5 -> 11, of which waited for: 2 -> 4; matrix products, arithmetic and copies ran while one was open for 3% -> 6% of each run, Pallas kernels for 11% -> 8%
where the time goes in v2:
time: 115 us
  Pallas kernels  41 us (36%)
  starting transfers between devices  36 us (31%)
  waiting for transfers between devices  19.7 us (17%)
  local copies, waits for them, and re-layouts  15.5 us (13%)
  other arithmetic  1.71 us (1%)
    pallas_call x6, Pallas kernels, call(): pl.pallas_call(body, out_shape=out_shape, in_specs=ins, out_specs=outs, s...  41 us
    unnamed x43, local copies, waits for them, and re-layouts  14.6 us
    ppermute x7, waiting for transfers between devices, per_device(): pieces[turn] = lax.ppermute(sent[turn], 'bins', partners)  13.8 us
    all_to_all x1, starting transfers between devices, per_device(): lax.all_to_all(routed.reshape(devices, 8, LANES), both, split_axis=0, con...  11.1 us
    ppermute x7, starting transfers between devices, per_device(): pieces[turn] = lax.ppermute(sent[turn], 'bins', partners)  10.4 us
    all_to_all x1, starting transfers between devices, per_device(): lax.all_to_all(surface, both, split_axis=0, concat_axis=0, tiled=True)  10.2 us
    all_to_all x1, waiting for transfers between devices, per_device(): lax.all_to_all(routed.reshape(devices, 8, LANES), both, split_axis=0, con...  5.91 us
    ppermute x1, starting transfers between devices, per_device(): lax.ppermute(jnp.stack([piece[0:2] for piece in pieces]), both, back)  2.31 us
  transfers between devices with their start and end apart: 11, of which 4 were waited for; matrix products, arithmetic and copies ran while one was open for 6% of the time, Pallas kernels for 8%

profile of v2, /device:TPU:1, one launch (start us, length us, event | category | flops | bytes accessed | tf_op | source)
XLA Modules:
  0.0 114.8 jit_solution(14758935867753250008)
XLA Ops:
  0.6 0.0 copy-start
  0.6 0.0 copy-start.17
  0.7 0.0 copy-start.11
  0.7 0.1 pad_add_fusion.ids_ref
  0.8 1.5 %copy-done.1 = bf16[144,24,256]{2,1,0:T(8,128)(2,1)S(1)} copy-done((bf16[144,24,256]{2,1,0:T(8,128)(2,1)S(1)}, bf16[144,24,256]{2,1,0:T(8,128)(2,1)}, u32[]{:S(2)}) %copy-start.1) | copy-done | bytes 1769496
  2.2 0.8 copy-done.6
  3.0 3.6 %shard_map.106 = (bf16[7,144,128]{2,1,0:T(8,128)(2,1)S(1)}, bf16[7,144,128]{2,1,0:T(8,128)(2,1)}, bf16[7,144,128]{2,1,0:T(8,128)(2,1)S(1)}, bf16[7,144,128]{2,1,...) custom-call(s32[3]{0:T(128)S(1)} %pad_add_fusion.ids_ref, ...), custom_call_target="tpu_custom_call" | custom-call | flops 2000000 | bytes 4000000 | tf_op jit(solution)/shard_map/pallas_call | solution.py:42
  6.6 0.0 copy-start.15
  6.6 1.5 %collective-permute-start = (bf16[7,144,128]{2,1,0:T(8,128)(2,1)}, bf16[7,144,128]{2,1,0:T(8,128)(2,1)S(1)}, u32[]{:S(2)}, u32[]{:S(2)}) collective-permute-start(bf16[7,144,128]{2,1,0:T(8,128)(2,1)} %get-tuple-element.17), channel_id=1, source_target_pairs={{0,1},{1,0},{2,3},{3,2},{4,5},{5,4},{6,7},{7,6},{8,9},{9,8},{10,11... | collective-permute-start | bytes 774152 | tf_op jit(solution)/shard_map/ppermute | solution.py:458
  8.1 1.4 %collective-permute-start.1 = (bf16[7,144,128]{2,1,0:T(8,128)(2,1)S(1)}, bf16[7,144,128]{2,1,0:T(8,128)(2,1)S(1)}, u32[]{:S(2)}, u32[]{:S(2)}) collective-permute-start(bf16[7,144,128]{2,1,0:T(8,128)(2,1)S(1)} %get-tuple-element.18), channel_id=1, source_target_pairs={{0,2},{1,3},{2,0},{3,1},{4,6},{5,7},{6,4},{7,5},{8,10},{9,11},{10,... | collective-permute-start | bytes 774152 | tf_op jit(solution)/shard_map/ppermute | solution.py:458
  9.5 0.3 collective-permute-start.2
  9.8 3.0 %collective-permute-start.3 = (bf16[7,144,128]{2,1,0:T(8,128)(2,1)}, bf16[7,144,128]{2,1,0:T(8,128)(2,1)S(1)}, u32[]{:S(2)}, u32[]{:S(2)}) collective-permute-start(bf16[7,144,128]{2,1,0:T(8,128)(2,1)} %get-tuple-element.20), channel_id=1, source_target_pairs={{0,4},{1,5},{2,6},{3,7},{4,0},{5,1},{6,2},{7,3},{8,12},{9,13},{10,... | collective-permute-start | bytes 774152 | tf_op jit(solution)/shard_map/ppermute | solution.py:458
  12.8 0.2 collective-permute-start.4
  13.1 0.0 copy-done.17
  13.1 0.1 constant_dynamic-slice_fusion.1
  13.2 0.1 reshape.21
  13.2 0.1 pad.4.speed_ref
  13.3 1.3 %shard_map.104 = f32[128,128]{1,0:T(8,128)} custom-call(f32[2,384,128]{2,1,0:T(8,128)S(1)} %copy-done.2, s32[2,384]{1,0:T(2,128)S(1)} %copy-done.11, f32[1,128]{1,0:T(1,128)S(1)} %pad.4.speed_ref), custom_call_target="tpu_custom_call" | custom-call | flops 4000000 | bytes 500000 | tf_op jit(solution)/shard_map/pallas_call | solution.py:42
  14.6 10.2 %all-to-all-start = ((f32[128,1,128]{2,1,0:T(1,128)}), f32[128,1,128]{2,1,0:T(1,128)S(1)}, u32[]{:S(2)}, u32[]{:S(2)}) async-start(f32[128,1,128]{2,1,0:T(1,128)} %bitcast.4), calls=%async_computation | async-start | bytes 131072 | tf_op jit(solution)/shard_map/all_to_all | solution.py:473
  24.8 0.7 bitcast_dynamic-update-slice_fusion
  25.5 0.0 collective-permute-done.refs_1_
  25.5 2.6 %collective-permute-start.5 = (bf16[7,144,128]{2,1,0:T(8,128)(2,1)S(1)}, bf16[7,144,128]{2,1,0:T(8,128)(2,1)S(1)}, u32[]{:S(2)}, u32[]{:S(2)}) collective-permute-start(bf16[7,144,128]{2,1,0:T(8,128)(2,1)S(1)} %get-tuple-element.22), channel_id=1, source_target_pairs={{0,6},{1,7},{2,4},{3,5},{4,2},{5,3},{6,0},{7,1},{8,14},{9,15},{10,... | collective-permute-start | bytes 774152 | tf_op jit(solution)/shard_map/ppermute | solution.py:458
  28.1 0.7 fusion.6
  28.8 0.0 collective-permute-done.1.refs_2_
  28.8 1.3 %collective-permute-start.6 = (bf16[7,144,128]{2,1,0:T(8,128)(2,1)S(1)}, bf16[7,144,128]{2,1,0:T(8,128)(2,1)S(1)}, u32[]{:S(2)}, u32[]{:S(2)}) collective-permute-start(bf16[7,144,128]{2,1,0:T(8,128)(2,1)S(1)} %get-tuple-element.23), channel_id=1, source_target_pairs={{0,7},{1,6},{2,5},{3,4},{4,3},{5,2},{6,1},{7,0},{8,15},{9,14},{10,... | collective-permute-start | bytes 774152 | tf_op jit(solution)/shard_map/ppermute | solution.py:458
  30.1 0.7 fusion.5
  30.8 0.0 collective-permute-done.2.refs_3_
  30.8 0.7 fusion.4
  31.5 0.0 collective-permute-done.3.refs_4_
  31.5 0.7 fusion.3
  32.1 4.0 %collective-permute-done.4.refs_5_ = bf16[7,144,128]{2,1,0:T(8,128)(2,1)S(1)} collective-permute-done((bf16[7,144,128]{2,1,0:T(8,128)(2,1)S(1)}, bf16[7,144,128]{2,1,0:T(8,128)(2,1)S(1)}, u32[]{:S(2)}, u32[]{:S(2)}) %collective-permute-start.4) | collective-permute-done | bytes 258080 | tf_op jit(solution)/shard_map/ppermute | solution.py:458
  36.1 0.7 fusion.2
  36.8 4.9 %collective-permute-done.5.refs_6_ = bf16[7,144,128]{2,1,0:T(8,128)(2,1)S(1)} collective-permute-done((bf16[7,144,128]{2,1,0:T(8,128)(2,1)S(1)}, bf16[7,144,128]{2,1,0:T(8,128)(2,1)S(1)}, u32[]{:S(2)}, u32[]{:S(2)}) %collective-permute-start.5) | collective-permute-done | bytes 258080 | tf_op jit(solution)/shard_map/ppermute | solution.py:458
  41.7 0.7 fusion.1
  42.4 4.9 %collective-permute-done.6.refs_7_ = bf16[7,144,128]{2,1,0:T(8,128)(2,1)S(1)} collective-permute-done((bf16[7,144,128]{2,1,0:T(8,128)(2,1)S(1)}, bf16[7,144,128]{2,1,0:T(8,128)(2,1)S(1)}, u32[]{:S(2)}, u32[]{:S(2)}) %collective-permute-start.6) | collective-permute-done | bytes 258080 | tf_op jit(solution)/shard_map/ppermute | solution.py:458
  47.2 0.7 fusion
  47.9 2.0 %collective-permute-start.7 = (bf16[8,2,144,128]{3,2,1,0:T(8,128)(2,1)}, bf16[8,2,144,128]{3,2,1,0:T(8,128)(2,1)S(1)}, u32[]{:S(2)}, u32[]{:S(2)}) collective-permute-start(bf16[8,2,144,128]{3,2,1,0:T(8,128)(2,1)} %get-tuple-element.29), channel_id=1, source_target_pairs={{0,1},{1,2},{2,3},{3,4},{4,5},{5,6},{6,7},{7,8},{8,9},{9,10},{10,1... | collective-permute-start | bytes 1769480 | tf_op jit(solution)/shard_map/ppermute | solution.py:491
  49.9 2.3 %collective-permute-start.8 = (bf16[8,2,144,128]{3,2,1,0:T(8,128)(2,1)}, bf16[8,2,144,128]{3,2,1,0:T(8,128)(2,1)}, u32[]{:S(2)}, u32[]{:S(2)}) collective-permute-start(bf16[8,2,144,128]{3,2,1,0:T(8,128)(2,1)} %get-tuple-element.28), channel_id=1, source_target_pairs={{1,0},{2,1},{3,2},{4,3},{5,4},{6,5},{7,6},{8,7},{9,8},{10,9},{11,1... | collective-permute-start | bytes 1769480 | tf_op jit(solution)/shard_map/ppermute | solution.py:492
  52.3 0.9 broadcast_multiply_fusion
  53.2 0.0 copy-done
  53.2 0.0 copy-done.13
  53.2 0.0 copy-done.15
  53.2 4.7 %shard_map.107 = (bf16[1024,128]{1,0:T(8,128)(2,1)S(1)}, f32[16,256]{1,0:T(8,128)S(1)}, bf16[32,1152]{1,0:T(8,128)(2,1)S(1)}) custom-call(s32[3]{0:T(128)S(1)} %pad_add_fusion.ids_ref, s32[1,128]{1,0:T(1,128)S(1)} %bitcast.74, bf16[7,144,128]{2,1,0:T(8,128)(2,1)S(1)} %get-tuple-element.16.refs_0_, bf16[7,144,128]{2,1,0:T(8,128)(2,1)S(1)} %collective-permute-done.refs_1_, ...), custom_call_target="tpu_custom_call" | custom-call | flops 300000000 | bytes 2500000 | tf_op jit(solution)/shard_map/pallas_call | solution.py:42
  57.9 0.0 copy-start.5
  57.9 0.7 copy-done.5
  58.6 0.0 all-to-all-done
  58.6 0.6 copy-done.9
  59.2 11.1 %all-to-all-start.1 = ((bf16[128,8,128]{2,1,0:T(8,128)(2,1)}), bf16[128,8,128]{2,1,0:T(8,128)(2,1)S(1)}, u32[]{:S(2)}, u32[]{:S(2)}) async-start(bf16[128,8,128]{2,1,0:T(8,128)(2,1)} %bitcast.72), calls=%async_computation.1 | async-start | bytes 524288 | tf_op jit(solution)/shard_map/all_to_all | solution.py:513
  70.3 0.7 broadcast_multiply_fusion.1.coef_hbm
  71.0 0.7 copy-done.16
  71.7 2.2 %shard_map.105 = (f32[32,256]{1,0:T(8,128)S(1)}, f32[2,1152,128]{2,1,0:T(8,128)S(1)}) custom-call(f32[128,128]{1,0:T(8,128)S(1)} %bitcast.73, s32[1,128]{1,0:T(1,128)S(1)} %bitcast.75), custom_call_target="tpu_custom_call" | custom-call | flops 600000000 | bytes 1300000 | tf_op jit(solution)/shard_map/pallas_call | solution.py:42
  73.9 0.0 copy-start.3
  73.9 1.0 copy-done.3
  74.9 0.6 copy-done.7
  75.5 5.9 %all-to-all-done.1 = bf16[128,8,128]{2,1,0:T(8,128)(2,1)S(1)} async-done(((bf16[128,8,128]{2,1,0:T(8,128)(2,1)}), bf16[128,8,128]{2,1,0:T(8,128)(2,1)S(1)}, u32[]{:S(2)}, u32[]{:S(2)}) %all-to-all-start.1) | async-done | bytes 262176 | tf_op jit(solution)/shard_map/all_to_all | solution.py:513
  81.4 0.7 copy-done.12
  82.1 1.4 %shard_map.109 = f32[2,384,128]{2,1,0:T(8,128)} custom-call(f32[2,384,128]{2,1,0:T(8,128)S(1)} %copy-done.2, bf16[1024,128]{1,0:T(8,128)(2,1)S(1)} %bitcast.71, s32[2,384]{1,0:T(2,128)S(1)} %copy-done.12), custom_call_target="tpu_custom_call" | custom-call | flops 4000000 | bytes 1500000 | tf_op jit(solution)/shard_map/pallas_call | solution.py:42
  83.5 0.0 collective-permute-done.7.below_hbm
  83.5 0.0 collective-permute-done.8.above_hbm
  83.5 1.3 %copy-done.4 = f32[2,1152,128]{2,1,0:T(8,128)S(1)} copy-done((f32[2,1152,128]{2,1,0:T(8,128)S(1)}, f32[2,1152,128]{2,1,0:T(8,128)}, u32[]{:S(2)}) %copy-start.4) | copy-done | bytes 1179672
  84.8 0.8 copy-done.8
  85.5 0.7 copy-done.10
  86.2 0.6 copy-done.14
  86.9 28.0 %shard_map.108 = bf16[3,1152,256]{2,1,0:T(8,128)(2,1)} custom-call(s32[3]{0:T(128)S(1)} %copy-done.14, f32[2,1152,128]{2,1,0:T(8,128)S(1)} %copy-done.4, s32[13824]{0:T(1024)S(1)} %mul.23.pair_hbm, f32[4608]{0:T(1024)S(1)} %broadcast_multiply_fusion.1.coef_hbm, bf16[8,2,144,128]{3,2,1,0:T(8,128)(2,1)S(1)} %collective-permute-done.7.below_hbm, ...), custom_call_target="tpu_custom_call" | custom-call | flops 40000000 | bytes 8000000 | tf_op jit(solution)/shard_map/pallas_call | solution.py:42
  (16 shorter events, 0.1 us)
Async XLA Ops:
  0.6 52.5 %copy-start = (s32[24,256]{1,0:T(8,128)S(1)}, s32[24,256]{1,0:T(8,128)}, u32[]{:S(2)}) copy-start(s32[24,256]{1,0:T(8,128)} %param.16) | copy-start | bytes 73732
  0.6 12.4 %copy-start.17 = (f32[2,144]{1,0:T(2,128)S(1)}, f32[2,144]{1,0:T(2,128)}, u32[]{:S(2)}) copy-start(f32[2,144]{1,0:T(2,128)} %param.10) | copy-start | bytes 3460
  0.7 12.7 %copy-start.11 = (s32[2,384]{1,0:T(2,128)S(1)}, s32[2,384]{1,0:T(2,128)}, u32[]{:S(2)}) copy-start(s32[2,384]{1,0:T(2,128)} %wet_ref.3) | copy-start | bytes 9220
  0.8 1.5 %copy-start.1 = (bf16[144,24,256]{2,1,0:T(8,128)(2,1)S(1)}, bf16[144,24,256]{2,1,0:T(8,128)(2,1)}, u32[]{:S(2)}) copy-start(bf16[144,24,256]{2,1,0:T(8,128)(2,1)} %spectrum_ref.1) | copy-start | bytes 5308420
  2.2 0.8 copy-start.6
  3.0 50.2 %copy-start.13 = (s32[3]{0:T(128)}, s32[3]{0:T(128)S(1)}, u32[]{:S(2)}) copy-start(s32[3]{0:T(128)S(1)} %pad_add_fusion.ids_ref) | copy-start | bytes 40
  3.0 10.3 %copy-start.2 = (f32[2,384,128]{2,1,0:T(8,128)S(1)}, f32[2,384,128]{2,1,0:T(8,128)}, u32[]{:S(2)}) copy-start(f32[2,384,128]{2,1,0:T(8,128)} %currents_ref.3) | copy-start | bytes 1179652
  6.6 46.6 %copy-start.15 = (s32[128]{0:T(128)S(1)}, s32[128]{0:T(128)}, u32[]{:S(2)}) copy-start(s32[128]{0:T(128)} %param.15) | copy-start | bytes 1540
  6.6 18.9 %collective-permute-start = (bf16[7,144,128]{2,1,0:T(8,128)(2,1)}, bf16[7,144,128]{2,1,0:T(8,128)(2,1)S(1)}, u32[]{:S(2)}, u32[]{:S(2)}) collective-permute-start(bf16[7,144,128]{2,1,0:T(8,128)(2,1)} %get-tuple-element.17), channel_id=1, source_target_pairs={{0,1},{1,0},{2,3},{3,2},{4,5},{5,4},{6,7},{7,6},{8,9},{9,8},{10,11... | collective-permute-start | bytes 774152 | tf_op jit(solution)/shard_map/ppermute | solution.py:458
  8.1 20.8 %collective-permute-start.1 = (bf16[7,144,128]{2,1,0:T(8,128)(2,1)S(1)}, bf16[7,144,128]{2,1,0:T(8,128)(2,1)S(1)}, u32[]{:S(2)}, u32[]{:S(2)}) collective-permute-start(bf16[7,144,128]{2,1,0:T(8,128)(2,1)S(1)} %get-tuple-element.18), channel_id=1, source_target_pairs={{0,2},{1,3},{2,0},{3,1},{4,6},{5,7},{6,4},{7,5},{8,10},{9,11},{10,... | collective-permute-start | bytes 774152 | tf_op jit(solution)/shard_map/ppermute | solution.py:458
  9.5 21.3 %collective-permute-start.2 = (bf16[7,144,128]{2,1,0:T(8,128)(2,1)}, bf16[7,144,128]{2,1,0:T(8,128)(2,1)S(1)}, u32[]{:S(2)}, u32[]{:S(2)}) collective-permute-start(bf16[7,144,128]{2,1,0:T(8,128)(2,1)} %get-tuple-element.19), channel_id=1, source_target_pairs={{0,3},{1,2},{2,1},{3,0},{4,7},{5,6},{6,5},{7,4},{8,11},{9,10},{10,... | collective-permute-start | bytes 774152 | tf_op jit(solution)/shard_map/ppermute | solution.py:458
  9.8 21.7 %collective-permute-start.3 = (bf16[7,144,128]{2,1,0:T(8,128)(2,1)}, bf16[7,144,128]{2,1,0:T(8,128)(2,1)S(1)}, u32[]{:S(2)}, u32[]{:S(2)}) collective-permute-start(bf16[7,144,128]{2,1,0:T(8,128)(2,1)} %get-tuple-element.20), channel_id=1, source_target_pairs={{0,4},{1,5},{2,6},{3,7},{4,0},{5,1},{6,2},{7,3},{8,12},{9,13},{10,... | collective-permute-start | bytes 774152 | tf_op jit(solution)/shard_map/ppermute | solution.py:458
  12.8 23.3 %collective-permute-start.4 = (bf16[7,144,128]{2,1,0:T(8,128)(2,1)S(1)}, bf16[7,144,128]{2,1,0:T(8,128)(2,1)S(1)}, u32[]{:S(2)}, u32[]{:S(2)}) collective-permute-start(bf16[7,144,128]{2,1,0:T(8,128)(2,1)S(1)} %get-tuple-element.21), channel_id=1, source_target_pairs={{0,5},{1,4},{2,7},{3,6},{4,1},{5,0},{6,3},{7,2},{8,13},{9,12},{10,... | collective-permute-start | bytes 774152 | tf_op jit(solution)/shard_map/ppermute | solution.py:458
  14.6 44.0 %all-to-all-start = ((f32[128,1,128]{2,1,0:T(1,128)}), f32[128,1,128]{2,1,0:T(1,128)S(1)}, u32[]{:S(2)}, u32[]{:S(2)}) async-start(f32[128,1,128]{2,1,0:T(1,128)} %bitcast.4), calls=%async_computation | async-start | bytes 131072 | tf_op jit(solution)/shard_map/all_to_all | solution.py:473
  25.5 16.2 %collective-permute-start.5 = (bf16[7,144,128]{2,1,0:T(8,128)(2,1)S(1)}, bf16[7,144,128]{2,1,0:T(8,128)(2,1)S(1)}, u32[]{:S(2)}, u32[]{:S(2)}) collective-permute-start(bf16[7,144,128]{2,1,0:T(8,128)(2,1)S(1)} %get-tuple-element.22), channel_id=1, source_target_pairs={{0,6},{1,7},{2,4},{3,5},{4,2},{5,3},{6,0},{7,1},{8,14},{9,15},{10,... | collective-permute-start | bytes 774152 | tf_op jit(solution)/shard_map/ppermute | solution.py:458
  28.8 18.4 %collective-permute-start.6 = (bf16[7,144,128]{2,1,0:T(8,128)(2,1)S(1)}, bf16[7,144,128]{2,1,0:T(8,128)(2,1)S(1)}, u32[]{:S(2)}, u32[]{:S(2)}) collective-permute-start(bf16[7,144,128]{2,1,0:T(8,128)(2,1)S(1)} %get-tuple-element.23), channel_id=1, source_target_pairs={{0,7},{1,6},{2,5},{3,4},{4,3},{5,2},{6,1},{7,0},{8,15},{9,14},{10,... | collective-permute-start | bytes 774152 | tf_op jit(solution)/shard_map/ppermute | solution.py:458
  47.9 35.6 %collective-permute-start.7 = (bf16[8,2,144,128]{3,2,1,0:T(8,128)(2,1)}, bf16[8,2,144,128]{3,2,1,0:T(8,128)(2,1)S(1)}, u32[]{:S(2)}, u32[]{:S(2)}) collective-permute-start(bf16[8,2,144,128]{3,2,1,0:T(8,128)(2,1)} %get-tuple-element.29), channel_id=1, source_target_pairs={{0,1},{1,2},{2,3},{3,4},{4,5},{5,6},{6,7},{7,8},{8,9},{9,10},{10,1... | collective-permute-start | bytes 1769480 | tf_op jit(solution)/shard_map/ppermute | solution.py:491
  49.9 33.6 %collective-permute-start.8 = (bf16[8,2,144,128]{3,2,1,0:T(8,128)(2,1)}, bf16[8,2,144,128]{3,2,1,0:T(8,128)(2,1)}, u32[]{:S(2)}, u32[]{:S(2)}) collective-permute-start(bf16[8,2,144,128]{3,2,1,0:T(8,128)(2,1)} %get-tuple-element.28), channel_id=1, source_target_pairs={{1,0},{2,1},{3,2},{4,3},{5,4},{6,5},{7,6},{8,7},{9,8},{10,9},{11,1... | collective-permute-start | bytes 1769480 | tf_op jit(solution)/shard_map/ppermute | solution.py:492
  57.9 0.7 copy-start.5
  58.6 0.6 copy-start.9
  59.2 22.2 %all-to-all-start.1 = ((bf16[128,8,128]{2,1,0:T(8,128)(2,1)}), bf16[128,8,128]{2,1,0:T(8,128)(2,1)S(1)}, u32[]{:S(2)}, u32[]{:S(2)}) async-start(bf16[128,8,128]{2,1,0:T(8,128)(2,1)} %bitcast.72), calls=%async_computation.1 | async-start | bytes 524288 | tf_op jit(solution)/shard_map/all_to_all | solution.py:513
  71.0 0.7 copy-start.16
  73.9 1.0 copy-start.3
  74.9 0.6 copy-start.7
  81.4 0.7 copy-start.12
  83.5 1.3 %copy-start.4 = (f32[2,1152,128]{2,1,0:T(8,128)S(1)}, f32[2,1152,128]{2,1,0:T(8,128)}, u32[]{:S(2)}) copy-start(f32[2,1152,128]{2,1,0:T(8,128)} %copy-done.3) | copy-start | bytes 3538948
  84.8 0.8 copy-start.8
  85.5 0.7 copy-start.10
  86.2 0.6 copy-start.14

commit v3 on v1

--- a/solution.py
+++ b/solution.py
@@ -7,6 +7,7 @@
 from jax.experimental.pallas import tpu as pltpu
 from jax.sharding import PartitionSpec as P
 
+
 DT_OCEAN = 0.5
 CORIOLIS = 0.8
 MIXING = 0.4
@@ -14,8 +15,10 @@
 DT_SOURCE = 0.5
 
 LANES = 128
-ACCS = 4
-UNROLL = 32
+ACCS = 3
+WAVE_LIMIT = 24
+CHUNKS = 7
+UNROLL = 48
 BLOCK = 16
 ROW_GAP = 400
 SPEED_LANE = 32
@@ -32,17 +35,74 @@
     return pl.BlockSpec(memory_space=SMEM)
 
 
-def call(body, out_shape, ins, outs, scratch, flops, moved, args, name):
+def in_hbm():
+    return pl.BlockSpec(memory_space=pltpu.HBM)
+
+
+def call(body, out_shape, ins, outs, scratch, flops, moved, args, limit=16):
     return pl.pallas_call(
         body,
         out_shape=out_shape,
         in_specs=ins,
         out_specs=outs,
         scratch_shapes=scratch,
-        name=name,
-        compiler_params=pltpu.CompilerParams(vmem_limit_bytes=58 * 2**20),
+        compiler_params=pltpu.CompilerParams(vmem_limit_bytes=limit * 2**20),
         cost_estimate=pl.CostEstimate(flops=flops, bytes_accessed=moved, transcendentals=0),
     )(*args)
+
+
+def pack_kernel(order, ids_ref, spectrum_hbm, stokes_hbm, *refs):
+    count = len(order)
+    out_refs = refs[:count]
+    narrow_ref, wide_ref, in_sems, stokes_sems = refs[count:]
+    local_bins, tile_rows, _ = spectrum_hbm.shape
+    rows = tile_rows // count
+    chunks = in_sems.shape[0]
+    part = local_bins // chunks
+    loads = []
+    for chunk in range(chunks):
+        span = pl.ds(chunk * part, part)
+        loads.append(
+            pltpu.make_async_copy(spectrum_hbm.at[span], narrow_ref.at[span], in_sems.at[chunk])
+        )
+        loads[-1].start()
+    stokes = [
+        pltpu.make_async_copy(stokes_hbm, out_refs[turn].at[6], stokes_sems.at[turn])
+        for turn in range(count)
+    ]
+    for copy in stokes:
+        copy.start()
+    own = ids_ref[0]
+    for chunk in range(chunks):
+        loads[chunk].wait()
+        first = chunk * part
+        for half in range(2):
+            lanes = slice(half * LANES, (half + 1) * LANES)
+            value = narrow_ref[first : first + part, :, lanes].astype(jnp.float32)
+            wide_ref[half, first * tile_rows : (first + part) * tile_rows] = value.reshape(
+                part * tile_rows, LANES
+            )
+        for turn in order:
+            base = (own ^ turn) * rows + first * tile_rows
+            for row in range(rows):
+                for half in range(2):
+                    value = wide_ref[half, pl.ds(base + row, part, stride=tile_rows), :]
+                    out_refs[turn][2 * row + half, first : first + part, :] = value.astype(
+                        jnp.bfloat16
+                    )
+    for copy in stokes:
+        copy.wait()
+
+
+def joined(refs, chunk):
+    return jnp.concatenate([ref[chunk] for ref in refs], axis=0)
+
+
+def edges_kernel(*refs):
+    last_ref, first_ref = refs[-2:]
+    for turn, ref in enumerate(refs[:-2]):
+        last_ref[turn] = ref[4:6]
+        first_ref[turn] = ref[0:2]
 
 
 def wet_columns(wet_ref):
@@ -87,7 +147,12 @@
     return (2.0 * column + float(slot)) == index
 
 
-def tables_kernel(recv_ref, map_ref, surface_ref, speeds_ref):
+def tables_kernel(recv_ref, map_ref, coef_ref, surface_ref, speeds_ref, coefs_ref):
+    for block in range(coef_ref.shape[0]):
+        row = DT_SOURCE * coef_ref[block : block + 1, :]
+        coefs_ref[block * LANES : (block + 1) * LANES, :] = jnp.broadcast_to(
+            row, (LANES, LANES)
+        ).T
     recv = recv_ref[...]
     turned = recv.T
     column = columns_of(map_ref)
@@ -115,12 +180,16 @@
         )
 
 
-def drift_kernel(whole_ref, map_ref, routed_ref, near_ref, weights_ref, rows_ref):
-    sources, _, local_bins, _ = whole_ref.shape
-    bins = sources * local_bins
-    turned = whole_ref[:, 6].reshape(bins, LANES).T
-    weights_ref[0:16, :] = turned[0:16]
-    weights_ref[16:32, :] = turned[64:80]
+def drift_kernel(count, ids_ref, map_ref, *refs):
+    piece_refs = refs[:count]
+    routed_ref, near_ref, weights_ref, rows_ref, stokes_ref = refs[count:]
+    own = ids_ref[0]
+    for turn, ref in enumerate(piece_refs):
+        stokes_ref[own ^ turn] = ref[6]
+    in_order = stokes_ref[...].reshape(-1, LANES).T
+    weights_ref[0:16, :] = in_order[0:16]
+    weights_ref[16:32, :] = in_order[64:80]
+    turned = joined(piece_refs, 6).T
     column = columns_of(map_ref)
     picks = [chosen(column, slot).astype(jnp.float32).astype(jnp.bfloat16) for slot in range(2)]
     rows_ref[...] = jnp.zeros_like(rows_ref)
@@ -128,7 +197,7 @@
     for row in range(3):
         parts = [jnp.zeros((LANES, LANES), jnp.float32) for _ in range(2)]
         for half in range(2):
-            cells = whole_ref[:, 2 * row + half].reshape(bins, LANES)
+            cells = joined(piece_refs, 2 * row + half)
             drift = jnp.dot(turned, cells, preferred_element_type=jnp.float32)
             lanes = slice(half * LANES, (half + 1) * LANES)
             near_ref[row : row + 1, lanes] = drift[0:1]
@@ -147,30 +216,36 @@
 
 
 def wave_kernel(
-    pair_ref,
+    count,
+    ids_ref,
+    pair_hbm,
     coef_ref,
-    whole_ref,
+    speeds_ref,
     below_ref,
     above_ref,
-    speeds_ref,
     surface_ref,
     near_ref,
     weights_ref,
     wet_ref,
-    out_ref,
-    field_ref,
-    cur_ref,
-    *acc_refs,
+    *refs,
 ):
-    sources, _, local_bins, _ = whole_ref.shape
-    bins = sources * local_bins
+    piece_refs = refs[:count]
+    out_hbm, pair_ref, out_ref, field_ref, cur_ref, pair_sem, out_sems, *acc_refs = refs[count:]
+    local_bins = piece_refs[0].shape[1]
+    bins = count * local_bins
     pairs = coef_ref.shape[0]
-    steps = local_bins // BLOCK
+
+    pair_copy = pltpu.make_async_copy(pair_hbm, pair_ref, pair_sem)
+    pair_copy.start()
+    own = ids_ref[0]
+    for ref in acc_refs:
+        ref[...] = jnp.zeros_like(ref)
 
     weights = weights_ref[...]
     for side, ref in enumerate((below_ref, above_ref)):
         for half in range(2):
-            cells = ref[:, half].reshape(bins, LANES)
+            blocks = [ref[ids_ref[1 + side] ^ block, half] for block in range(count)]
+            cells = jnp.concatenate(blocks, axis=0)
             drift = jnp.dot(weights, cells, preferred_element_type=jnp.float32)
             lanes = slice(half * LANES, (half + 1) * LANES)
             cur_ref[24 + side : 25 + side, lanes] = drift[0:1]
@@ -196,26 +271,27 @@
     at_first = lane == 0
     at_last = lane == LANES - 1
 
-    def advect(step, carry):
-        source = step // steps
-        start = pl.multiple_of((step - source * steps) * BLOCK, BLOCK)
-        first = source * local_bins + start
+    def advect(piece_ref, block, step):
+        start = pl.multiple_of(step * BLOCK, BLOCK)
+        first = block * local_bins + start
         span = pl.ds(start, BLOCK)
+        below_at = ids_ref[1] ^ block
+        above_at = ids_ref[2] ^ block
         speed_x = speeds_ref[0, pl.ds(pl.multiple_of(first, BLOCK), BLOCK), :]
         speed_y = speeds_ref[1, pl.ds(pl.multiple_of(first, BLOCK), BLOCK), :]
-
-        def cells(ref, chunk):
-            return ref[source, chunk, span, :].astype(jnp.float32)
 
         def row_flux(energy, row, half):
             current = cur_ref[row : row + 1, half * LANES : (half + 1) * LANES]
             return (speed_x + current) * energy
 
-        energy = [[cells(whole_ref, 2 * row + half) for half in range(2)] for row in range(3)]
+        energy = [
+            [piece_ref[2 * row + half, span, :].astype(jnp.float32) for half in range(2)]
+            for row in range(3)
+        ]
         for half in range(2):
-            flux = [row_flux(cells(below_ref, half), 0, half)]
+            flux = [row_flux(below_ref[below_at, half, span, :].astype(jnp.float32), 0, half)]
             flux += [row_flux(energy[row][half], row + 1, half) for row in range(3)]
-            flux += [row_flux(cells(above_ref, half), 4, half)]
+            flux += [row_flux(above_ref[above_at, half, span, :].astype(jnp.float32), 4, half)]
             for row in range(3):
                 energy[row][half] = (
                     energy[row][half],
@@ -248,13 +324,16 @@
                 result = wet * (moved[half] + left[half] - right[half])
                 rows = pl.ds(first * 8 + (2 * row + half), BLOCK, stride=8)
                 field_ref[rows, :] = result
-                acc_refs[0][rows, :] = result
-        zeros = jnp.zeros((BLOCK * 8, LANES), jnp.float32)
-        for ref in acc_refs[1:]:
-            ref[pl.ds(pl.multiple_of(first * 8, BLOCK * 8), BLOCK * 8), :] = zeros
-        return carry
-
-    lax.fori_loop(0, sources * steps, advect, 0)
+
+    for turn, piece_ref in enumerate(piece_refs):
+        block = own ^ turn
+
+        def one(step, carry, piece_ref=piece_ref, block=block):
+            advect(piece_ref, block, step)
+            return carry
+
+        lax.fori_loop(0, local_bins // BLOCK, one, 0)
+    pair_copy.wait()
 
     def interact(step, carry):
         start = pl.multiple_of(step * UNROLL, UNROLL)
@@ -267,7 +346,7 @@
             second = pl.ds(pl.multiple_of(seconds[item], 8), 8)
             target = pl.ds(pl.multiple_of(targets[item], 8), 8)
             ref = acc_refs[item % ACCS]
-            product = coefs[item] * (field_ref[first, :] * field_ref[second, :])
+            product = coefs[item : item + 1, :] * (field_ref[first, :] * field_ref[second, :])
             ref[target, :] = ref[target, :] + product
         return carry
 
@@ -278,15 +357,29 @@
         for row in range(3):
             for half in range(2):
                 rows = pl.ds(first * 8 + (2 * row + half), BLOCK, stride=8)
-                total = acc_refs[0][rows, :]
-                for ref in acc_refs[1:]:
+                total = field_ref[rows, :]
+                for ref in acc_refs:
                     total = total + ref[rows, :]
                 out_ref[row, pl.ds(first, BLOCK), half * LANES : (half + 1) * LANES] = (
                     total.astype(jnp.bfloat16)
                 )
         return carry
 
-    lax.fori_loop(0, bins // BLOCK, finish, 0)
+    parts = 4
+    out_copies = []
+    for part in range(parts):
+        span = pl.ds(part * (bins // parts), bins // parts)
+        each = bins // BLOCK // parts
+        lax.fori_loop(part * each, (part + 1) * each, finish, 0)
+        for row in range(3):
+            out_copies.append(
+                pltpu.make_async_copy(
+                    out_ref.at[row, span], out_hbm.at[row, span], out_sems.at[3 * part + row]
+                )
+            )
+            out_copies[-1].start()
+    for copy in out_copies:
+        copy.wait()
 
 
 def ocean_kernel(currents_ref, recv_ref, wet_ref, out_ref, wide_ref, rows_ref):
@@ -308,6 +401,32 @@
         cross = sign * pltpu.roll(x + rows_ref[...], half, 1)
         mixed = upper + lower - 2.0 * x
         out_ref[slot] = wet[:, slot : slot + 1] * (x + DT_OCEAN * (cross + MIXING * mixed))
+
+
+def wave_program(ids, pair_rows, coefs, speeds, below, above, surface, near, weights, wet, *pieces):
+    f32 = jnp.float32
+    count = len(pieces)
+    rows, columns = wet.shape
+    bins = speeds.shape[1]
+    return call(
+        functools.partial(wave_kernel, count),
+        jax.ShapeDtypeStruct((rows, bins, columns), jnp.bfloat16),
+        [in_smem(), in_hbm()] + [in_vmem()] * (8 + count),
+        in_hbm(),
+        [
+            SMEM(pair_rows.shape, jnp.int32),
+            VMEM((rows, bins, columns), jnp.bfloat16),
+            VMEM((bins * 8, LANES), f32),
+            VMEM((40, columns), f32),
+            pltpu.SemaphoreType.DMA,
+            pltpu.SemaphoreType.DMA((12,)),
+        ]
+        + [VMEM((bins * 8, LANES), f32)] * ACCS,
+        40_000_000,
+        8_000_000,
+        (ids, pair_rows, coefs, speeds, below, above, surface, near, weights, wet, *pieces),
+        WAVE_LIMIT,
+    )
 
 
 def per_device(
@@ -334,18 +453,34 @@
     space_at = lax.axis_index("space")
     bins_at = lax.axis_index("bins")
 
-    cells = spectrum.reshape(local_bins, bins_count, rows, 2, LANES)
-    cells = jnp.transpose(cells, (1, 2, 3, 0, 4)).reshape(bins_count, 6, local_bins, LANES)
-    kernel_copies = jnp.broadcast_to(
-        stokes_kernel[None, None], (bins_count, 1, local_bins, LANES)
-    )
-    whole = lax.all_to_all(
-        jnp.concatenate([cells, kernel_copies], axis=1),
-        "bins",
-        split_axis=0,
-        concat_axis=0,
-        tiled=True,
-    )
+    near_ids = [lax.rem(bins_at + step, bins_count) for step in (bins_count - 1, 1)]
+    ids = jnp.stack([bins_at, *near_ids]).astype(jnp.int32)
+
+    order = (4, 5, 2, 3, 6, 7, 1, 0)
+    piece_shape = (CHUNKS, local_bins, LANES)
+    sent = call(
+        functools.partial(pack_kernel, order),
+        [jax.ShapeDtypeStruct(piece_shape, bf16)] * bins_count,
+        [in_smem(), in_hbm(), in_hbm()],
+        [in_vmem()] * bins_count,
+        [
+            VMEM(spectrum.shape, bf16),
+            VMEM((2, local_bins * tile_rows, LANES), f32),
+            pltpu.SemaphoreType.DMA((3,)),
+            pltpu.SemaphoreType.DMA((bins_count,)),
+        ],
+        2_000_000,
+        4_000_000,
+        (
+            ids,
+            pltpu.with_memory_space_constraint(spectrum, pltpu.HBM),
+            pltpu.with_memory_space_constraint(stokes_kernel, pltpu.HBM),
+        ),
+    )
+    pieces = [sent[0]] * bins_count
+    for turn in order[:-1]:
+        partners = [(at, at ^ turn) for at in range(bins_count)]
+        pieces[turn] = lax.ppermute(sent[turn], "bins", partners)
 
     piece = local_bins // space_count
     speeds = lax.dynamic_slice(group_speed, (0, space_at * piece), (2, piece)).reshape(1, -1)
@@ -359,72 +494,74 @@
         4_000_000,
         500_000,
         (currents, ocean_wet, speeds),
-        "surface",
     )
     arrived = lax.all_to_all(surface, both, split_axis=0, concat_axis=0, tiled=True)
     map_row = col_map.reshape(1, -1)
-    surface_rows, speed_rows = call(
+    surface_rows, speed_rows, coefs = call(
         tables_kernel,
         (
             jax.ShapeDtypeStruct((32, columns), f32),
             jax.ShapeDtypeStruct((2, bins, LANES), f32),
+            jax.ShapeDtypeStruct((pairs, LANES), f32),
         ),
-        [in_vmem()] * 2,
-        (in_vmem(), in_vmem()),
+        [in_vmem()] * 3,
+        (in_vmem(),) * 3,
         [],
         600_000_000,
         1_300_000,
-        (arrived, map_row),
-        "tables",
-    )
+        (arrived.reshape(devices, LANES), map_row, pair_coef.reshape(-1, LANES)),
+    )
+
+    pair_rows = pair_bins.reshape(-1) * 8
 
     ahead = [(at, at + 1) for at in range(devices - 1)]
     back = [(at + 1, at) for at in range(devices - 1)]
-    below = lax.ppermute(whole[:, 4:6], both, ahead)
-    above = lax.ppermute(whole[:, 0:2], both, back)
+    halo_shape = (bins_count, 2, local_bins, LANES)
+    last_rows, first_rows = call(
+        edges_kernel,
+        [jax.ShapeDtypeStruct(halo_shape, bf16)] * 2,
+        [in_vmem()] * bins_count,
+        [in_vmem()] * 2,
+        [],
+        1_000_000,
+        2_400_000,
+        tuple(pieces),
+    )
+    below = lax.ppermute(last_rows, both, ahead)
+    above = lax.ppermute(first_rows, both, back)
 
     routed, near, weights = call(
-        drift_kernel,
+        functools.partial(drift_kernel, bins_count),
         (
             jax.ShapeDtypeStruct((devices * 8, LANES), bf16),
             jax.ShapeDtypeStruct((16, columns), f32),
             jax.ShapeDtypeStruct((32, bins), bf16),
         ),
-        [in_vmem()] * 2,
+        [in_smem(), in_vmem()] + [in_vmem()] * bins_count,
         (in_vmem(),) * 3,
-        [VMEM((devices * 8, LANES), f32)],
+        [VMEM((devices * 8, LANES), f32), VMEM((bins_count, local_bins, LANES), bf16)],
         300_000_000,
         2_500_000,
-        (whole, map_row),
-        "drift",
+        (ids, map_row, *pieces),
     )
     routed = lax.all_to_all(
         routed.reshape(devices, 8, LANES), both, split_axis=0, concat_axis=0, tiled=True
-    ).reshape(devices * 8, LANES)
+    )
+    routed = routed.reshape(devices * 8, LANES)
 
     own_wet = lax.dynamic_slice(wave_wet, (bins_at * rows, 0), (rows, columns))
-    new_spectrum = call(
-        wave_kernel,
-        jax.ShapeDtypeStruct((rows, bins, columns), bf16),
-        [in_smem()] * 2 + [in_vmem()] * 8,
-        in_vmem(),
-        [VMEM((bins * 8, LANES), f32), VMEM((40, columns), f32)]
-        + [VMEM((bins * 8, LANES), f32)] * ACCS,
-        40_000_000,
-        8_000_000,
-        (
-            pair_bins.reshape(-1) * 8,
-            pair_coef * DT_SOURCE,
-            whole,
-            below,
-            above,
-            speed_rows,
-            surface_rows,
-            near,
-            weights,
-            own_wet,
-        ),
-        "waves",
+    new_spectrum = wave_program(
+        ids,
+        pair_rows,
+        coefs,
+        speed_rows,
+        below,
+        above,
+        surface_rows,
+        near,
+        weights,
+        own_wet,
+        *pieces,
     )
     new_currents = call(
         ocean_kernel,
@@ -435,7 +572,6 @@
         4_000_000,
         1_500_000,
         (currents, routed, ocean_wet),
-        "ocean",
     )
     return (jnp.transpose(new_spectrum, (1, 0, 2)), new_currents)
 
@@ -452,6 +588,7 @@
         P("space", None),
         P(("space", "bins"), None),
     )
+
     return jax.shard_map(
         per_device,
         mesh=mesh,

time: 110 us -> 101 us (0.918)
  waiting for transfers between devices: 29.3 us -> 15.2 us
  starting transfers between devices: 30.3 us -> 36.9 us
  local copies, waits for them, and re-layouts: 9.23 us -> 12.3 us
  Pallas kernels: 37.5 us -> 35.3 us
  other arithmetic: 2.13 us -> 0.09 us
    all_to_all x1 -> x0, waiting for transfers between devices: 22.8 us -> none  [per_device(): lax.all_to_all(jnp.concatenate([cells, kernel_copies], axis=1), 'bins', s...]
    ppermute x2 -> x9, starting transfers between devices: 5.45 us -> 18.6 us  [the longest x7 13.4 us: per_device(): pieces[turn] = lax.ppermute(sent[turn], 'bins', partners)]
    ppermute x2 -> x9, waiting for transfers between devices: 0.01 us -> 10.6 us  [the longest x7 10.6 us: per_device(): pieces[turn] = lax.ppermute(sent[turn], 'bins', partners)]
    unnamed x20 -> x54, local copies, waits for them, and re-layouts: 2.03 us -> 12 us
    all_to_all x1 -> x0, starting transfers between devices: 6.09 us -> none  [per_device(): lax.all_to_all(jnp.concatenate([cells, kernel_copies], axis=1), 'bins', s...]
    reshape x2 -> x0, local copies, waits for them, and re-layouts: 4.07 us -> none  [per_device(): cells = spectrum.reshape(local_bins, bins_count, rows, 2, LANES)]
    pallas_call x5 -> x7, Pallas kernels: 37.5 us -> 35.3 us  [call(): pl.pallas_call(body, out_shape=out_shape, in_specs=ins, out_specs=outs, s...]
    all_to_all x1, waiting for transfers between devices: 6.44 us -> 4.6 us  [per_device(): lax.all_to_all(routed.reshape(devices, 8, LANES), both, split_axis=0, con...]
  transfers between devices with their start and end apart: 5 -> 11, of which waited for: 2 -> 4; matrix products, arithmetic and copies ran while one was open for 3% -> 0% of each run, Pallas kernels for 11% -> 9%
where the time goes in v3:
time: 101 us
  starting transfers between devices  36.9 us (37%)
  Pallas kernels  35.3 us (35%)
  waiting for transfers between devices  15.2 us (15%)
  local copies, waits for them, and re-layouts  12.3 us (12%)
    pallas_call x7, Pallas kernels, call(): pl.pallas_call(body, out_shape=out_shape, in_specs=ins, out_specs=outs, s...  35.3 us
    ppermute x7, starting transfers between devices, per_device(): pieces[turn] = lax.ppermute(sent[turn], 'bins', partners)  13.4 us
    unnamed x54, local copies, waits for them, and re-layouts  12 us
    all_to_all x1, starting transfers between devices, per_device(): lax.all_to_all(routed.reshape(devices, 8, LANES), both, split_axis=0, con...  10.7 us
    ppermute x7, waiting for transfers between devices, per_device(): pieces[turn] = lax.ppermute(sent[turn], 'bins', partners)  10.6 us
    all_to_all x1, starting transfers between devices, per_device(): lax.all_to_all(surface, both, split_axis=0, concat_axis=0, tiled=True)  7.54 us
    all_to_all x1, waiting for transfers between devices, per_device(): lax.all_to_all(routed.reshape(devices, 8, LANES), both, split_axis=0, con...  4.6 us
    ppermute x1, starting transfers between devices, per_device(): above = lax.ppermute(first_rows, both, back)  3.21 us
  transfers between devices with their start and end apart: 11, of which 4 were waited for; matrix products, arithmetic and copies ran while one was open for 0% of the time, Pallas kernels for 9%

profile of v3, /device:TPU:1, one launch (start us, length us, event | category | flops | bytes accessed | tf_op | source)
XLA Modules:
  0.0 100.6 jit_solution(13467342260305273822)
XLA Ops:
  0.6 0.0 copy-start
  0.6 0.0 copy-start.26
  0.7 0.0 copy-start.9
  0.7 0.0 copy-start.19
  0.7 0.1 pad_add_fusion.ids_ref
  0.8 3.4 %shard_map.106 = (bf16[7,144,128]{2,1,0:T(8,128)(2,1)S(1)}, bf16[7,144,128]{2,1,0:T(8,128)(2,1)S(1)}, bf16[7,144,128]{2,1,0:T(8,128)(2,1)S(1)}, bf16[7,144,128]{...) custom-call(s32[3]{0:T(128)S(1)} %pad_add_fusion.ids_ref, ...), custom_call_target="tpu_custom_call" | custom-call | flops 2000000 | bytes 4000000 | tf_op jit(solution)/shard_map/pallas_call | solution.py:43
  4.2 0.0 copy-start.22
  4.2 1.5 %collective-permute-start = (bf16[7,144,128]{2,1,0:T(8,128)(2,1)S(1)}, bf16[7,144,128]{2,1,0:T(8,128)(2,1)S(1)}, u32[]{:S(2)}, u32[]{:S(2)}) collective-permute-start(bf16[7,144,128]{2,1,0:T(8,128)(2,1)S(1)} %get-tuple-element.21), channel_id=1, source_target_pairs={{0,1},{1,0},{2,3},{3,2},{4,5},{5,4},{6,7},{7,6},{8,9},{9,8},{10,11... | collective-permute-start | bytes 774152 | tf_op jit(solution)/shard_map/ppermute | solution.py:483
  5.6 1.4 %collective-permute-start.1 = (bf16[7,144,128]{2,1,0:T(8,128)(2,1)S(1)}, bf16[7,144,128]{2,1,0:T(8,128)(2,1)S(1)}, u32[]{:S(2)}, u32[]{:S(2)}) collective-permute-start(bf16[7,144,128]{2,1,0:T(8,128)(2,1)S(1)} %get-tuple-element.22), channel_id=1, source_target_pairs={{0,2},{1,3},{2,0},{3,1},{4,6},{5,7},{6,4},{7,5},{8,10},{9,11},{10,... | collective-permute-start | bytes 774152 | tf_op jit(solution)/shard_map/ppermute | solution.py:483
  7.1 0.3 collective-permute-start.2
  7.4 3.0 %collective-permute-start.3 = (bf16[7,144,128]{2,1,0:T(8,128)(2,1)}, bf16[7,144,128]{2,1,0:T(8,128)(2,1)S(1)}, u32[]{:S(2)}, u32[]{:S(2)}) collective-permute-start(bf16[7,144,128]{2,1,0:T(8,128)(2,1)} %get-tuple-element.24), channel_id=1, source_target_pairs={{0,4},{1,5},{2,6},{3,7},{4,0},{5,1},{6,2},{7,3},{8,12},{9,13},{10,... | collective-permute-start | bytes 774152 | tf_op jit(solution)/shard_map/ppermute | solution.py:483
  10.4 0.2 collective-permute-start.4
  10.6 0.0 collective-permute-done.refs_1_
  10.6 2.9 %collective-permute-start.5 = (bf16[7,144,128]{2,1,0:T(8,128)(2,1)S(1)}, bf16[7,144,128]{2,1,0:T(8,128)(2,1)S(1)}, u32[]{:S(2)}, u32[]{:S(2)}) collective-permute-start(bf16[7,144,128]{2,1,0:T(8,128)(2,1)S(1)} %get-tuple-element.26), channel_id=1, source_target_pairs={{0,6},{1,7},{2,4},{3,5},{4,2},{5,3},{6,0},{7,1},{8,14},{9,15},{10,... | collective-permute-start | bytes 774152 | tf_op jit(solution)/shard_map/ppermute | solution.py:483
  13.5 0.0 collective-permute-done.1.refs_2_
  13.5 4.1 %collective-permute-start.6 = (bf16[7,144,128]{2,1,0:T(8,128)(2,1)S(1)}, bf16[7,144,128]{2,1,0:T(8,128)(2,1)S(1)}, u32[]{:S(2)}, u32[]{:S(2)}) collective-permute-start(bf16[7,144,128]{2,1,0:T(8,128)(2,1)S(1)} %get-tuple-element.27), channel_id=1, source_target_pairs={{0,7},{1,6},{2,5},{3,4},{4,3},{5,2},{6,1},{7,0},{8,15},{9,14},{10,... | collective-permute-start | bytes 774152 | tf_op jit(solution)/shard_map/ppermute | solution.py:483
  17.6 0.0 copy-done.26
  17.6 0.1 constant_dynamic-slice_fusion.1
  17.6 0.1 reshape.24
  17.7 0.1 pad.4.speed_ref
  17.8 0.0 copy-done.9
  17.8 0.0 copy-done.19
  17.8 1.3 %shard_map.104 = f32[128,128]{1,0:T(8,128)} custom-call(f32[2,384,128]{2,1,0:T(8,128)S(1)} %copy-done.9, s32[2,384]{1,0:T(2,128)S(1)} %copy-done.19, f32[1,128]{1,0:T(1,128)S(1)} %pad.4.speed_ref), custom_call_target="tpu_custom_call" | custom-call | flops 4000000 | bytes 500000 | tf_op jit(solution)/shard_map/pallas_call | solution.py:43
  19.1 7.5 %all-to-all-start = ((f32[128,1,128]{2,1,0:T(1,128)}), f32[128,1,128]{2,1,0:T(1,128)S(1)}, u32[]{:S(2)}, u32[]{:S(2)}) async-start(f32[128,1,128]{2,1,0:T(1,128)} %bitcast.4), calls=%async_computation | async-start | bytes 131072 | tf_op jit(solution)/shard_map/all_to_all | solution.py:498
  26.6 0.0 collective-permute-done.2.refs_3_
  26.6 0.4 collective-permute-done.3.refs_4_
  27.0 6.7 %collective-permute-done.4.refs_5_ = bf16[7,144,128]{2,1,0:T(8,128)(2,1)S(1)} collective-permute-done((bf16[7,144,128]{2,1,0:T(8,128)(2,1)S(1)}, bf16[7,144,128]{2,1,0:T(8,128)(2,1)S(1)}, u32[]{:S(2)}, u32[]{:S(2)}) %collective-permute-start.4) | collective-permute-done | bytes 258080 | tf_op jit(solution)/shard_map/ppermute | solution.py:483
  33.7 0.0 collective-permute-done.5.refs_6_
  33.7 3.5 %collective-permute-done.6.refs_7_ = bf16[7,144,128]{2,1,0:T(8,128)(2,1)S(1)} collective-permute-done((bf16[7,144,128]{2,1,0:T(8,128)(2,1)S(1)}, bf16[7,144,128]{2,1,0:T(8,128)(2,1)S(1)}, u32[]{:S(2)}, u32[]{:S(2)}) %collective-permute-start.6) | collective-permute-done | bytes 258080 | tf_op jit(solution)/shard_map/ppermute | solution.py:483
  37.2 1.1 %shard_map.107 = (bf16[8,2,144,128]{3,2,1,0:T(8,128)(2,1)}, bf16[8,2,144,128]{3,2,1,0:T(8,128)(2,1)}) custom-call(bf16[7,144,128]{2,1,0:T(8,128)(2,1)S(1)} %get-tuple-element.20.refs_0_, bf16[7,144,128]{2,1,0:T(8,128)(2,1)S(1)} %collective-permute-done.refs_1_, bf16[7,144,128]{2,1,0:T(8,128)(2,1)S(1)} %collective-permute-done.1.refs_2_, ...), custom_call_target="tpu_custom_call" | custom-call | flops 1000000 | bytes 2400000 | tf_op jit(solution)/shard_map/pallas_call | solution.py:43
  38.3 2.0 %collective-permute-start.7 = (bf16[8,2,144,128]{3,2,1,0:T(8,128)(2,1)}, bf16[8,2,144,128]{3,2,1,0:T(8,128)(2,1)}, u32[]{:S(2)}, u32[]{:S(2)}) collective-permute-start(bf16[8,2,144,128]{3,2,1,0:T(8,128)(2,1)} %get-tuple-element.28), channel_id=1, source_target_pairs={{0,1},{1,2},{2,3},{3,4},{4,5},{5,6},{6,7},{7,8},{8,9},{9,10},{10,1... | collective-permute-start | bytes 1769480 | tf_op jit(solution)/shard_map/ppermute | solution.py:530
  40.4 3.2 %collective-permute-start.8 = (bf16[8,2,144,128]{3,2,1,0:T(8,128)(2,1)}, bf16[8,2,144,128]{3,2,1,0:T(8,128)(2,1)}, u32[]{:S(2)}, u32[]{:S(2)}) collective-permute-start(bf16[8,2,144,128]{3,2,1,0:T(8,128)(2,1)} %get-tuple-element.29), channel_id=1, source_target_pairs={{1,0},{2,1},{3,2},{4,3},{5,4},{6,5},{7,6},{8,7},{9,8},{10,9},{11,1... | collective-permute-start | bytes 1769480 | tf_op jit(solution)/shard_map/ppermute | solution.py:531
  43.6 0.0 copy-done.20
  43.6 0.0 copy-done.22
  43.6 2.6 %shard_map.108 = (bf16[1024,128]{1,0:T(8,128)(2,1)}, f32[16,256]{1,0:T(8,128)S(1)}, bf16[32,1152]{1,0:T(8,128)(2,1)S(1)}) custom-call(s32[3]{0:T(128)S(1)} %pad_add_fusion.ids_ref, s32[1,128]{1,0:T(1,128)S(1)} %bitcast.13, bf16[7,144,128]{2,1,0:T(8,128)(2,1)S(1)} %get-tuple-element.20.refs_0_, bf16[7,144,128]{2,1,0:T(8,128)(2,1)S(1)} %collective-permute-done.refs_1_, ...), custom_call_target="tpu_custom_call" | custom-call | flops 300000000 | bytes 2500000 | tf_op jit(solution)/shard_map/pallas_call | solution.py:43
  46.3 0.0 copy-done.1
  46.3 0.0 copy-done.3
  46.3 0.0 copy-done.5
  46.3 0.0 copy-done.7
  46.3 0.0 all-to-all-done
  46.3 0.0 copy-start.13
  46.3 10.7 %all-to-all-start.1 = ((bf16[128,8,128]{2,1,0:T(8,128)(2,1)}), bf16[128,8,128]{2,1,0:T(8,128)(2,1)}, u32[]{:S(2)}, u32[]{:S(2)}) async-start(bf16[128,8,128]{2,1,0:T(8,128)(2,1)} %bitcast.9), calls=%async_computation.1 | async-start | bytes 524288 | tf_op jit(solution)/shard_map/all_to_all | solution.py:547
  57.2 0.0 copy-start.14
  57.2 0.8 copy-done.14
  58.0 0.7 copy-done.23
  58.7 0.7 copy-done.24
  59.4 2.2 %shard_map.105 = (f32[32,256]{1,0:T(8,128)S(1)}, f32[2,1152,128]{2,1,0:T(8,128)S(1)}, f32[4608,128]{1,0:T(8,128)S(1)}) custom-call(f32[128,128]{1,0:T(8,128)S(1)} %bitcast.12, s32[1,128]{1,0:T(1,128)S(1)} %bitcast.14, f32[36,128]{1,0:T(8,128)S(1)} %bitcast.15), custom_call_target="tpu_custom_call" | custom-call | flops 600000000 | bytes 1300000 | tf_op jit(solution)/shard_map/pallas_call | solution.py:43
  61.6 0.0 copy-start.11
  61.6 1.0 copy-done.11
  62.6 0.6 copy-done.15
  63.2 4.6 %all-to-all-done.1 = bf16[128,8,128]{2,1,0:T(8,128)(2,1)} async-done(((bf16[128,8,128]{2,1,0:T(8,128)(2,1)}), bf16[128,8,128]{2,1,0:T(8,128)(2,1)}, u32[]{:S(2)}, u32[]{:S(2)}) %all-to-all-start.1) | async-done | bytes 262176 | tf_op jit(solution)/shard_map/all_to_all | solution.py:547
  67.8 1.0 copy-done.10
  68.8 2.3 %shard_map.110 = f32[2,384,128]{2,1,0:T(8,128)} custom-call(f32[2,384,128]{2,1,0:T(8,128)S(1)} %copy-done.10, bf16[1024,128]{1,0:T(8,128)(2,1)} %bitcast.10.recv_ref, s32[2,384]{1,0:T(2,128)S(1)} %copy-done.19), custom_call_target="tpu_custom_call" | custom-call | flops 4000000 | bytes 1500000 | tf_op jit(solution)/shard_map/pallas_call | solution.py:43
  71.1 0.0 collective-permute-done.7.below_ref
  71.1 0.0 collective-permute-done.8.above_ref
  71.1 0.9 copy-done.2
  72.1 0.9 copy-done.4
  73.0 0.9 copy-done.6
  74.0 0.9 copy-done.8
  74.9 1.3 %copy-done.12 = f32[2,1152,128]{2,1,0:T(8,128)S(1)} copy-done((f32[2,1152,128]{2,1,0:T(8,128)S(1)}, f32[2,1152,128]{2,1,0:T(8,128)}, u32[]{:S(2)}) %copy-start.12) | copy-done | bytes 1179672
  76.2 0.8 copy-done.16
  76.9 0.7 copy-done.18
  77.7 0.6 copy-done.21
  78.2 22.4 %shard_map.109 = bf16[3,1152,256]{2,1,0:T(8,128)(2,1)} custom-call(s32[3]{0:T(128)S(1)} %copy-done.21, s32[13824]{0:T(1024)S(1)} %mul.16.pair_hbm, f32[4608,128]{1,0:T(8,128)S(1)} %get-tuple-element.18.coef_ref, f32[2,1152,128]{2,1,0:T(8,128)S(1)} %copy-done.12, bf16[8,2,144,128]{3,2,1,0:T(8,128)(2,1)} %collective-permute-done.7.below_ref, ...), custom_call_target="tpu_custom_call" | custom-call | flops 40000000 | bytes 8000000 | tf_op jit(solution)/shard_map/pallas_call | solution.py:43
  (26 shorter events, 0.1 us)
Async XLA Ops:
  0.6 56.5 %copy-start = (s32[24,256]{1,0:T(8,128)S(1)}, s32[24,256]{1,0:T(8,128)}, u32[]{:S(2)}) copy-start(s32[24,256]{1,0:T(8,128)} %param.16) | copy-start | bytes 73732
  0.6 16.9 %copy-start.26 = (f32[2,144]{1,0:T(2,128)S(1)}, f32[2,144]{1,0:T(2,128)}, u32[]{:S(2)}) copy-start(f32[2,144]{1,0:T(2,128)} %param.10) | copy-start | bytes 3460
  0.7 17.1 %copy-start.9 = (f32[2,384,128]{2,1,0:T(8,128)S(1)}, f32[2,384,128]{2,1,0:T(8,128)}, u32[]{:S(2)}) copy-start(f32[2,384,128]{2,1,0:T(8,128)} %currents_ref.3) | copy-start | bytes 1179652
  0.7 17.1 %copy-start.19 = (s32[2,384]{1,0:T(2,128)S(1)}, s32[2,384]{1,0:T(2,128)}, u32[]{:S(2)}) copy-start(s32[2,384]{1,0:T(2,128)} %wet_ref.3) | copy-start | bytes 9220
  0.8 42.9 %copy-start.20 = (s32[3]{0:T(128)}, s32[3]{0:T(128)S(1)}, u32[]{:S(2)}) copy-start(s32[3]{0:T(128)S(1)} %pad_add_fusion.ids_ref) | copy-start | bytes 40
  4.2 39.5 %copy-start.22 = (s32[128]{0:T(128)S(1)}, s32[128]{0:T(128)}, u32[]{:S(2)}) copy-start(s32[128]{0:T(128)} %param.15) | copy-start | bytes 1540
  4.2 6.5 %collective-permute-start = (bf16[7,144,128]{2,1,0:T(8,128)(2,1)S(1)}, bf16[7,144,128]{2,1,0:T(8,128)(2,1)S(1)}, u32[]{:S(2)}, u32[]{:S(2)}) collective-permute-start(bf16[7,144,128]{2,1,0:T(8,128)(2,1)S(1)} %get-tuple-element.21), channel_id=1, source_target_pairs={{0,1},{1,0},{2,3},{3,2},{4,5},{5,4},{6,7},{7,6},{8,9},{9,8},{10,11... | collective-permute-start | bytes 774152 | tf_op jit(solution)/shard_map/ppermute | solution.py:483
  5.6 7.9 %collective-permute-start.1 = (bf16[7,144,128]{2,1,0:T(8,128)(2,1)S(1)}, bf16[7,144,128]{2,1,0:T(8,128)(2,1)S(1)}, u32[]{:S(2)}, u32[]{:S(2)}) collective-permute-start(bf16[7,144,128]{2,1,0:T(8,128)(2,1)S(1)} %get-tuple-element.22), channel_id=1, source_target_pairs={{0,2},{1,3},{2,0},{3,1},{4,6},{5,7},{6,4},{7,5},{8,10},{9,11},{10,... | collective-permute-start | bytes 774152 | tf_op jit(solution)/shard_map/ppermute | solution.py:483
  7.1 19.6 %collective-permute-start.2 = (bf16[7,144,128]{2,1,0:T(8,128)(2,1)}, bf16[7,144,128]{2,1,0:T(8,128)(2,1)S(1)}, u32[]{:S(2)}, u32[]{:S(2)}) collective-permute-start(bf16[7,144,128]{2,1,0:T(8,128)(2,1)} %get-tuple-element.23), channel_id=1, source_target_pairs={{0,3},{1,2},{2,1},{3,0},{4,7},{5,6},{6,5},{7,4},{8,11},{9,10},{10,... | collective-permute-start | bytes 774152 | tf_op jit(solution)/shard_map/ppermute | solution.py:483
  7.4 19.6 %collective-permute-start.3 = (bf16[7,144,128]{2,1,0:T(8,128)(2,1)}, bf16[7,144,128]{2,1,0:T(8,128)(2,1)S(1)}, u32[]{:S(2)}, u32[]{:S(2)}) collective-permute-start(bf16[7,144,128]{2,1,0:T(8,128)(2,1)} %get-tuple-element.24), channel_id=1, source_target_pairs={{0,4},{1,5},{2,6},{3,7},{4,0},{5,1},{6,2},{7,3},{8,12},{9,13},{10,... | collective-permute-start | bytes 774152 | tf_op jit(solution)/shard_map/ppermute | solution.py:483
  10.4 23.3 %collective-permute-start.4 = (bf16[7,144,128]{2,1,0:T(8,128)(2,1)S(1)}, bf16[7,144,128]{2,1,0:T(8,128)(2,1)S(1)}, u32[]{:S(2)}, u32[]{:S(2)}) collective-permute-start(bf16[7,144,128]{2,1,0:T(8,128)(2,1)S(1)} %get-tuple-element.25), channel_id=1, source_target_pairs={{0,5},{1,4},{2,7},{3,6},{4,1},{5,0},{6,3},{7,2},{8,13},{9,12},{10,... | collective-permute-start | bytes 774152 | tf_op jit(solution)/shard_map/ppermute | solution.py:483
  10.6 23.1 %collective-permute-start.5 = (bf16[7,144,128]{2,1,0:T(8,128)(2,1)S(1)}, bf16[7,144,128]{2,1,0:T(8,128)(2,1)S(1)}, u32[]{:S(2)}, u32[]{:S(2)}) collective-permute-start(bf16[7,144,128]{2,1,0:T(8,128)(2,1)S(1)} %get-tuple-element.26), channel_id=1, source_target_pairs={{0,6},{1,7},{2,4},{3,5},{4,2},{5,3},{6,0},{7,1},{8,14},{9,15},{10,... | collective-permute-start | bytes 774152 | tf_op jit(solution)/shard_map/ppermute | solution.py:483
  13.5 23.7 %collective-permute-start.6 = (bf16[7,144,128]{2,1,0:T(8,128)(2,1)S(1)}, bf16[7,144,128]{2,1,0:T(8,128)(2,1)S(1)}, u32[]{:S(2)}, u32[]{:S(2)}) collective-permute-start(bf16[7,144,128]{2,1,0:T(8,128)(2,1)S(1)} %get-tuple-element.27), channel_id=1, source_target_pairs={{0,7},{1,6},{2,5},{3,4},{4,3},{5,2},{6,1},{7,0},{8,15},{9,14},{10,... | collective-permute-start | bytes 774152 | tf_op jit(solution)/shard_map/ppermute | solution.py:483
  19.1 27.2 %all-to-all-start = ((f32[128,1,128]{2,1,0:T(1,128)}), f32[128,1,128]{2,1,0:T(1,128)S(1)}, u32[]{:S(2)}, u32[]{:S(2)}) async-start(f32[128,1,128]{2,1,0:T(1,128)} %bitcast.4), calls=%async_computation | async-start | bytes 131072 | tf_op jit(solution)/shard_map/all_to_all | solution.py:498
  27.0 19.2 %copy-start.1 = (bf16[7,144,128]{2,1,0:T(8,128)(2,1)}, bf16[7,144,128]{2,1,0:T(8,128)(2,1)S(1)}, u32[]{:S(2)}) copy-start(bf16[7,144,128]{2,1,0:T(8,128)(2,1)S(1)} %collective-permute-done.3.refs_4_) | copy-start | bytes 774148
  33.7 12.6 %copy-start.3 = (bf16[7,144,128]{2,1,0:T(8,128)(2,1)}, bf16[7,144,128]{2,1,0:T(8,128)(2,1)S(1)}, u32[]{:S(2)}) copy-start(bf16[7,144,128]{2,1,0:T(8,128)(2,1)S(1)} %collective-permute-done.4.refs_5_) | copy-start | bytes 774148
  33.7 12.6 %copy-start.5 = (bf16[7,144,128]{2,1,0:T(8,128)(2,1)}, bf16[7,144,128]{2,1,0:T(8,128)(2,1)S(1)}, u32[]{:S(2)}) copy-start(bf16[7,144,128]{2,1,0:T(8,128)(2,1)S(1)} %collective-permute-done.5.refs_6_) | copy-start | bytes 774148
  37.2 9.0 %copy-start.7 = (bf16[7,144,128]{2,1,0:T(8,128)(2,1)}, bf16[7,144,128]{2,1,0:T(8,128)(2,1)S(1)}, u32[]{:S(2)}) copy-start(bf16[7,144,128]{2,1,0:T(8,128)(2,1)S(1)} %collective-permute-done.6.refs_7_) | copy-start | bytes 774148
  38.3 18.7 %copy-start.25 = (s32[3,4608]{1,0:T(4,128)S(1)}, s32[3,4608]{1,0:T(4,128)}, u32[]{:S(2)}) copy-start(s32[3,4608]{1,0:T(4,128)} %param.12) | copy-start | bytes 165892
  38.3 32.8 %collective-permute-start.7 = (bf16[8,2,144,128]{3,2,1,0:T(8,128)(2,1)}, bf16[8,2,144,128]{3,2,1,0:T(8,128)(2,1)}, u32[]{:S(2)}, u32[]{:S(2)}) collective-permute-start(bf16[8,2,144,128]{3,2,1,0:T(8,128)(2,1)} %get-tuple-element.28), channel_id=1, source_target_pairs={{0,1},{1,2},{2,3},{3,4},{4,5},{5,6},{6,7},{7,8},{8,9},{9,10},{10,1... | collective-permute-start | bytes 1769480 | tf_op jit(solution)/shard_map/ppermute | solution.py:530
  40.4 30.7 %collective-permute-start.8 = (bf16[8,2,144,128]{3,2,1,0:T(8,128)(2,1)}, bf16[8,2,144,128]{3,2,1,0:T(8,128)(2,1)}, u32[]{:S(2)}, u32[]{:S(2)}) collective-permute-start(bf16[8,2,144,128]{3,2,1,0:T(8,128)(2,1)} %get-tuple-element.29), channel_id=1, source_target_pairs={{1,0},{2,1},{3,2},{4,3},{5,4},{6,5},{7,6},{8,7},{9,8},{10,9},{11,1... | collective-permute-start | bytes 1769480 | tf_op jit(solution)/shard_map/ppermute | solution.py:531
  46.3 10.8 %copy-start.17 = (f32[16,256]{1,0:T(8,128)}, f32[16,256]{1,0:T(8,128)S(1)}, u32[]{:S(2)}) copy-start(f32[16,256]{1,0:T(8,128)S(1)} %get-tuple-element.31.near_ref) | copy-start | bytes 49156
  46.3 10.9 %copy-start.13 = (f32[128,1,128]{2,1,0:T(1,128)}, f32[128,1,128]{2,1,0:T(1,128)S(1)}, u32[]{:S(2)}) copy-start(f32[128,1,128]{2,1,0:T(1,128)S(1)} %all-to-all-done) | copy-start | bytes 196612
  46.3 21.5 %all-to-all-start.1 = ((bf16[128,8,128]{2,1,0:T(8,128)(2,1)}), bf16[128,8,128]{2,1,0:T(8,128)(2,1)}, u32[]{:S(2)}, u32[]{:S(2)}) async-start(bf16[128,8,128]{2,1,0:T(8,128)(2,1)} %bitcast.9), calls=%async_computation.1 | async-start | bytes 524288 | tf_op jit(solution)/shard_map/all_to_all | solution.py:547
  57.2 0.8 copy-start.14
  58.0 0.7 copy-start.23
  58.7 0.7 copy-start.24
  61.6 1.0 %copy-start.11 = (f32[2,1152,128]{2,1,0:T(8,128)}, f32[2,1152,128]{2,1,0:T(8,128)S(1)}, u32[]{:S(2)}) copy-start(f32[2,1152,128]{2,1,0:T(8,128)S(1)} %get-tuple-element.19.speeds_ref) | copy-start | bytes 3538948
  62.6 0.6 copy-start.15
  67.8 1.0 copy-start.10
  71.1 1.0 copy-start.2
  72.1 0.9 copy-start.4
  73.0 0.9 copy-start.6
  74.0 0.9 copy-start.8
  74.9 1.3 %copy-start.12 = (f32[2,1152,128]{2,1,0:T(8,128)S(1)}, f32[2,1152,128]{2,1,0:T(8,128)}, u32[]{:S(2)}) copy-start(f32[2,1152,128]{2,1,0:T(8,128)} %copy-done.11) | copy-start | bytes 3538948
  76.2 0.8 copy-start.16
  76.9 0.7 copy-start.18
  77.7 0.6 copy-start.21

commit v4 on v3

--- a/solution.py
+++ b/solution.py
@@ -16,12 +16,14 @@
 
 LANES = 128
 ACCS = 3
-WAVE_LIMIT = 24
+WAVE_LIMIT = 36
 CHUNKS = 7
 UNROLL = 48
 BLOCK = 16
+PITCH = 24
 ROW_GAP = 400
 SPEED_LANE = 32
+PIECES = 16
 HIGHEST = lax.Precision.HIGHEST
 VMEM = pltpu.VMEM
 SMEM = pltpu.SMEM
@@ -37,6 +39,10 @@
 
 def in_hbm():
     return pl.BlockSpec(memory_space=pltpu.HBM)
+
+
+def kept_in(space, *values):
+    return [pltpu.with_memory_space_constraint(value, space) for value in values]
 
 
 def call(body, out_shape, ins, outs, scratch, flops, moved, args, limit=16):
@@ -111,7 +117,7 @@
     return jnp.concatenate([wet, jnp.zeros((6, rows), jnp.float32)], axis=0).T
 
 
-def surface_kernel(currents_ref, wet_ref, speed_ref, out_ref, rows_ref):
+def surface_kernel(ids_ref, currents_ref, wet_ref, speed_ref, out_ref, rows_ref):
     rows = currents_ref.shape[1]
     half = LANES // 2
     lane = lax.broadcasted_iota(jnp.int32, (rows, LANES), 1)
@@ -127,7 +133,21 @@
         value = column * (x + DT_OCEAN * (cross + MIXING * (below - x)))
         value = jnp.where(lane == 1, column, value)
         rows_ref[pl.ds(slot * ROW_GAP + 8, rows), :] = jnp.where(kept, value, 0.0)
-    total = jnp.broadcast_to(speed_ref[...], (LANES, LANES))
+    local_bins = speed_ref.shape[1]
+    piece = local_bins // PIECES
+    index = lax.broadcasted_iota(jnp.int32, (local_bins, LANES), 0) - ids_ref[3] * piece
+    place = lax.broadcasted_iota(jnp.int32, (local_bins, LANES), 1) - SPEED_LANE
+    inside = (index >= 0) & (index < piece)
+    speeds = jnp.zeros((1, LANES), jnp.float32)
+    for part in range(2):
+        pick = (inside & (place == index + part * piece)).astype(jnp.float32)
+        speeds = speeds + jnp.dot(
+            speed_ref[part : part + 1, :],
+            pick,
+            precision=HIGHEST,
+            preferred_element_type=jnp.float32,
+        )
+    total = jnp.broadcast_to(speeds, (LANES, LANES))
     for slot in range(2):
         for row in range(5):
             part = rows_ref[pl.ds(slot * ROW_GAP + 7 + row, LANES, stride=3), :]
@@ -147,8 +167,14 @@
     return (2.0 * column + float(slot)) == index
 
 
-def tables_kernel(recv_ref, map_ref, coef_ref, surface_ref, speeds_ref, coefs_ref):
+def tables_kernel(
+    recv_ref, map_ref, coef_ref, pair_ref, surface_ref, speeds_ref, coefs_ref, rows_ref
+):
     for block in range(coef_ref.shape[0]):
+        lanes = slice(block * LANES, (block + 1) * LANES)
+        for side in range(3):
+            at = side * coef_ref.shape[0] + block
+            rows_ref[at : at + 1, :] = pair_ref[side : side + 1, lanes] * 8
         row = DT_SOURCE * coef_ref[block : block + 1, :]
         coefs_ref[block * LANES : (block + 1) * LANES, :] = jnp.broadcast_to(
             row, (LANES, LANES)
@@ -219,10 +245,10 @@
     count,
     ids_ref,
     pair_hbm,
-    coef_ref,
-    speeds_ref,
-    below_ref,
-    above_ref,
+    coef_hbm,
+    speeds_hbm,
+    below_hbm,
+    above_hbm,
     surface_ref,
     near_ref,
     weights_ref,
@@ -230,17 +256,59 @@
     *refs,
 ):
     piece_refs = refs[:count]
-    out_hbm, pair_ref, out_ref, field_ref, cur_ref, pair_sem, out_sems, *acc_refs = refs[count:]
+    (
+        out_hbm,
+        pair_ref,
+        coef_ref,
+        speeds_ref,
+        below_ref,
+        above_ref,
+        out_ref,
+        field_ref,
+        cur_ref,
+        turn_ref,
+        beside_ref,
+        in_sems,
+        out_sems,
+        *acc_refs,
+    ) = refs[count:]
     local_bins = piece_refs[0].shape[1]
     bins = count * local_bins
     pairs = coef_ref.shape[0]
 
-    pair_copy = pltpu.make_async_copy(pair_hbm, pair_ref, pair_sem)
-    pair_copy.start()
+    moves = (
+        (below_hbm, below_ref),
+        (above_hbm, above_ref),
+        (speeds_hbm, speeds_ref),
+        (pair_hbm, pair_ref),
+        (coef_hbm, coef_ref),
+    )
+    loads = [
+        pltpu.make_async_copy(src, dst, in_sems.at[at]) for at, (src, dst) in enumerate(moves)
+    ]
+    for copy in loads:
+        copy.start()
     own = ids_ref[0]
-    for ref in acc_refs:
-        ref[...] = jnp.zeros_like(ref)
-
+    turn_ref[...] = jnp.zeros_like(turn_ref)
+
+    columns = 2 * LANES
+    given = lax.broadcasted_iota(jnp.int32, (columns, 2 * columns), 0)
+    taken = lax.broadcasted_iota(jnp.int32, (columns, 2 * columns), 1)
+    pick = given == jnp.where(taken < columns, taken - 1, taken - columns + 1)
+    pick = pick.astype(jnp.float32)
+    narrow_pick = pick.astype(jnp.bfloat16)
+    for row in range(3):
+        cells = jnp.concatenate(
+            [joined(piece_refs, 2 * row), joined(piece_refs, 2 * row + 1)], axis=1
+        )
+        beside = jnp.dot(cells, narrow_pick, preferred_element_type=jnp.float32)
+        for part in range(4):
+            beside_ref[row, part] = beside[:, part * LANES : (part + 1) * LANES].astype(
+                jnp.bfloat16
+            )
+
+    loads[0].wait()
+    loads[1].wait()
     weights = weights_ref[...]
     for side, ref in enumerate((below_ref, above_ref)):
         for half in range(2):
@@ -265,13 +333,17 @@
         cur_ref[row : row + 1, :] = CURRENT_SCALE * jnp.tanh(fixed_east + factor * north)
         cur_ref[8 + row : 9 + row, :] = CURRENT_SCALE * jnp.tanh(fixed_north - factor * east)
     for row in range(3):
-        cur_ref[16 + row : 17 + row, :] = wet_ref[row : row + 1, :].astype(jnp.float32)
-
-    lane = lax.broadcasted_iota(jnp.int32, (BLOCK, LANES), 1)
-    at_first = lane == 0
-    at_last = lane == LANES - 1
-
-    def advect(piece_ref, block, step):
+        wet = wet_ref[pl.ds(own * 3 + row, 1), :]
+        cur_ref[16 + row : 17 + row, :] = wet.astype(jnp.float32)
+
+    near_cur = jnp.dot(
+        cur_ref[8:16, :], pick, precision=HIGHEST, preferred_element_type=jnp.float32
+    )
+    cur_ref[40:48, :] = near_cur[:, :columns]
+    cur_ref[48:56, :] = near_cur[:, columns:]
+    loads[2].wait()
+
+    def advect(piece_ref, turn, block, step):
         start = pl.multiple_of(step * BLOCK, BLOCK)
         first = block * local_bins + start
         span = pl.ds(start, BLOCK)
@@ -301,39 +373,40 @@
                     - jnp.minimum(flux[row + 2], 0.0),
                 )
         for row in range(3):
-            forward = []
-            backward = []
-            moved = []
             for half in range(2):
                 old, value = energy[row][half]
-                current = cur_ref[9 + row : 10 + row, half * LANES : (half + 1) * LANES]
-                side = (speed_y + current) * old
-                moved.append(value - jnp.abs(side))
-                forward.append(pltpu.roll(jnp.maximum(side, 0.0), 1, 1))
-                backward.append(pltpu.roll(jnp.minimum(side, 0.0), LANES - 1, 1))
-            left = [
-                jnp.where(at_first, 0.0, forward[0]),
-                jnp.where(at_first, forward[0], forward[1]),
-            ]
-            right = [
-                jnp.where(at_last, backward[1], backward[0]),
-                jnp.where(at_last, 0.0, backward[1]),
-            ]
-            for half in range(2):
-                wet = cur_ref[16 + row : 17 + row, half * LANES : (half + 1) * LANES]
-                result = wet * (moved[half] + left[half] - right[half])
-                rows = pl.ds(first * 8 + (2 * row + half), BLOCK, stride=8)
-                field_ref[rows, :] = result
+                lanes = slice(half * LANES, (half + 1) * LANES)
+                spot = pl.ds(pl.multiple_of(turn * local_bins + start, BLOCK), BLOCK)
+
+                def side(at, cells, row=row, lanes=lanes):
+                    return (speed_y + cur_ref[at + 1 + row : at + 2 + row, lanes]) * cells
+
+                left = side(40, beside_ref[row, half, spot, :].astype(jnp.float32))
+                right = side(48, beside_ref[row, 2 + half, spot, :].astype(jnp.float32))
+                wet = cur_ref[16 + row : 17 + row, lanes]
+                moved = value - jnp.abs(side(8, old))
+                result = wet * (moved + jnp.maximum(left, 0.0) - jnp.minimum(right, 0.0))
+                at = (2 * row + half) * PITCH
+                turn_ref[at : at + BLOCK, :] = result
+        zeros = jnp.zeros((8, LANES), jnp.float32)
+        for item in range(BLOCK):
+            rows = pl.ds(pl.multiple_of((first + item) * 8, 8), 8)
+            tile = turn_ref[pl.ds(item, 8, stride=PITCH), :]
+            field_ref[rows, :] = tile
+            acc_refs[0][rows, :] = tile
+            for ref in acc_refs[1:]:
+                ref[rows, :] = zeros
 
     for turn, piece_ref in enumerate(piece_refs):
         block = own ^ turn
 
-        def one(step, carry, piece_ref=piece_ref, block=block):
-            advect(piece_ref, block, step)
+        def one(step, carry, piece_ref=piece_ref, turn=turn, block=block):
+            advect(piece_ref, turn, block, step)
             return carry
 
         lax.fori_loop(0, local_bins // BLOCK, one, 0)
-    pair_copy.wait()
+    loads[3].wait()
+    loads[4].wait()
 
     def interact(step, carry):
         start = pl.multiple_of(step * UNROLL, UNROLL)
@@ -357,8 +430,8 @@
         for row in range(3):
             for half in range(2):
                 rows = pl.ds(first * 8 + (2 * row + half), BLOCK, stride=8)
-                total = field_ref[rows, :]
-                for ref in acc_refs:
+                total = acc_refs[0][rows, :]
+                for ref in acc_refs[1:]:
                     total = total + ref[rows, :]
                 out_ref[row, pl.ds(first, BLOCK), half * LANES : (half + 1) * LANES] = (
                     total.astype(jnp.bfloat16)
@@ -406,25 +479,40 @@
 def wave_program(ids, pair_rows, coefs, speeds, below, above, surface, near, weights, wet, *pieces):
     f32 = jnp.float32
     count = len(pieces)
-    rows, columns = wet.shape
+    columns = wet.shape[1]
+    rows = wet.shape[0] // count
     bins = speeds.shape[1]
     return call(
         functools.partial(wave_kernel, count),
         jax.ShapeDtypeStruct((rows, bins, columns), jnp.bfloat16),
-        [in_smem(), in_hbm()] + [in_vmem()] * (8 + count),
+        [in_smem()] + [in_hbm()] * 5 + [in_vmem()] * (4 + count),
         in_hbm(),
         [
             SMEM(pair_rows.shape, jnp.int32),
+            VMEM(coefs.shape, f32),
+            VMEM(speeds.shape, f32),
+            VMEM(below.shape, jnp.bfloat16),
+            VMEM(above.shape, jnp.bfloat16),
             VMEM((rows, bins, columns), jnp.bfloat16),
             VMEM((bins * 8, LANES), f32),
-            VMEM((40, columns), f32),
-            pltpu.SemaphoreType.DMA,
+            VMEM((56, columns), f32),
+            VMEM((8 * PITCH, LANES), f32),
+            VMEM((rows, 4, bins, LANES), jnp.bfloat16),
+            pltpu.SemaphoreType.DMA((5,)),
             pltpu.SemaphoreType.DMA((12,)),
         ]
         + [VMEM((bins * 8, LANES), f32)] * ACCS,
         40_000_000,
         8_000_000,
-        (ids, pair_rows, coefs, speeds, below, above, surface, near, weights, wet, *pieces),
+        (
+            ids,
+            *kept_in(pltpu.HBM, pair_rows, coefs, speeds, below, above),
+            surface,
+            near,
+            weights,
+            wet,
+            *kept_in(VMEM, *pieces),
+        ),
         WAVE_LIMIT,
     )
 
@@ -444,7 +532,6 @@
     space_count = lax.axis_size("space")
     bins_count = lax.axis_size("bins")
     devices = space_count * bins_count
-    rows = tile_rows // bins_count
     bins = local_bins * bins_count
     pairs = pair_bins.shape[1]
     both = ("space", "bins")
@@ -454,9 +541,9 @@
     bins_at = lax.axis_index("bins")
 
     near_ids = [lax.rem(bins_at + step, bins_count) for step in (bins_count - 1, 1)]
-    ids = jnp.stack([bins_at, *near_ids]).astype(jnp.int32)
-
-    order = (4, 5, 2, 3, 6, 7, 1, 0)
+    ids = jnp.stack([bins_at, *near_ids, space_at]).astype(jnp.int32)
+
+    order = (4, 5, 2, 6, 3, 7, 1, 0)
     piece_shape = (CHUNKS, local_bins, LANES)
     sent = call(
         functools.partial(pack_kernel, order),
@@ -482,37 +569,33 @@
         partners = [(at, at ^ turn) for at in range(bins_count)]
         pieces[turn] = lax.ppermute(sent[turn], "bins", partners)
 
-    piece = local_bins // space_count
-    speeds = lax.dynamic_slice(group_speed, (0, space_at * piece), (2, piece)).reshape(1, -1)
-    speeds = jnp.pad(speeds, ((0, 0), (SPEED_LANE, LANES - SPEED_LANE - 2 * piece)))
     surface = call(
         surface_kernel,
         jax.ShapeDtypeStruct((devices, LANES), f32),
-        [in_vmem()] * 3,
+        [in_smem()] + [in_vmem()] * 3,
         in_vmem(),
         [VMEM((2 * ROW_GAP, LANES), f32)],
         4_000_000,
         500_000,
-        (currents, ocean_wet, speeds),
+        (ids, currents, ocean_wet, group_speed),
     )
     arrived = lax.all_to_all(surface, both, split_axis=0, concat_axis=0, tiled=True)
     map_row = col_map.reshape(1, -1)
-    surface_rows, speed_rows, coefs = call(
+    surface_rows, speed_rows, coefs, pair_rows = call(
         tables_kernel,
         (
             jax.ShapeDtypeStruct((32, columns), f32),
             jax.ShapeDtypeStruct((2, bins, LANES), f32),
             jax.ShapeDtypeStruct((pairs, LANES), f32),
+            jax.ShapeDtypeStruct((3 * pairs // LANES, LANES), jnp.int32),
         ),
-        [in_vmem()] * 3,
-        (in_vmem(),) * 3,
+        [in_vmem()] * 4,
+        (in_vmem(),) * 4,
         [],
         600_000_000,
         1_300_000,
-        (arrived.reshape(devices, LANES), map_row, pair_coef.reshape(-1, LANES)),
-    )
-
-    pair_rows = pair_bins.reshape(-1) * 8
+        (arrived.reshape(devices, LANES), map_row, pair_coef.reshape(-1, LANES), pair_bins),
+    )
 
     ahead = [(at, at + 1) for at in range(devices - 1)]
     back = [(at + 1, at) for at in range(devices - 1)]
@@ -549,10 +632,9 @@
     )
     routed = routed.reshape(devices * 8, LANES)
 
-    own_wet = lax.dynamic_slice(wave_wet, (bins_at * rows, 0), (rows, columns))
     new_spectrum = wave_program(
         ids,
-        pair_rows,
+        pair_rows.reshape(-1),
         coefs,
         speed_rows,
         below,
@@ -560,7 +642,7 @@
         surface_rows,
         near,
         weights,
-        own_wet,
+        wave_wet,
         *pieces,
     )
     new_currents = call(

time: 101 us -> 100 us (0.990)
  waiting for transfers between devices: 15.2 us -> 30.9 us
  local copies, waits for them, and re-layouts: 12.3 us -> 3.99 us
  Pallas kernels: 35.3 us -> 30.6 us
  starting transfers between devices: 36.9 us -> 33.4 us
    ppermute x7, waiting for transfers between devices: 10.6 us -> 19 us  [per_device(): pieces[turn] = lax.ppermute(sent[turn], 'bins', partners)]
    unnamed x54 -> x20, local copies, waits for them, and re-layouts: 12 us -> 3.99 us
    all_to_all x1, waiting for transfers between devices: 0.01 us -> 7 us  [per_device(): lax.all_to_all(surface, both, split_axis=0, concat_axis=0, tiled=True)]
    all_to_all x1, starting transfers between devices: 10.7 us -> 4.42 us  [per_device(): lax.all_to_all(routed.reshape(devices, 8, LANES), both, split_axis=0, con...]
    pallas_call x7, Pallas kernels: 35.3 us -> 30.6 us  [call(): pl.pallas_call(body, out_shape=out_shape, in_specs=ins, out_specs=outs, s...]
    all_to_all x1, starting transfers between devices: 7.54 us -> 10.3 us  [per_device(): lax.all_to_all(surface, both, split_axis=0, concat_axis=0, tiled=True)]
  transfers between devices with their start and end apart: 11 -> 11, of which waited for: 4 -> 6; matrix products, arithmetic and copies ran while one was open for 0% -> 0% of each run, Pallas kernels for 9% -> 8%
where the time goes in v4:
time: 100 us; the launch traced here: 99.7 us
  starting transfers between devices  33.4 us (33%)
  waiting for transfers between devices  30.9 us (31%)
  Pallas kernels  30.6 us (31%)
  local copies, waits for them, and re-layouts  3.99 us (4%)
    pallas_call x7, Pallas kernels, call(): pl.pallas_call(body, out_shape=out_shape, in_specs=ins, out_specs=outs, s...  30.6 us
    ppermute x7, waiting for transfers between devices, per_device(): pieces[turn] = lax.ppermute(sent[turn], 'bins', partners)  19 us
    ppermute x7, starting transfers between devices, per_device(): pieces[turn] = lax.ppermute(sent[turn], 'bins', partners)  13.4 us
    all_to_all x1, starting transfers between devices, per_device(): lax.all_to_all(surface, both, split_axis=0, concat_axis=0, tiled=True)  10.3 us
    all_to_all x1, waiting for transfers between devices, per_device(): lax.all_to_all(surface, both, split_axis=0, concat_axis=0, tiled=True)  7 us
    all_to_all x1, waiting for transfers between devices, per_device(): lax.all_to_all(routed.reshape(devices, 8, LANES), both, split_axis=0, con...  4.91 us
    all_to_all x1, starting transfers between devices, per_device(): lax.all_to_all(routed.reshape(devices, 8, LANES), both, split_axis=0, con...  4.42 us
    unnamed x20, local copies, waits for them, and re-layouts  3.99 us
  transfers between devices with their start and end apart: 11, of which 6 were waited for; matrix products, arithmetic and copies ran while one was open for 0% of the time, Pallas kernels for 8%

profile of v4, /device:TPU:1, one launch (start us, length us, event | category | flops | bytes accessed | tf_op | source)
XLA Modules:
  0.0 99.7 jit_solution(5458182432093399628)
XLA Ops:
  0.6 0.1 pad_add_fusion.ids_ref
  0.7 0.0 copy-start.1
  0.7 0.0 copy-start.5
  0.7 0.0 copy-start.6
  0.7 2.6 %shard_map.106 = (bf16[7,144,128]{2,1,0:T(8,128)(2,1)S(1)}, bf16[7,144,128]{2,1,0:T(8,128)(2,1)S(1)}, bf16[7,144,128]{2,1,0:T(8,128)(2,1)S(1)}, bf16[7,144,128]{...) custom-call(s32[4]{0:T(128)S(1)} %pad_add_fusion.ids_ref, ...), custom_call_target="tpu_custom_call" | custom-call | flops 2000000 | bytes 4000000 | tf_op jit(solution)/shard_map/pallas_call | solution.py:49
  3.3 0.0 copy-start.7
  3.3 1.5 %collective-permute-start = (bf16[7,144,128]{2,1,0:T(8,128)(2,1)S(1)}, bf16[7,144,128]{2,1,0:T(8,128)(2,1)S(1)}, u32[]{:S(2)}, u32[]{:S(2)}) collective-permute-start(bf16[7,144,128]{2,1,0:T(8,128)(2,1)S(1)} %get-tuple-element.23), channel_id=1, source_target_pairs={{0,1},{1,0},{2,3},{3,2},{4,5},{5,4},{6,7},{7,6},{8,9},{9,8},{10,11... | collective-permute-start | bytes 774152 | tf_op jit(solution)/shard_map/ppermute | solution.py:570
  4.8 1.4 %collective-permute-start.1 = (bf16[7,144,128]{2,1,0:T(8,128)(2,1)S(1)}, bf16[7,144,128]{2,1,0:T(8,128)(2,1)S(1)}, u32[]{:S(2)}, u32[]{:S(2)}) collective-permute-start(bf16[7,144,128]{2,1,0:T(8,128)(2,1)S(1)} %get-tuple-element.24), channel_id=1, source_target_pairs={{0,2},{1,3},{2,0},{3,1},{4,6},{5,7},{6,4},{7,5},{8,10},{9,11},{10,... | collective-permute-start | bytes 774152 | tf_op jit(solution)/shard_map/ppermute | solution.py:570
  6.2 0.3 collective-permute-start.2
  6.5 3.0 %collective-permute-start.3 = (bf16[7,144,128]{2,1,0:T(8,128)(2,1)S(1)}, bf16[7,144,128]{2,1,0:T(8,128)(2,1)S(1)}, u32[]{:S(2)}, u32[]{:S(2)}) collective-permute-start(bf16[7,144,128]{2,1,0:T(8,128)(2,1)S(1)} %get-tuple-element.26), channel_id=1, source_target_pairs={{0,4},{1,5},{2,6},{3,7},{4,0},{5,1},{6,2},{7,3},{8,12},{9,13},{10,... | collective-permute-start | bytes 774152 | tf_op jit(solution)/shard_map/ppermute | solution.py:570
  9.6 0.2 collective-permute-start.4
  9.8 0.0 collective-permute-done.refs_1_
  9.8 2.9 %collective-permute-start.5 = (bf16[7,144,128]{2,1,0:T(8,128)(2,1)S(1)}, bf16[7,144,128]{2,1,0:T(8,128)(2,1)S(1)}, u32[]{:S(2)}, u32[]{:S(2)}) collective-permute-start(bf16[7,144,128]{2,1,0:T(8,128)(2,1)S(1)} %get-tuple-element.28), channel_id=1, source_target_pairs={{0,6},{1,7},{2,4},{3,5},{4,2},{5,3},{6,0},{7,1},{8,14},{9,15},{10,... | collective-permute-start | bytes 774152 | tf_op jit(solution)/shard_map/ppermute | solution.py:570
  12.7 0.0 collective-permute-done.1.refs_2_
  12.7 4.1 %collective-permute-start.6 = (bf16[7,144,128]{2,1,0:T(8,128)(2,1)S(1)}, bf16[7,144,128]{2,1,0:T(8,128)(2,1)S(1)}, u32[]{:S(2)}, u32[]{:S(2)}) collective-permute-start(bf16[7,144,128]{2,1,0:T(8,128)(2,1)S(1)} %get-tuple-element.29), channel_id=1, source_target_pairs={{0,7},{1,6},{2,5},{3,4},{4,3},{5,2},{6,1},{7,0},{8,15},{9,14},{10,... | collective-permute-start | bytes 774152 | tf_op jit(solution)/shard_map/ppermute | solution.py:570
  16.7 2.4 %collective-permute-done.2.refs_3_ = bf16[7,144,128]{2,1,0:T(8,128)(2,1)S(1)} collective-permute-done((bf16[7,144,128]{2,1,0:T(8,128)(2,1)S(1)}, bf16[7,144,128]{2,1,0:T(8,128)(2,1)S(1)}, u32[]{:S(2)}, u32[]{:S(2)}) %collective-permute-start.2) | collective-permute-done | bytes 258080 | tf_op jit(solution)/shard_map/ppermute | solution.py:570
  19.1 7.0 %collective-permute-done.3.refs_4_ = bf16[7,144,128]{2,1,0:T(8,128)(2,1)S(1)} collective-permute-done((bf16[7,144,128]{2,1,0:T(8,128)(2,1)S(1)}, bf16[7,144,128]{2,1,0:T(8,128)(2,1)S(1)}, u32[]{:S(2)}, u32[]{:S(2)}) %collective-permute-start.3) | collective-permute-done | bytes 258080 | tf_op jit(solution)/shard_map/ppermute | solution.py:570
  26.2 5.8 %collective-permute-done.4.refs_5_ = bf16[7,144,128]{2,1,0:T(8,128)(2,1)S(1)} collective-permute-done((bf16[7,144,128]{2,1,0:T(8,128)(2,1)S(1)}, bf16[7,144,128]{2,1,0:T(8,128)(2,1)S(1)}, u32[]{:S(2)}, u32[]{:S(2)}) %collective-permute-start.4) | collective-permute-done | bytes 258080 | tf_op jit(solution)/shard_map/ppermute | solution.py:570
  32.0 0.0 collective-permute-done.5.refs_6_
  32.0 3.7 %collective-permute-done.6.refs_7_ = bf16[7,144,128]{2,1,0:T(8,128)(2,1)S(1)} collective-permute-done((bf16[7,144,128]{2,1,0:T(8,128)(2,1)S(1)}, bf16[7,144,128]{2,1,0:T(8,128)(2,1)S(1)}, u32[]{:S(2)}, u32[]{:S(2)}) %collective-permute-start.6) | collective-permute-done | bytes 258080 | tf_op jit(solution)/shard_map/ppermute | solution.py:570
  35.7 0.9 shard_map.107
  36.6 0.0 copy-start.9
  36.6 2.1 %collective-permute-start.7 = (bf16[8,2,144,128]{3,2,1,0:T(8,128)(2,1)}, bf16[8,2,144,128]{3,2,1,0:T(8,128)(2,1)}, u32[]{:S(2)}, u32[]{:S(2)}) collective-permute-start(bf16[8,2,144,128]{3,2,1,0:T(8,128)(2,1)} %get-tuple-element.30), channel_id=1, source_target_pairs={{0,1},{1,2},{2,3},{3,4},{4,5},{5,6},{6,7},{7,8},{8,9},{9,10},{10,1... | collective-permute-start | bytes 1769480 | tf_op jit(solution)/shard_map/ppermute | solution.py:613
  38.7 3.2 %collective-permute-start.8 = (bf16[8,2,144,128]{3,2,1,0:T(8,128)(2,1)S(1)}, bf16[8,2,144,128]{3,2,1,0:T(8,128)(2,1)}, u32[]{:S(2)}, u32[]{:S(2)}) collective-permute-start(bf16[8,2,144,128]{3,2,1,0:T(8,128)(2,1)S(1)} %get-tuple-element.31), channel_id=1, source_target_pairs={{1,0},{2,1},{3,2},{4,3},{5,4},{6,5},{7,6},{8,7},{9,8},{10,9},{11,1... | collective-permute-start | bytes 1769480 | tf_op jit(solution)/shard_map/ppermute | solution.py:614
  41.9 0.0 copy-done.1
  41.9 0.0 copy-done.5
  41.9 0.0 copy-done.6
  41.9 1.8 %shard_map.104 = f32[128,128]{1,0:T(8,128)} custom-call(s32[4]{0:T(128)S(1)} %pad_add_fusion.ids_ref, f32[2,384,128]{2,1,0:T(8,128)S(1)} %copy-done.1, s32[2,384]{1,0:T(2,128)S(1)} %copy-done.5, f32[2,144]{1,0:T(2,128)S(1)} %copy-done.6), custom_call_target="tpu_custom_call" | custom-call | flops 4000000 | bytes 500000 | tf_op jit(solution)/shard_map/pallas_call | solution.py:49
  43.7 10.3 %all-to-all-start = ((f32[128,1,128]{2,1,0:T(1,128)}), f32[128,1,128]{2,1,0:T(1,128)S(1)}, u32[]{:S(2)}, u32[]{:S(2)}) async-start(f32[128,1,128]{2,1,0:T(1,128)} %bitcast.5), calls=%async_computation | async-start | bytes 131072 | tf_op jit(solution)/shard_map/all_to_all | solution.py:582
  54.0 0.0 copy-done.7
  54.1 2.6 %shard_map.108 = (bf16[1024,128]{1,0:T(8,128)(2,1)}, f32[16,256]{1,0:T(8,128)S(1)}, bf16[32,1152]{1,0:T(8,128)(2,1)S(1)}) custom-call(s32[4]{0:T(128)S(1)} %pad_add_fusion.ids_ref, s32[1,128]{1,0:T(1,128)S(1)} %bitcast.17, bf16[7,144,128]{2,1,0:T(8,128)(2,1)S(1)} %get-tuple-element.22.refs_0_, bf16[7,144,128]{2,1,0:T(8,128)(2,1)S(1)} %collective-permute-done.refs_1_, ...), custom_call_target="tpu_custom_call" | custom-call | flops 300000000 | bytes 2500000 | tf_op jit(solution)/shard_map/pallas_call | solution.py:49
  56.7 7.0 %all-to-all-done = f32[128,1,128]{2,1,0:T(1,128)S(1)} async-done(((f32[128,1,128]{2,1,0:T(1,128)}), f32[128,1,128]{2,1,0:T(1,128)S(1)}, u32[]{:S(2)}, u32[]{:S(2)}) %all-to-all-start) | async-done | bytes 65568 | tf_op jit(solution)/shard_map/all_to_all | solution.py:582
  63.7 4.4 %all-to-all-start.1 = ((bf16[128,8,128]{2,1,0:T(8,128)(2,1)}), bf16[128,8,128]{2,1,0:T(8,128)(2,1)S(1)}, u32[]{:S(2)}, u32[]{:S(2)}) async-start(bf16[128,8,128]{2,1,0:T(8,128)(2,1)} %bitcast.11), calls=%async_computation.1 | async-start | bytes 524288 | tf_op jit(solution)/shard_map/all_to_all | solution.py:630
  68.1 0.0 copy-start.4
  68.1 0.0 copy-done.9
  68.1 0.0 copy-start.8
  68.1 0.9 copy-done.8
  69.0 2.2 %shard_map.105 = (f32[32,256]{1,0:T(8,128)S(1)}, f32[2,1152,128]{2,1,0:T(8,128)S(1)}, f32[4608,128]{1,0:T(8,128)S(1)}, s32[108,128]{1,0:T(8,128)S(1)}) custom-call(f32[128,128]{1,0:T(8,128)S(1)} %bitcast.15, s32[1,128]{1,0:T(1,128)S(1)} %bitcast.18, f32[36,128]{1,0:T(8,128)S(1)} %bitcast.19, s32[3,4608]{1,0:T(4,128)S(1)} %copy-done.8), custom_call_target="tpu_custom_call" | custom-call | flops 600000000 | bytes 1300000 | tf_op jit(solution)/shard_map/pallas_call | solution.py:49
  71.2 0.0 copy-start
  71.2 1.4 %copy-done = f32[4608,128]{1,0:T(8,128)} copy-done((f32[4608,128]{1,0:T(8,128)}, f32[4608,128]{1,0:T(8,128)S(1)}, u32[]{:S(2)}) %copy-start) | copy-done | bytes 2359320
  72.6 0.0 copy-start.2
  72.6 1.0 %copy-done.2 = f32[2,1152,128]{2,1,0:T(8,128)} copy-done((f32[2,1152,128]{2,1,0:T(8,128)}, f32[2,1152,128]{2,1,0:T(8,128)S(1)}, u32[]{:S(2)}) %copy-start.2) | copy-done | bytes 1179672
  73.6 0.0 copy-start.3
  73.6 0.6 copy-done.3
  74.3 4.9 %all-to-all-done.1 = bf16[128,8,128]{2,1,0:T(8,128)(2,1)S(1)} async-done(((bf16[128,8,128]{2,1,0:T(8,128)(2,1)}), bf16[128,8,128]{2,1,0:T(8,128)(2,1)S(1)}, u32[]{:S(2)}, u32[]{:S(2)}) %all-to-all-start.1) | async-done | bytes 262176 | tf_op jit(solution)/shard_map/all_to_all | solution.py:630
  79.2 1.4 %shard_map.110 = f32[2,384,128]{2,1,0:T(8,128)} custom-call(f32[2,384,128]{2,1,0:T(8,128)S(1)} %copy-done.1, bf16[1024,128]{1,0:T(8,128)(2,1)S(1)} %bitcast.14, s32[2,384]{1,0:T(2,128)S(1)} %copy-done.5), custom_call_target="tpu_custom_call" | custom-call | flops 4000000 | bytes 1500000 | tf_op jit(solution)/shard_map/pallas_call | solution.py:49
  80.5 0.0 collective-permute-done.7.below_hbm
  80.6 0.0 collective-permute-done.8.above_hbm
  80.6 0.0 copy-done.4
  80.6 19.2 %shard_map.109 = bf16[3,1152,256]{2,1,0:T(8,128)(2,1)} custom-call(s32[4]{0:T(128)S(1)} %pad_add_fusion.ids_ref, s32[13824]{0:T(1024)} %bitcast.16, f32[4608,128]{1,0:T(8,128)} %copy-done, f32[2,1152,128]{2,1,0:T(8,128)} %copy-done.2, bf16[8,2,144,128]{3,2,1,0:T(8,128)(2,1)} %collective-permute-done.7.below_hbm, ...), custom_call_target="tpu_custom_call" | custom-call | flops 40000000 | bytes 8000000 | tf_op jit(solution)/shard_map/pallas_call | solution.py:49
Async XLA Ops:
  0.7 41.2 %copy-start.1 = (f32[2,384,128]{2,1,0:T(8,128)S(1)}, f32[2,384,128]{2,1,0:T(8,128)}, u32[]{:S(2)}) copy-start(f32[2,384,128]{2,1,0:T(8,128)} %currents_ref.3) | copy-start | bytes 1179652
  0.7 41.2 %copy-start.5 = (s32[2,384]{1,0:T(2,128)S(1)}, s32[2,384]{1,0:T(2,128)}, u32[]{:S(2)}) copy-start(s32[2,384]{1,0:T(2,128)} %wet_ref.5) | copy-start | bytes 9220
  0.7 41.2 %copy-start.6 = (f32[2,144]{1,0:T(2,128)S(1)}, f32[2,144]{1,0:T(2,128)}, u32[]{:S(2)}) copy-start(f32[2,144]{1,0:T(2,128)} %speed_ref.1) | copy-start | bytes 3460
  3.3 50.7 %copy-start.7 = (s32[128]{0:T(128)S(1)}, s32[128]{0:T(128)}, u32[]{:S(2)}) copy-start(s32[128]{0:T(128)} %param.15) | copy-start | bytes 1540
  3.3 6.5 %collective-permute-start = (bf16[7,144,128]{2,1,0:T(8,128)(2,1)S(1)}, bf16[7,144,128]{2,1,0:T(8,128)(2,1)S(1)}, u32[]{:S(2)}, u32[]{:S(2)}) collective-permute-start(bf16[7,144,128]{2,1,0:T(8,128)(2,1)S(1)} %get-tuple-element.23), channel_id=1, source_target_pairs={{0,1},{1,0},{2,3},{3,2},{4,5},{5,4},{6,7},{7,6},{8,9},{9,8},{10,11... | collective-permute-start | bytes 774152 | tf_op jit(solution)/shard_map/ppermute | solution.py:570
  4.8 7.9 %collective-permute-start.1 = (bf16[7,144,128]{2,1,0:T(8,128)(2,1)S(1)}, bf16[7,144,128]{2,1,0:T(8,128)(2,1)S(1)}, u32[]{:S(2)}, u32[]{:S(2)}) collective-permute-start(bf16[7,144,128]{2,1,0:T(8,128)(2,1)S(1)} %get-tuple-element.24), channel_id=1, source_target_pairs={{0,2},{1,3},{2,0},{3,1},{4,6},{5,7},{6,4},{7,5},{8,10},{9,11},{10,... | collective-permute-start | bytes 774152 | tf_op jit(solution)/shard_map/ppermute | solution.py:570
  6.2 12.9 %collective-permute-start.2 = (bf16[7,144,128]{2,1,0:T(8,128)(2,1)S(1)}, bf16[7,144,128]{2,1,0:T(8,128)(2,1)S(1)}, u32[]{:S(2)}, u32[]{:S(2)}) collective-permute-start(bf16[7,144,128]{2,1,0:T(8,128)(2,1)S(1)} %get-tuple-element.25), channel_id=1, source_target_pairs={{0,3},{1,2},{2,1},{3,0},{4,7},{5,6},{6,5},{7,4},{8,11},{9,10},{10,... | collective-permute-start | bytes 774152 | tf_op jit(solution)/shard_map/ppermute | solution.py:570
  6.5 19.6 %collective-permute-start.3 = (bf16[7,144,128]{2,1,0:T(8,128)(2,1)S(1)}, bf16[7,144,128]{2,1,0:T(8,128)(2,1)S(1)}, u32[]{:S(2)}, u32[]{:S(2)}) collective-permute-start(bf16[7,144,128]{2,1,0:T(8,128)(2,1)S(1)} %get-tuple-element.26), channel_id=1, source_target_pairs={{0,4},{1,5},{2,6},{3,7},{4,0},{5,1},{6,2},{7,3},{8,12},{9,13},{10,... | collective-permute-start | bytes 774152 | tf_op jit(solution)/shard_map/ppermute | solution.py:570
  9.6 22.5 %collective-permute-start.4 = (bf16[7,144,128]{2,1,0:T(8,128)(2,1)S(1)}, bf16[7,144,128]{2,1,0:T(8,128)(2,1)S(1)}, u32[]{:S(2)}, u32[]{:S(2)}) collective-permute-start(bf16[7,144,128]{2,1,0:T(8,128)(2,1)S(1)} %get-tuple-element.27), channel_id=1, source_target_pairs={{0,5},{1,4},{2,7},{3,6},{4,1},{5,0},{6,3},{7,2},{8,13},{9,12},{10,... | collective-permute-start | bytes 774152 | tf_op jit(solution)/shard_map/ppermute | solution.py:570
  9.8 22.2 %collective-permute-start.5 = (bf16[7,144,128]{2,1,0:T(8,128)(2,1)S(1)}, bf16[7,144,128]{2,1,0:T(8,128)(2,1)S(1)}, u32[]{:S(2)}, u32[]{:S(2)}) collective-permute-start(bf16[7,144,128]{2,1,0:T(8,128)(2,1)S(1)} %get-tuple-element.28), channel_id=1, source_target_pairs={{0,6},{1,7},{2,4},{3,5},{4,2},{5,3},{6,0},{7,1},{8,14},{9,15},{10,... | collective-permute-start | bytes 774152 | tf_op jit(solution)/shard_map/ppermute | solution.py:570
  12.7 23.1 %collective-permute-start.6 = (bf16[7,144,128]{2,1,0:T(8,128)(2,1)S(1)}, bf16[7,144,128]{2,1,0:T(8,128)(2,1)S(1)}, u32[]{:S(2)}, u32[]{:S(2)}) collective-permute-start(bf16[7,144,128]{2,1,0:T(8,128)(2,1)S(1)} %get-tuple-element.29), channel_id=1, source_target_pairs={{0,7},{1,6},{2,5},{3,4},{4,3},{5,2},{6,1},{7,0},{8,15},{9,14},{10,... | collective-permute-start | bytes 774152 | tf_op jit(solution)/shard_map/ppermute | solution.py:570
  36.6 31.5 %copy-start.9 = (f32[4608]{0:T(1024)S(1)}, f32[4608]{0:T(1024)}, u32[]{:S(2)}) copy-start(f32[4608]{0:T(1024)} %param.13) | copy-start | bytes 55300
  36.6 43.9 %collective-permute-start.7 = (bf16[8,2,144,128]{3,2,1,0:T(8,128)(2,1)}, bf16[8,2,144,128]{3,2,1,0:T(8,128)(2,1)}, u32[]{:S(2)}, u32[]{:S(2)}) collective-permute-start(bf16[8,2,144,128]{3,2,1,0:T(8,128)(2,1)} %get-tuple-element.30), channel_id=1, source_target_pairs={{0,1},{1,2},{2,3},{3,4},{4,5},{5,6},{6,7},{7,8},{8,9},{9,10},{10,1... | collective-permute-start | bytes 1769480 | tf_op jit(solution)/shard_map/ppermute | solution.py:613
  38.7 41.8 %collective-permute-start.8 = (bf16[8,2,144,128]{3,2,1,0:T(8,128)(2,1)S(1)}, bf16[8,2,144,128]{3,2,1,0:T(8,128)(2,1)}, u32[]{:S(2)}, u32[]{:S(2)}) collective-permute-start(bf16[8,2,144,128]{3,2,1,0:T(8,128)(2,1)S(1)} %get-tuple-element.31), channel_id=1, source_target_pairs={{1,0},{2,1},{3,2},{4,3},{5,4},{6,5},{7,6},{8,7},{9,8},{10,9},{11,1... | collective-permute-start | bytes 1769480 | tf_op jit(solution)/shard_map/ppermute | solution.py:614
  43.7 19.9 %all-to-all-start = ((f32[128,1,128]{2,1,0:T(1,128)}), f32[128,1,128]{2,1,0:T(1,128)S(1)}, u32[]{:S(2)}, u32[]{:S(2)}) async-start(f32[128,1,128]{2,1,0:T(1,128)} %bitcast.5), calls=%async_computation | async-start | bytes 131072 | tf_op jit(solution)/shard_map/all_to_all | solution.py:582
  63.7 15.5 %all-to-all-start.1 = ((bf16[128,8,128]{2,1,0:T(8,128)(2,1)}), bf16[128,8,128]{2,1,0:T(8,128)(2,1)S(1)}, u32[]{:S(2)}, u32[]{:S(2)}) async-start(bf16[128,8,128]{2,1,0:T(8,128)(2,1)} %bitcast.11), calls=%async_computation.1 | async-start | bytes 524288 | tf_op jit(solution)/shard_map/all_to_all | solution.py:630
  68.1 12.5 %copy-start.4 = (s32[24,256]{1,0:T(8,128)S(1)}, s32[24,256]{1,0:T(8,128)}, u32[]{:S(2)}) copy-start(s32[24,256]{1,0:T(8,128)} %wet_ref.4) | copy-start | bytes 73732
  68.1 0.9 copy-start.8
  71.2 1.4 %copy-start = (f32[4608,128]{1,0:T(8,128)}, f32[4608,128]{1,0:T(8,128)S(1)}, u32[]{:S(2)}) copy-start(f32[4608,128]{1,0:T(8,128)S(1)} %get-tuple-element.20.coef_hbm) | copy-start | bytes 7077892
  72.6 1.0 %copy-start.2 = (f32[2,1152,128]{2,1,0:T(8,128)}, f32[2,1152,128]{2,1,0:T(8,128)S(1)}, u32[]{:S(2)}) copy-start(f32[2,1152,128]{2,1,0:T(8,128)S(1)} %get-tuple-element.21.speeds_hbm) | copy-start | bytes 3538948
  73.6 0.6 copy-start.3

commit v5 on v4

--- a/solution.py
+++ b/solution.py
@@ -37,6 +37,10 @@
     return pl.BlockSpec(memory_space=SMEM)
 
 
+def anywhere():
+    return pl.BlockSpec(memory_space=pl.ANY)
+
+
 def in_hbm():
     return pl.BlockSpec(memory_space=pltpu.HBM)
 
@@ -60,10 +64,10 @@
 def pack_kernel(order, ids_ref, spectrum_hbm, stokes_hbm, *refs):
     count = len(order)
     out_refs = refs[:count]
-    narrow_ref, wide_ref, in_sems, stokes_sems = refs[count:]
+    narrow_ref, wide_ref, stokes_ref, piece_ref, in_sems, out_sems = refs[count:]
     local_bins, tile_rows, _ = spectrum_hbm.shape
     rows = tile_rows // count
-    chunks = in_sems.shape[0]
+    chunks = in_sems.shape[0] - 1
     part = local_bins // chunks
     loads = []
     for chunk in range(chunks):
@@ -71,17 +75,15 @@
         loads.append(
             pltpu.make_async_copy(spectrum_hbm.at[span], narrow_ref.at[span], in_sems.at[chunk])
         )
-        loads[-1].start()
-    stokes = [
-        pltpu.make_async_copy(stokes_hbm, out_refs[turn].at[6], stokes_sems.at[turn])
-        for turn in range(count)
-    ]
-    for copy in stokes:
+    loads.append(pltpu.make_async_copy(stokes_hbm, stokes_ref, in_sems.at[chunks]))
+    for copy in loads:
         copy.start()
     own = ids_ref[0]
+    stores = []
     for chunk in range(chunks):
         loads[chunk].wait()
         first = chunk * part
+        span = pl.ds(first, part)
         for half in range(2):
             lanes = slice(half * LANES, (half + 1) * LANES)
             value = narrow_ref[first : first + part, :, lanes].astype(jnp.float32)
@@ -90,13 +92,31 @@
             )
         for turn in order:
             base = (own ^ turn) * rows + first * tile_rows
+            ref = piece_ref.at[turn - 1] if turn else out_refs[0]
             for row in range(rows):
                 for half in range(2):
                     value = wide_ref[half, pl.ds(base + row, part, stride=tile_rows), :]
-                    out_refs[turn][2 * row + half, first : first + part, :] = value.astype(
-                        jnp.bfloat16
+                    ref[2 * row + half, first : first + part, :] = value.astype(jnp.bfloat16)
+            if turn:
+                stores.append(
+                    pltpu.make_async_copy(
+                        piece_ref.at[turn - 1, pl.ds(0, 6), span],
+                        out_refs[turn].at[pl.ds(0, 6), span],
+                        out_sems.at[turn, chunk],
                     )
-    for copy in stokes:
+                )
+                stores[-1].start()
+        if chunk == 0:
+            loads[chunks].wait()
+            out_refs[0][6] = stokes_ref[...]
+            for turn in range(1, count):
+                stores.append(
+                    pltpu.make_async_copy(
+                        stokes_ref, out_refs[turn].at[6], out_sems.at[turn, chunks]
+                    )
+                )
+                stores[-1].start()
+    for copy in stores:
         copy.wait()
 
 
@@ -104,11 +124,12 @@
     return jnp.concatenate([ref[chunk] for ref in refs], axis=0)
 
 
-def edges_kernel(*refs):
-    last_ref, first_ref = refs[-2:]
+def edges_kernel(ids_ref, *refs):
+    inner_ref, outer_ref = refs[-2:]
+    core = ids_ref[0] & 1
     for turn, ref in enumerate(refs[:-2]):
-        last_ref[turn] = ref[4:6]
-        first_ref[turn] = ref[0:2]
+        inner_ref[turn] = ref[pl.ds(4 - 4 * core, 2)]
+        outer_ref[turn] = ref[pl.ds(4 * core, 2)]
 
 
 def wet_columns(wet_ref):
@@ -168,17 +189,35 @@
 
 
 def tables_kernel(
-    recv_ref, map_ref, coef_ref, pair_ref, surface_ref, speeds_ref, coefs_ref, rows_ref
+    recv_ref,
+    map_ref,
+    coef_ref,
+    pair_ref,
+    surface_ref,
+    speeds_hbm,
+    coefs_hbm,
+    rows_ref,
+    speeds_ref,
+    coefs_ref,
+    sems,
 ):
-    for block in range(coef_ref.shape[0]):
+    blocks = coef_ref.shape[0]
+    copies = []
+    for block in range(blocks):
         lanes = slice(block * LANES, (block + 1) * LANES)
         for side in range(3):
-            at = side * coef_ref.shape[0] + block
+            at = side * blocks + block
             rows_ref[at : at + 1, :] = pair_ref[side : side + 1, lanes] * 8
         row = DT_SOURCE * coef_ref[block : block + 1, :]
-        coefs_ref[block * LANES : (block + 1) * LANES, :] = jnp.broadcast_to(
-            row, (LANES, LANES)
-        ).T
+        coefs_ref[lanes, :] = jnp.broadcast_to(row, (LANES, LANES)).T
+        if (block + 1) % (blocks // 4) == 0:
+            span = pl.ds((block + 1 - blocks // 4) * LANES, blocks // 4 * LANES)
+            copies.append(
+                pltpu.make_async_copy(
+                    coefs_ref.at[span], coefs_hbm.at[span], sems.at[len(copies)]
+                )
+            )
+            copies[-1].start()
     recv = recv_ref[...]
     turned = recv.T
     column = columns_of(map_ref)
@@ -204,11 +243,19 @@
         speeds_ref[part] = jnp.dot(
             value, ones, precision=HIGHEST, preferred_element_type=jnp.float32
         )
+        copies.append(
+            pltpu.make_async_copy(
+                speeds_ref.at[part], speeds_hbm.at[part], sems.at[len(copies)]
+            )
+        )
+        copies[-1].start()
+    for copy in copies:
+        copy.wait()
 
 
 def drift_kernel(count, ids_ref, map_ref, *refs):
     piece_refs = refs[:count]
-    routed_ref, near_ref, weights_ref, rows_ref, stokes_ref = refs[count:]
+    routed_hbm, near_ref, weights_ref, rows_ref, stokes_ref, routed_ref, sems = refs[count:]
     own = ids_ref[0]
     for turn, ref in enumerate(piece_refs):
         stokes_ref[own ^ turn] = ref[6]
@@ -238,7 +285,18 @@
                 )
         for slot in range(2):
             rows_ref[pl.ds(slot * 3 + row, LANES, stride=8), :] = parts[slot]
-    routed_ref[...] = rows_ref[...].astype(jnp.bfloat16)
+    parts = sems.shape[0]
+    size = rows_ref.shape[0] // parts
+    copies = []
+    for part in range(parts):
+        span = pl.ds(part * size, size)
+        routed_ref[span, :] = rows_ref[span, :].astype(jnp.bfloat16)
+        copies.append(
+            pltpu.make_async_copy(routed_ref.at[span], routed_hbm.at[span], sems.at[part])
+        )
+        copies[-1].start()
+    for copy in copies:
+        copy.wait()
 
 
 def wave_kernel(
@@ -247,8 +305,8 @@
     pair_hbm,
     coef_hbm,
     speeds_hbm,
-    below_hbm,
-    above_hbm,
+    inner_hbm,
+    outer_hbm,
     surface_ref,
     near_ref,
     weights_ref,
@@ -261,8 +319,7 @@
         pair_ref,
         coef_ref,
         speeds_ref,
-        below_ref,
-        above_ref,
+        halo_ref,
         out_ref,
         field_ref,
         cur_ref,
@@ -276,9 +333,10 @@
     bins = count * local_bins
     pairs = coef_ref.shape[0]
 
+    core = ids_ref[0] & 1
     moves = (
-        (below_hbm, below_ref),
-        (above_hbm, above_ref),
+        (inner_hbm, halo_ref.at[1 - core]),
+        (outer_hbm, halo_ref.at[core]),
         (speeds_hbm, speeds_ref),
         (pair_hbm, pair_ref),
         (coef_hbm, coef_ref),
@@ -310,9 +368,9 @@
     loads[0].wait()
     loads[1].wait()
     weights = weights_ref[...]
-    for side, ref in enumerate((below_ref, above_ref)):
+    for side in range(2):
         for half in range(2):
-            blocks = [ref[ids_ref[1 + side] ^ block, half] for block in range(count)]
+            blocks = [halo_ref[side, ids_ref[1 + side] ^ block, half] for block in range(count)]
             cells = jnp.concatenate(blocks, axis=0)
             drift = jnp.dot(weights, cells, preferred_element_type=jnp.float32)
             lanes = slice(half * LANES, (half + 1) * LANES)
@@ -361,9 +419,9 @@
             for row in range(3)
         ]
         for half in range(2):
-            flux = [row_flux(below_ref[below_at, half, span, :].astype(jnp.float32), 0, half)]
+            flux = [row_flux(halo_ref[0, below_at, half, span, :].astype(jnp.float32), 0, half)]
             flux += [row_flux(energy[row][half], row + 1, half) for row in range(3)]
-            flux += [row_flux(above_ref[above_at, half, span, :].astype(jnp.float32), 4, half)]
+            flux += [row_flux(halo_ref[1, above_at, half, span, :].astype(jnp.float32), 4, half)]
             for row in range(3):
                 energy[row][half] = (
                     energy[row][half],
@@ -476,7 +534,7 @@
         out_ref[slot] = wet[:, slot : slot + 1] * (x + DT_OCEAN * (cross + MIXING * mixed))
 
 
-def wave_program(ids, pair_rows, coefs, speeds, below, above, surface, near, weights, wet, *pieces):
+def wave_program(ids, pair_rows, coefs, speeds, inner, outer, surface, near, weights, wet, *pieces):
     f32 = jnp.float32
     count = len(pieces)
     columns = wet.shape[1]
@@ -485,14 +543,13 @@
     return call(
         functools.partial(wave_kernel, count),
         jax.ShapeDtypeStruct((rows, bins, columns), jnp.bfloat16),
-        [in_smem()] + [in_hbm()] * 5 + [in_vmem()] * (4 + count),
+        [in_smem(), anywhere()] + [in_hbm()] * 4 + [in_vmem()] * (4 + count),
         in_hbm(),
         [
             SMEM(pair_rows.shape, jnp.int32),
             VMEM(coefs.shape, f32),
             VMEM(speeds.shape, f32),
-            VMEM(below.shape, jnp.bfloat16),
-            VMEM(above.shape, jnp.bfloat16),
+            VMEM((2, *inner.shape), jnp.bfloat16),
             VMEM((rows, bins, columns), jnp.bfloat16),
             VMEM((bins * 8, LANES), f32),
             VMEM((56, columns), f32),
@@ -506,7 +563,8 @@
         8_000_000,
         (
             ids,
-            *kept_in(pltpu.HBM, pair_rows, coefs, speeds, below, above),
+            pair_rows,
+            *kept_in(pltpu.HBM, coefs, speeds, inner, outer),
             surface,
             near,
             weights,
@@ -547,14 +605,17 @@
     piece_shape = (CHUNKS, local_bins, LANES)
     sent = call(
         functools.partial(pack_kernel, order),
-        [jax.ShapeDtypeStruct(piece_shape, bf16)] * bins_count,
+        [jax.ShapeDtypeStruct(piece_shape, bf16)]
+        + [pltpu.HBM(piece_shape, bf16)] * (bins_count - 1),
         [in_smem(), in_hbm(), in_hbm()],
-        [in_vmem()] * bins_count,
+        [in_vmem()] + [in_hbm()] * (bins_count - 1),
         [
             VMEM(spectrum.shape, bf16),
             VMEM((2, local_bins * tile_rows, LANES), f32),
-            pltpu.SemaphoreType.DMA((3,)),
-            pltpu.SemaphoreType.DMA((bins_count,)),
+            VMEM(stokes_kernel.shape, bf16),
+            VMEM((bins_count - 1, *piece_shape), bf16),
+            pltpu.SemaphoreType.DMA((4,)),
+            pltpu.SemaphoreType.DMA((bins_count, 4)),
         ],
         2_000_000,
         4_000_000,
@@ -585,44 +646,53 @@
         tables_kernel,
         (
             jax.ShapeDtypeStruct((32, columns), f32),
-            jax.ShapeDtypeStruct((2, bins, LANES), f32),
-            jax.ShapeDtypeStruct((pairs, LANES), f32),
+            pltpu.HBM((2, bins, LANES), f32),
+            pltpu.HBM((pairs, LANES), f32),
             jax.ShapeDtypeStruct((3 * pairs // LANES, LANES), jnp.int32),
         ),
         [in_vmem()] * 4,
-        (in_vmem(),) * 4,
-        [],
+        (in_vmem(), in_hbm(), in_hbm(), in_vmem()),
+        [
+            VMEM((2, bins, LANES), f32),
+            VMEM((pairs, LANES), f32),
+            pltpu.SemaphoreType.DMA((6,)),
+        ],
         600_000_000,
         1_300_000,
         (arrived.reshape(devices, LANES), map_row, pair_coef.reshape(-1, LANES), pair_bins),
     )
 
-    ahead = [(at, at + 1) for at in range(devices - 1)]
-    back = [(at + 1, at) for at in range(devices - 1)]
     halo_shape = (bins_count, 2, local_bins, LANES)
-    last_rows, first_rows = call(
+    inner, outer = call(
         edges_kernel,
         [jax.ShapeDtypeStruct(halo_shape, bf16)] * 2,
-        [in_vmem()] * bins_count,
+        [in_smem()] + [in_vmem()] * bins_count,
         [in_vmem()] * 2,
         [],
         1_000_000,
         2_400_000,
-        tuple(pieces),
-    )
-    below = lax.ppermute(last_rows, both, ahead)
-    above = lax.ppermute(first_rows, both, back)
+        (ids, *pieces),
+    )
+    outward = [(at, at + 1) for at in range(1, devices - 1, 2)]
+    outward += [(at + 1, at) for at, _ in outward]
+    outer = lax.ppermute(outer, both, outward)
+    inner = lax.ppermute(inner, both, [(at, at ^ 1) for at in range(devices)])
 
     routed, near, weights = call(
         functools.partial(drift_kernel, bins_count),
         (
-            jax.ShapeDtypeStruct((devices * 8, LANES), bf16),
+            pltpu.HBM((devices * 8, LANES), bf16),
             jax.ShapeDtypeStruct((16, columns), f32),
             jax.ShapeDtypeStruct((32, bins), bf16),
         ),
         [in_smem(), in_vmem()] + [in_vmem()] * bins_count,
-        (in_vmem(),) * 3,
-        [VMEM((devices * 8, LANES), f32), VMEM((bins_count, local_bins, LANES), bf16)],
+        (in_hbm(), in_vmem(), in_vmem()),
+        [
+            VMEM((devices * 8, LANES), f32),
+            VMEM((bins_count, local_bins, LANES), bf16),
+            VMEM((devices * 8, LANES), bf16),
+            pltpu.SemaphoreType.DMA((4,)),
+        ],
         300_000_000,
         2_500_000,
         (ids, map_row, *pieces),
@@ -637,8 +707,8 @@
         pair_rows.reshape(-1),
         coefs,
         speed_rows,
-        below,
-        above,
+        inner,
+        outer,
         surface_rows,
         near,
         weights,

time: 100 us -> 99.4 us (level)
  local copies, waits for them, and re-layouts: 3.99 us -> 0.03 us
  Pallas kernels: 30.6 us -> 33.4 us
  waiting for transfers between devices: 30.9 us -> 33.6 us
  starting transfers between devices: 33.4 us -> 31.3 us
    unnamed x20 -> x14, local copies, waits for them, and re-layouts: 3.99 us -> 0.03 us
    ppermute x2, starting transfers between devices: 5.25 us -> 2.32 us  [the longest x1 2.08 us: per_device(): outer = lax.ppermute(outer, both, outward)]
    pallas_call x7, Pallas kernels: 30.6 us -> 33.4 us  [call(): pl.pallas_call(body, out_shape=out_shape, in_specs=ins, out_specs=outs, s...]
    all_to_all x1, waiting for transfers between devices: 4.91 us -> 7.59 us  [per_device(): lax.all_to_all(routed.reshape(devices, 8, LANES), both, split_axis=0, con...]
  transfers between devices with their start and end apart: 11 -> 11, of which waited for: 6 -> 6; matrix products, arithmetic and copies ran while one was open for 0% -> 0% of each run, Pallas kernels for 8% -> 9%
where the time goes in v5:
time: 99.4 us; the launch traced here: 99.2 us
  waiting for transfers between devices  33.6 us (34%)
  Pallas kernels  33.4 us (34%)
  starting transfers between devices  31.3 us (31%)
    pallas_call x7, Pallas kernels, call(): pl.pallas_call(body, out_shape=out_shape, in_specs=ins, out_specs=outs, s...  33.4 us
    ppermute x7, waiting for transfers between devices, per_device(): pieces[turn] = lax.ppermute(sent[turn], 'bins', partners)  19 us
    ppermute x7, starting transfers between devices, per_device(): pieces[turn] = lax.ppermute(sent[turn], 'bins', partners)  13.6 us
    all_to_all x1, starting transfers between devices, per_device(): lax.all_to_all(surface, both, split_axis=0, concat_axis=0, tiled=True)  11 us
    all_to_all x1, waiting for transfers between devices, per_device(): lax.all_to_all(routed.reshape(devices, 8, LANES), both, split_axis=0, con...  7.59 us
    all_to_all x1, waiting for transfers between devices, per_device(): lax.all_to_all(surface, both, split_axis=0, concat_axis=0, tiled=True)  6.99 us
    all_to_all x1, starting transfers between devices, per_device(): lax.all_to_all(routed.reshape(devices, 8, LANES), both, split_axis=0, con...  4.4 us
    ppermute x1, starting transfers between devices, per_device(): outer = lax.ppermute(outer, both, outward)  2.08 us
  transfers between devices with their start and end apart: 11, of which 6 were waited for; matrix products, arithmetic and copies ran while one was open for 0% of the time, Pallas kernels for 9%

profile of v5, /device:TPU:1, one launch (start us, length us, event | category | flops | bytes accessed | tf_op | source)
XLA Modules:
  0.0 99.2 jit_solution(3332443486878834872)
XLA Ops:
  0.6 0.1 pad_add_fusion.ids_ref
  0.7 0.0 copy-start
  0.7 0.0 copy-start.2
  0.7 0.0 copy-start.3
  0.7 3.4 %shard_map.106 = (bf16[7,144,128]{2,1,0:T(8,128)(2,1)S(1)}, bf16[7,144,128]{2,1,0:T(8,128)(2,1)}, bf16[7,144,128]{2,1,0:T(8,128)(2,1)}, bf16[7,144,128]{2,1,0:T(...) custom-call(s32[4]{0:T(128)S(1)} %pad_add_fusion.ids_ref, ...), custom_call_target="tpu_custom_call" | custom-call | flops 2000000 | bytes 4000000 | tf_op jit(solution)/shard_map/pallas_call | solution.py:53
  4.1 0.0 copy-start.4
  4.1 1.5 %collective-permute-start = (bf16[7,144,128]{2,1,0:T(8,128)(2,1)}, bf16[7,144,128]{2,1,0:T(8,128)(2,1)S(1)}, u32[]{:S(2)}, u32[]{:S(2)}) collective-permute-start(bf16[7,144,128]{2,1,0:T(8,128)(2,1)} %get-tuple-element.23), channel_id=1, source_target_pairs={{0,1},{1,0},{2,3},{3,2},{4,5},{5,4},{6,7},{7,6},{8,9},{9,8},{10,11... | collective-permute-start | bytes 774152 | tf_op jit(solution)/shard_map/ppermute | solution.py:631
  5.6 1.4 %collective-permute-start.1 = (bf16[7,144,128]{2,1,0:T(8,128)(2,1)}, bf16[7,144,128]{2,1,0:T(8,128)(2,1)S(1)}, u32[]{:S(2)}, u32[]{:S(2)}) collective-permute-start(bf16[7,144,128]{2,1,0:T(8,128)(2,1)} %get-tuple-element.24), channel_id=1, source_target_pairs={{0,2},{1,3},{2,0},{3,1},{4,6},{5,7},{6,4},{7,5},{8,10},{9,11},{10,... | collective-permute-start | bytes 774152 | tf_op jit(solution)/shard_map/ppermute | solution.py:631
  7.0 0.3 collective-permute-start.2
  7.3 3.0 %collective-permute-start.3 = (bf16[7,144,128]{2,1,0:T(8,128)(2,1)}, bf16[7,144,128]{2,1,0:T(8,128)(2,1)S(1)}, u32[]{:S(2)}, u32[]{:S(2)}) collective-permute-start(bf16[7,144,128]{2,1,0:T(8,128)(2,1)} %get-tuple-element.26), channel_id=1, source_target_pairs={{0,4},{1,5},{2,6},{3,7},{4,0},{5,1},{6,2},{7,3},{8,12},{9,13},{10,... | collective-permute-start | bytes 774152 | tf_op jit(solution)/shard_map/ppermute | solution.py:631
  10.3 0.2 collective-permute-start.4
  10.6 0.0 collective-permute-done.refs_1_
  10.6 2.9 %collective-permute-start.5 = (bf16[7,144,128]{2,1,0:T(8,128)(2,1)}, bf16[7,144,128]{2,1,0:T(8,128)(2,1)S(1)}, u32[]{:S(2)}, u32[]{:S(2)}) collective-permute-start(bf16[7,144,128]{2,1,0:T(8,128)(2,1)} %get-tuple-element.28), channel_id=1, source_target_pairs={{0,6},{1,7},{2,4},{3,5},{4,2},{5,3},{6,0},{7,1},{8,14},{9,15},{10,... | collective-permute-start | bytes 774152 | tf_op jit(solution)/shard_map/ppermute | solution.py:631
  13.4 0.0 collective-permute-done.1.refs_2_
  13.4 4.2 %collective-permute-start.6 = (bf16[7,144,128]{2,1,0:T(8,128)(2,1)}, bf16[7,144,128]{2,1,0:T(8,128)(2,1)S(1)}, u32[]{:S(2)}, u32[]{:S(2)}) collective-permute-start(bf16[7,144,128]{2,1,0:T(8,128)(2,1)} %get-tuple-element.29), channel_id=1, source_target_pairs={{0,7},{1,6},{2,5},{3,4},{4,3},{5,2},{6,1},{7,0},{8,15},{9,14},{10,... | collective-permute-start | bytes 774152 | tf_op jit(solution)/shard_map/ppermute | solution.py:631
  17.7 2.4 %collective-permute-done.2.refs_3_ = bf16[7,144,128]{2,1,0:T(8,128)(2,1)S(1)} collective-permute-done((bf16[7,144,128]{2,1,0:T(8,128)(2,1)}, bf16[7,144,128]{2,1,0:T(8,128)(2,1)S(1)}, u32[]{:S(2)}, u32[]{:S(2)}) %collective-permute-start.2) | collective-permute-done | bytes 258080 | tf_op jit(solution)/shard_map/ppermute | solution.py:631
  20.1 7.0 %collective-permute-done.3.refs_4_ = bf16[7,144,128]{2,1,0:T(8,128)(2,1)S(1)} collective-permute-done((bf16[7,144,128]{2,1,0:T(8,128)(2,1)}, bf16[7,144,128]{2,1,0:T(8,128)(2,1)S(1)}, u32[]{:S(2)}, u32[]{:S(2)}) %collective-permute-start.3) | collective-permute-done | bytes 258080 | tf_op jit(solution)/shard_map/ppermute | solution.py:631
  27.1 5.8 %collective-permute-done.4.refs_5_ = bf16[7,144,128]{2,1,0:T(8,128)(2,1)S(1)} collective-permute-done((bf16[7,144,128]{2,1,0:T(8,128)(2,1)}, bf16[7,144,128]{2,1,0:T(8,128)(2,1)S(1)}, u32[]{:S(2)}, u32[]{:S(2)}) %collective-permute-start.4) | collective-permute-done | bytes 258080 | tf_op jit(solution)/shard_map/ppermute | solution.py:631
  33.0 0.0 collective-permute-done.5.refs_6_
  33.0 3.7 %collective-permute-done.6.refs_7_ = bf16[7,144,128]{2,1,0:T(8,128)(2,1)S(1)} collective-permute-done((bf16[7,144,128]{2,1,0:T(8,128)(2,1)}, bf16[7,144,128]{2,1,0:T(8,128)(2,1)S(1)}, u32[]{:S(2)}, u32[]{:S(2)}) %collective-permute-start.6) | collective-permute-done | bytes 258080 | tf_op jit(solution)/shard_map/ppermute | solution.py:631
  36.7 1.6 %shard_map.107 = (bf16[8,2,144,128]{3,2,1,0:T(8,128)(2,1)}, bf16[8,2,144,128]{3,2,1,0:T(8,128)(2,1)}) custom-call(s32[4]{0:T(128)S(1)} %pad_add_fusion.ids_ref, bf16[7,144,128]{2,1,0:T(8,128)(2,1)S(1)} %get-tuple-element.22.refs_0_, bf16[7,144,128]{2,1,0:T(8,128)(2,1)S(1)} %collective-permute-done.refs_1_, ...), custom_call_target="tpu_custom_call" | custom-call | flops 1000000 | bytes 2400000 | tf_op jit(solution)/shard_map/pallas_call | solution.py:53
  38.3 0.0 copy-start.5
  38.3 0.0 copy-start.6
  38.3 0.2 collective-permute-start.7
  38.6 2.1 %collective-permute-start.8 = (bf16[8,2,144,128]{3,2,1,0:T(8,128)(2,1)}, bf16[8,2,144,128]{3,2,1,0:T(8,128)(2,1)}, u32[]{:S(2)}, u32[]{:S(2)}) collective-permute-start(bf16[8,2,144,128]{3,2,1,0:T(8,128)(2,1)} %get-tuple-element.31), channel_id=1, source_target_pairs={{1,2},{3,4},{5,6},{7,8},{9,10},{11,12},{13,14},{15,16},{17,18},{19... | collective-permute-start | bytes 1769480 | tf_op jit(solution)/shard_map/ppermute | solution.py:678
  40.7 0.0 copy-done
  40.7 0.0 copy-done.2
  40.7 0.0 copy-done.3
  40.7 1.8 %shard_map.104 = f32[128,128]{1,0:T(8,128)} custom-call(s32[4]{0:T(128)S(1)} %pad_add_fusion.ids_ref, f32[2,384,128]{2,1,0:T(8,128)S(1)} %copy-done, s32[2,384]{1,0:T(2,128)S(1)} %copy-done.2, f32[2,144]{1,0:T(2,128)S(1)} %copy-done.3), custom_call_target="tpu_custom_call" | custom-call | flops 4000000 | bytes 500000 | tf_op jit(solution)/shard_map/pallas_call | solution.py:53
  42.5 11.0 %all-to-all-start = ((f32[128,1,128]{2,1,0:T(1,128)}), f32[128,1,128]{2,1,0:T(1,128)S(1)}, u32[]{:S(2)}, u32[]{:S(2)}) async-start(f32[128,1,128]{2,1,0:T(1,128)} %bitcast.5), calls=%async_computation | async-start | bytes 131072 | tf_op jit(solution)/shard_map/all_to_all | solution.py:643
  53.5 0.0 copy-done.4
  53.5 2.6 %shard_map.108 = (bf16[1024,128]{1,0:T(8,128)(2,1)}, f32[16,256]{1,0:T(8,128)S(1)}, bf16[32,1152]{1,0:T(8,128)(2,1)S(1)}) custom-call(s32[4]{0:T(128)S(1)} %pad_add_fusion.ids_ref, s32[1,128]{1,0:T(1,128)S(1)} %bitcast.17, bf16[7,144,128]{2,1,0:T(8,128)(2,1)S(1)} %get-tuple-element.22.refs_0_, bf16[7,144,128]{2,1,0:T(8,128)(2,1)S(1)} %collective-permute-done.refs_1_, ...), custom_call_target="tpu_custom_call" | custom-call | flops 300000000 | bytes 2500000 | tf_op jit(solution)/shard_map/pallas_call | solution.py:53
  56.1 7.0 %all-to-all-done = f32[128,1,128]{2,1,0:T(1,128)S(1)} async-done(((f32[128,1,128]{2,1,0:T(1,128)}), f32[128,1,128]{2,1,0:T(1,128)S(1)}, u32[]{:S(2)}, u32[]{:S(2)}) %all-to-all-start) | async-done | bytes 65568 | tf_op jit(solution)/shard_map/all_to_all | solution.py:643
  63.1 4.4 %all-to-all-start.1 = ((bf16[128,8,128]{2,1,0:T(8,128)(2,1)}), bf16[128,8,128]{2,1,0:T(8,128)(2,1)S(1)}, u32[]{:S(2)}, u32[]{:S(2)}) async-start(bf16[128,8,128]{2,1,0:T(8,128)(2,1)} %bitcast.21), calls=%async_computation.1 | async-start | bytes 524288 | tf_op jit(solution)/shard_map/all_to_all | solution.py:700
  67.5 0.0 copy-start.1
  67.5 0.0 copy-done.5
  67.5 0.0 copy-done.6
  67.6 3.5 %shard_map.105 = (f32[32,256]{1,0:T(8,128)S(1)}, f32[2,1152,128]{2,1,0:T(8,128)}, f32[4608,128]{1,0:T(8,128)}, s32[108,128]{1,0:T(8,128)S(1)}) custom-call(f32[128,128]{1,0:T(8,128)S(1)} %bitcast.15, s32[1,128]{1,0:T(1,128)S(1)} %bitcast.18, f32[36,128]{1,0:T(8,128)S(1)} %bitcast.19, s32[3,4608]{1,0:T(4,128)S(1)} %copy-done.5), custom_call_target="tpu_custom_call" | custom-call | flops 600000000 | bytes 1300000 | tf_op jit(solution)/shard_map/pallas_call | solution.py:53
  71.0 7.6 %all-to-all-done.1 = bf16[128,8,128]{2,1,0:T(8,128)(2,1)S(1)} async-done(((bf16[128,8,128]{2,1,0:T(8,128)(2,1)}), bf16[128,8,128]{2,1,0:T(8,128)(2,1)S(1)}, u32[]{:S(2)}, u32[]{:S(2)}) %all-to-all-start.1) | async-done | bytes 262176 | tf_op jit(solution)/shard_map/all_to_all | solution.py:700
  78.6 1.4 %shard_map.110 = f32[2,384,128]{2,1,0:T(8,128)} custom-call(f32[2,384,128]{2,1,0:T(8,128)S(1)} %copy-done, bf16[1024,128]{1,0:T(8,128)(2,1)S(1)} %bitcast.14, s32[2,384]{1,0:T(2,128)S(1)} %copy-done.2), custom_call_target="tpu_custom_call" | custom-call | flops 4000000 | bytes 1500000 | tf_op jit(solution)/shard_map/pallas_call | solution.py:53
  80.0 0.0 collective-permute-done.7.inner_hbm
  80.0 0.0 collective-permute-done.8.outer_hbm
  80.0 0.0 copy-done.1
  80.0 19.2 %shard_map.109 = bf16[3,1152,256]{2,1,0:T(8,128)(2,1)} custom-call(s32[4]{0:T(128)S(1)} %pad_add_fusion.ids_ref, s32[13824]{0:T(1024)S(1)} %bitcast.16, f32[4608,128]{1,0:T(8,128)} %get-tuple-element.20.coef_hbm, f32[2,1152,128]{2,1,0:T(8,128)} %get-tuple-element.21.speeds_hbm, bf16[8,2,144,128]{3,2,1,0:T(8,128)(2,1)} %collective-permute-done.7.inner_hbm, ...), custom_call_target="tpu_custom_call" | custom-call | flops 40000000 | bytes 8000000 | tf_op jit(solution)/shard_map/pallas_call | solution.py:53
Async XLA Ops:
  0.7 39.9 %copy-start = (f32[2,384,128]{2,1,0:T(8,128)S(1)}, f32[2,384,128]{2,1,0:T(8,128)}, u32[]{:S(2)}) copy-start(f32[2,384,128]{2,1,0:T(8,128)} %currents_ref.3) | copy-start | bytes 1179652
  0.7 39.9 %copy-start.2 = (s32[2,384]{1,0:T(2,128)S(1)}, s32[2,384]{1,0:T(2,128)}, u32[]{:S(2)}) copy-start(s32[2,384]{1,0:T(2,128)} %wet_ref.5) | copy-start | bytes 9220
  0.7 40.0 %copy-start.3 = (f32[2,144]{1,0:T(2,128)S(1)}, f32[2,144]{1,0:T(2,128)}, u32[]{:S(2)}) copy-start(f32[2,144]{1,0:T(2,128)} %speed_ref.1) | copy-start | bytes 3460
  4.1 49.4 %copy-start.4 = (s32[128]{0:T(128)S(1)}, s32[128]{0:T(128)}, u32[]{:S(2)}) copy-start(s32[128]{0:T(128)} %param.15) | copy-start | bytes 1540
  4.1 6.5 %collective-permute-start = (bf16[7,144,128]{2,1,0:T(8,128)(2,1)}, bf16[7,144,128]{2,1,0:T(8,128)(2,1)S(1)}, u32[]{:S(2)}, u32[]{:S(2)}) collective-permute-start(bf16[7,144,128]{2,1,0:T(8,128)(2,1)} %get-tuple-element.23), channel_id=1, source_target_pairs={{0,1},{1,0},{2,3},{3,2},{4,5},{5,4},{6,7},{7,6},{8,9},{9,8},{10,11... | collective-permute-start | bytes 774152 | tf_op jit(solution)/shard_map/ppermute | solution.py:631
  5.6 7.9 %collective-permute-start.1 = (bf16[7,144,128]{2,1,0:T(8,128)(2,1)}, bf16[7,144,128]{2,1,0:T(8,128)(2,1)S(1)}, u32[]{:S(2)}, u32[]{:S(2)}) collective-permute-start(bf16[7,144,128]{2,1,0:T(8,128)(2,1)} %get-tuple-element.24), channel_id=1, source_target_pairs={{0,2},{1,3},{2,0},{3,1},{4,6},{5,7},{6,4},{7,5},{8,10},{9,11},{10,... | collective-permute-start | bytes 774152 | tf_op jit(solution)/shard_map/ppermute | solution.py:631
  7.0 13.1 %collective-permute-start.2 = (bf16[7,144,128]{2,1,0:T(8,128)(2,1)}, bf16[7,144,128]{2,1,0:T(8,128)(2,1)S(1)}, u32[]{:S(2)}, u32[]{:S(2)}) collective-permute-start(bf16[7,144,128]{2,1,0:T(8,128)(2,1)} %get-tuple-element.25), channel_id=1, source_target_pairs={{0,3},{1,2},{2,1},{3,0},{4,7},{5,6},{6,5},{7,4},{8,11},{9,10},{10,... | collective-permute-start | bytes 774152 | tf_op jit(solution)/shard_map/ppermute | solution.py:631
  7.3 19.8 %collective-permute-start.3 = (bf16[7,144,128]{2,1,0:T(8,128)(2,1)}, bf16[7,144,128]{2,1,0:T(8,128)(2,1)S(1)}, u32[]{:S(2)}, u32[]{:S(2)}) collective-permute-start(bf16[7,144,128]{2,1,0:T(8,128)(2,1)} %get-tuple-element.26), channel_id=1, source_target_pairs={{0,4},{1,5},{2,6},{3,7},{4,0},{5,1},{6,2},{7,3},{8,12},{9,13},{10,... | collective-permute-start | bytes 774152 | tf_op jit(solution)/shard_map/ppermute | solution.py:631
  10.3 22.7 %collective-permute-start.4 = (bf16[7,144,128]{2,1,0:T(8,128)(2,1)}, bf16[7,144,128]{2,1,0:T(8,128)(2,1)S(1)}, u32[]{:S(2)}, u32[]{:S(2)}) collective-permute-start(bf16[7,144,128]{2,1,0:T(8,128)(2,1)} %get-tuple-element.27), channel_id=1, source_target_pairs={{0,5},{1,4},{2,7},{3,6},{4,1},{5,0},{6,3},{7,2},{8,13},{9,12},{10,... | collective-permute-start | bytes 774152 | tf_op jit(solution)/shard_map/ppermute | solution.py:631
  10.6 22.4 %collective-permute-start.5 = (bf16[7,144,128]{2,1,0:T(8,128)(2,1)}, bf16[7,144,128]{2,1,0:T(8,128)(2,1)S(1)}, u32[]{:S(2)}, u32[]{:S(2)}) collective-permute-start(bf16[7,144,128]{2,1,0:T(8,128)(2,1)} %get-tuple-element.28), channel_id=1, source_target_pairs={{0,6},{1,7},{2,4},{3,5},{4,2},{5,3},{6,0},{7,1},{8,14},{9,15},{10,... | collective-permute-start | bytes 774152 | tf_op jit(solution)/shard_map/ppermute | solution.py:631
  13.4 23.2 %collective-permute-start.6 = (bf16[7,144,128]{2,1,0:T(8,128)(2,1)}, bf16[7,144,128]{2,1,0:T(8,128)(2,1)S(1)}, u32[]{:S(2)}, u32[]{:S(2)}) collective-permute-start(bf16[7,144,128]{2,1,0:T(8,128)(2,1)} %get-tuple-element.29), channel_id=1, source_target_pairs={{0,7},{1,6},{2,5},{3,4},{4,3},{5,2},{6,1},{7,0},{8,15},{9,14},{10,... | collective-permute-start | bytes 774152 | tf_op jit(solution)/shard_map/ppermute | solution.py:631
  38.3 29.2 %copy-start.5 = (s32[3,4608]{1,0:T(4,128)S(1)}, s32[3,4608]{1,0:T(4,128)}, u32[]{:S(2)}) copy-start(s32[3,4608]{1,0:T(4,128)} %pair_ref.1) | copy-start | bytes 165892
  38.3 29.2 %copy-start.6 = (f32[4608]{0:T(1024)S(1)}, f32[4608]{0:T(1024)}, u32[]{:S(2)}) copy-start(f32[4608]{0:T(1024)} %param.13) | copy-start | bytes 55300
  38.3 41.7 %collective-permute-start.7 = (bf16[8,2,144,128]{3,2,1,0:T(8,128)(2,1)}, bf16[8,2,144,128]{3,2,1,0:T(8,128)(2,1)}, u32[]{:S(2)}, u32[]{:S(2)}) collective-permute-start(bf16[8,2,144,128]{3,2,1,0:T(8,128)(2,1)} %get-tuple-element.30), channel_id=1, source_target_pairs={{0,1},{1,0},{2,3},{3,2},{4,5},{5,4},{6,7},{7,6},{8,9},{9,8},{10,11... | collective-permute-start | bytes 1769480 | tf_op jit(solution)/shard_map/ppermute | solution.py:679
  38.6 41.4 %collective-permute-start.8 = (bf16[8,2,144,128]{3,2,1,0:T(8,128)(2,1)}, bf16[8,2,144,128]{3,2,1,0:T(8,128)(2,1)}, u32[]{:S(2)}, u32[]{:S(2)}) collective-permute-start(bf16[8,2,144,128]{3,2,1,0:T(8,128)(2,1)} %get-tuple-element.31), channel_id=1, source_target_pairs={{1,2},{3,4},{5,6},{7,8},{9,10},{11,12},{13,14},{15,16},{17,18},{19... | collective-permute-start | bytes 1769480 | tf_op jit(solution)/shard_map/ppermute | solution.py:678
  42.5 20.7 %all-to-all-start = ((f32[128,1,128]{2,1,0:T(1,128)}), f32[128,1,128]{2,1,0:T(1,128)S(1)}, u32[]{:S(2)}, u32[]{:S(2)}) async-start(f32[128,1,128]{2,1,0:T(1,128)} %bitcast.5), calls=%async_computation | async-start | bytes 131072 | tf_op jit(solution)/shard_map/all_to_all | solution.py:643
  63.1 15.5 %all-to-all-start.1 = ((bf16[128,8,128]{2,1,0:T(8,128)(2,1)}), bf16[128,8,128]{2,1,0:T(8,128)(2,1)S(1)}, u32[]{:S(2)}, u32[]{:S(2)}) async-start(bf16[128,8,128]{2,1,0:T(8,128)(2,1)} %bitcast.21), calls=%async_computation.1 | async-start | bytes 524288 | tf_op jit(solution)/shard_map/all_to_all | solution.py:700
  67.5 12.5 %copy-start.1 = (s32[24,256]{1,0:T(8,128)S(1)}, s32[24,256]{1,0:T(8,128)}, u32[]{:S(2)}) copy-start(s32[24,256]{1,0:T(8,128)} %wet_ref.4) | copy-start | bytes 73732

commit v6 on v5

--- a/solution.py
+++ b/solution.py
@@ -59,6 +59,10 @@
         compiler_params=pltpu.CompilerParams(vmem_limit_bytes=limit * 2**20),
         cost_estimate=pl.CostEstimate(flops=flops, bytes_accessed=moved, transcendentals=0),
     )(*args)
+
+
+def placed(device, row):
+    return row + (device & 1) * (2 - 2 * row)
 
 
 def pack_kernel(order, ids_ref, spectrum_hbm, stokes_hbm, *refs):
@@ -91,11 +95,14 @@
                 part * tile_rows, LANES
             )
         for turn in order:
-            base = (own ^ turn) * rows + first * tile_rows
+            target = own ^ turn
+            base = target * rows + first * tile_rows
             ref = piece_ref.at[turn - 1] if turn else out_refs[0]
             for row in range(rows):
                 for half in range(2):
-                    value = wide_ref[half, pl.ds(base + row, part, stride=tile_rows), :]
+                    value = wide_ref[
+                        half, pl.ds(base + placed(target, row), part, stride=tile_rows), :
+                    ]
                     ref[2 * row + half, first : first + part, :] = value.astype(jnp.bfloat16)
             if turn:
                 stores.append(
@@ -109,7 +116,7 @@
         if chunk == 0:
             loads[chunks].wait()
             out_refs[0][6] = stokes_ref[...]
-            for turn in range(1, count):
+            for turn in range(2, count, 2):
                 stores.append(
                     pltpu.make_async_copy(
                         stokes_ref, out_refs[turn].at[6], out_sems.at[turn, chunks]
@@ -124,12 +131,13 @@
     return jnp.concatenate([ref[chunk] for ref in refs], axis=0)
 
 
-def edges_kernel(ids_ref, *refs):
-    inner_ref, outer_ref = refs[-2:]
-    core = ids_ref[0] & 1
-    for turn, ref in enumerate(refs[:-2]):
-        inner_ref[turn] = ref[pl.ds(4 - 4 * core, 2)]
-        outer_ref[turn] = ref[pl.ds(4 * core, 2)]
+def edges_kernel(*refs):
+    inner_ref, outer_ref, stokes_ref = refs[-3:]
+    for turn, ref in enumerate(refs[:-3]):
+        outer_ref[turn] = ref[0:2]
+        inner_ref[turn] = ref[4:6]
+        if turn % 2 == 0:
+            stokes_ref[turn // 2] = ref[6]
 
 
 def wet_columns(wet_ref):
@@ -188,19 +196,15 @@
     return (2.0 * column + float(slot)) == index
 
 
-def tables_kernel(
-    recv_ref,
-    map_ref,
-    coef_ref,
-    pair_ref,
-    surface_ref,
-    speeds_hbm,
-    coefs_hbm,
-    rows_ref,
-    speeds_ref,
-    coefs_ref,
-    sems,
-):
+def thirds(value):
+    high = value.astype(jnp.bfloat16)
+    rest = value - high.astype(jnp.float32)
+    middle = rest.astype(jnp.bfloat16)
+    low = (rest - middle.astype(jnp.float32)).astype(jnp.bfloat16)
+    return [high, middle, low]
+
+
+def pairs_kernel(coef_ref, pair_ref, coefs_hbm, rows_ref, coefs_ref, sems):
     blocks = coef_ref.shape[0]
     copies = []
     for block in range(blocks):
@@ -218,51 +222,61 @@
                 )
             )
             copies[-1].start()
-    recv = recv_ref[...]
-    turned = recv.T
-    column = columns_of(map_ref)
-    parts = []
-    for slot in range(2):
-        pick = chosen(column, slot).astype(jnp.float32)
-        parts.append(jnp.dot(turned, pick, precision=HIGHEST, preferred_element_type=jnp.float32))
-    surface_ref[...] = jnp.zeros_like(surface_ref)
-    surface_ref[0:10, :] = parts[0][0:10] + parts[1][10:20]
-    surface_ref[16:26, :] = parts[0][64:74] + parts[1][74:84]
+    for copy in copies:
+        copy.wait()
+
+
+def tables_kernel(recv_ref, map_ref, surface_ref, speeds_hbm, speeds_ref, sems):
+    bf16 = jnp.bfloat16
+    parts = thirds(recv_ref[...])
+    copies = []
     bins = speeds_ref.shape[1]
     lane = lax.broadcasted_iota(jnp.int32, (bins, LANES), 1)
     index = lax.broadcasted_iota(jnp.int32, (bins, LANES), 0)
     first = ((lane & 7) * 16 + (lane >> 3)) * 9
-    own = (index >= first) & (index < first + 9)
-    rows = jnp.dot(
-        own.astype(jnp.float32), recv, precision=HIGHEST, preferred_element_type=jnp.float32
-    )
+    own = ((index >= first) & (index < first + 9)).astype(jnp.float32).astype(bf16)
+    rows = [jnp.dot(own, part, preferred_element_type=jnp.float32) for part in parts]
     place = index - ((index * 7282) >> 16) * 9
-    ones = jnp.ones((LANES, LANES), jnp.float32)
+    ones = jnp.ones((LANES, LANES), bf16)
     for part in range(2):
-        value = jnp.where(lane == place + (SPEED_LANE + 9 * part), rows, 0.0)
-        speeds_ref[part] = jnp.dot(
-            value, ones, precision=HIGHEST, preferred_element_type=jnp.float32
-        )
+        mine = lane == place + (SPEED_LANE + 9 * part)
+        total = jnp.zeros((bins, LANES), jnp.float32)
+        for value in rows:
+            kept = jnp.where(mine, value, 0.0).astype(bf16)
+            total = total + jnp.dot(kept, ones, preferred_element_type=jnp.float32)
+        speeds_ref[part] = total
         copies.append(
-            pltpu.make_async_copy(
-                speeds_ref.at[part], speeds_hbm.at[part], sems.at[len(copies)]
-            )
+            pltpu.make_async_copy(speeds_ref.at[part], speeds_hbm.at[part], sems.at[part])
         )
         copies[-1].start()
+    turned = thirds(recv_ref[...].T)
+    column = columns_of(map_ref)
+    found = []
+    for slot in range(2):
+        pick = chosen(column, slot).astype(jnp.float32).astype(bf16)
+        found.append(
+            sum(jnp.dot(part, pick, preferred_element_type=jnp.float32) for part in turned)
+        )
+    surface_ref[...] = jnp.zeros_like(surface_ref)
+    surface_ref[0:10, :] = found[0][0:10] + found[1][10:20]
+    surface_ref[16:26, :] = found[0][64:74] + found[1][74:84]
     for copy in copies:
         copy.wait()
 
 
-def drift_kernel(count, ids_ref, map_ref, *refs):
+def drift_kernel(count, ids_ref, map_ref, other_ref, *refs):
     piece_refs = refs[:count]
     routed_hbm, near_ref, weights_ref, rows_ref, stokes_ref, routed_ref, sems = refs[count:]
     own = ids_ref[0]
-    for turn, ref in enumerate(piece_refs):
-        stokes_ref[own ^ turn] = ref[6]
+    stokes = [
+        other_ref[turn // 2] if turn % 2 else ref[6] for turn, ref in enumerate(piece_refs)
+    ]
+    for turn, value in enumerate(stokes):
+        stokes_ref[own ^ turn] = value
     in_order = stokes_ref[...].reshape(-1, LANES).T
     weights_ref[0:16, :] = in_order[0:16]
     weights_ref[16:32, :] = in_order[64:80]
-    turned = joined(piece_refs, 6).T
+    turned = jnp.concatenate(stokes, axis=0).T
     column = columns_of(map_ref)
     picks = [chosen(column, slot).astype(jnp.float32).astype(jnp.bfloat16) for slot in range(2)]
     rows_ref[...] = jnp.zeros_like(rows_ref)
@@ -270,7 +284,7 @@
     for row in range(3):
         parts = [jnp.zeros((LANES, LANES), jnp.float32) for _ in range(2)]
         for half in range(2):
-            cells = joined(piece_refs, 2 * row + half)
+            cells = joined(piece_refs, 2 * placed(own, row) + half)
             drift = jnp.dot(turned, cells, preferred_element_type=jnp.float32)
             lanes = slice(half * LANES, (half + 1) * LANES)
             near_ref[row : row + 1, lanes] = drift[0:1]
@@ -357,7 +371,7 @@
     narrow_pick = pick.astype(jnp.bfloat16)
     for row in range(3):
         cells = jnp.concatenate(
-            [joined(piece_refs, 2 * row), joined(piece_refs, 2 * row + 1)], axis=1
+            [joined(piece_refs, 2 * row + half) for half in range(2)], axis=1
         )
         beside = jnp.dot(cells, narrow_pick, preferred_element_type=jnp.float32)
         for part in range(4):
@@ -415,7 +429,10 @@
             return (speed_x + current) * energy
 
         energy = [
-            [piece_ref[2 * row + half, span, :].astype(jnp.float32) for half in range(2)]
+            [
+                piece_ref[2 * placed(own, row) + half, span, :].astype(jnp.float32)
+                for half in range(2)
+            ]
             for row in range(3)
         ]
         for half in range(2):
@@ -434,13 +451,14 @@
             for half in range(2):
                 old, value = energy[row][half]
                 lanes = slice(half * LANES, (half + 1) * LANES)
+                at_row = placed(own, row)
                 spot = pl.ds(pl.multiple_of(turn * local_bins + start, BLOCK), BLOCK)
 
                 def side(at, cells, row=row, lanes=lanes):
                     return (speed_y + cur_ref[at + 1 + row : at + 2 + row, lanes]) * cells
 
-                left = side(40, beside_ref[row, half, spot, :].astype(jnp.float32))
-                right = side(48, beside_ref[row, 2 + half, spot, :].astype(jnp.float32))
+                left = side(40, beside_ref[at_row, half, spot, :].astype(jnp.float32))
+                right = side(48, beside_ref[at_row, 2 + half, spot, :].astype(jnp.float32))
                 wet = cur_ref[16 + row : 17 + row, lanes]
                 moved = value - jnp.abs(side(8, old))
                 result = wet * (moved + jnp.maximum(left, 0.0) - jnp.minimum(right, 0.0))
@@ -606,7 +624,10 @@
     sent = call(
         functools.partial(pack_kernel, order),
         [jax.ShapeDtypeStruct(piece_shape, bf16)]
-        + [pltpu.HBM(piece_shape, bf16)] * (bins_count - 1),
+        + [
+            pltpu.HBM((CHUNKS - turn % 2, local_bins, LANES), bf16)
+            for turn in range(1, bins_count)
+        ],
         [in_smem(), in_hbm(), in_hbm()],
         [in_vmem()] + [in_hbm()] * (bins_count - 1),
         [
@@ -642,41 +663,51 @@
     )
     arrived = lax.all_to_all(surface, both, split_axis=0, concat_axis=0, tiled=True)
     map_row = col_map.reshape(1, -1)
-    surface_rows, speed_rows, coefs, pair_rows = call(
+    coefs, pair_rows = call(
+        pairs_kernel,
+        (
+            pltpu.HBM((pairs, LANES), f32),
+            jax.ShapeDtypeStruct((3 * pairs // LANES, LANES), jnp.int32),
+        ),
+        [in_vmem()] * 2,
+        (in_hbm(), in_vmem()),
+        [VMEM((pairs, LANES), f32), pltpu.SemaphoreType.DMA((4,))],
+        1_000_000,
+        2_500_000,
+        (pair_coef.reshape(-1, LANES), pair_bins),
+    )
+    surface_rows, speed_rows = call(
         tables_kernel,
         (
             jax.ShapeDtypeStruct((32, columns), f32),
             pltpu.HBM((2, bins, LANES), f32),
-            pltpu.HBM((pairs, LANES), f32),
-            jax.ShapeDtypeStruct((3 * pairs // LANES, LANES), jnp.int32),
         ),
-        [in_vmem()] * 4,
-        (in_vmem(), in_hbm(), in_hbm(), in_vmem()),
-        [
-            VMEM((2, bins, LANES), f32),
-            VMEM((pairs, LANES), f32),
-            pltpu.SemaphoreType.DMA((6,)),
-        ],
+        [in_vmem()] * 2,
+        (in_vmem(), in_hbm()),
+        [VMEM((2, bins, LANES), f32), pltpu.SemaphoreType.DMA((2,))],
         600_000_000,
         1_300_000,
-        (arrived.reshape(devices, LANES), map_row, pair_coef.reshape(-1, LANES), pair_bins),
+        (arrived.reshape(devices, LANES), map_row),
     )
 
     halo_shape = (bins_count, 2, local_bins, LANES)
-    inner, outer = call(
+    stokes_shape = (bins_count // 2, local_bins, LANES)
+    inner, outer, stokes = call(
         edges_kernel,
-        [jax.ShapeDtypeStruct(halo_shape, bf16)] * 2,
-        [in_smem()] + [in_vmem()] * bins_count,
-        [in_vmem()] * 2,
+        [jax.ShapeDtypeStruct(halo_shape, bf16)] * 2 + [jax.ShapeDtypeStruct(stokes_shape, bf16)],
+        [in_vmem()] * bins_count,
+        [in_vmem()] * 3,
         [],
         1_000_000,
         2_400_000,
-        (ids, *pieces),
+        tuple(pieces),
     )
     outward = [(at, at + 1) for at in range(1, devices - 1, 2)]
     outward += [(at + 1, at) for at, _ in outward]
     outer = lax.ppermute(outer, both, outward)
-    inner = lax.ppermute(inner, both, [(at, at ^ 1) for at in range(devices)])
+    within = [(at, at ^ 1) for at in range(devices)]
+    inner = lax.ppermute(inner, both, within)
+    stokes = lax.ppermute(stokes, both, within)
 
     routed, near, weights = call(
         functools.partial(drift_kernel, bins_count),
@@ -685,7 +716,7 @@
             jax.ShapeDtypeStruct((16, columns), f32),
             jax.ShapeDtypeStruct((32, bins), bf16),
         ),
-        [in_smem(), in_vmem()] + [in_vmem()] * bins_count,
+        [in_smem()] + [in_vmem()] * (2 + bins_count),
         (in_hbm(), in_vmem(), in_vmem()),
         [
             VMEM((devices * 8, LANES), f32),
@@ -695,7 +726,7 @@
         ],
         300_000_000,
         2_500_000,
-        (ids, map_row, *pieces),
+        (ids, map_row, stokes, *pieces),
     )
     routed = lax.all_to_all(
         routed.reshape(devices, 8, LANES), both, split_axis=0, concat_axis=0, tiled=True

time: 99.4 us -> 96.3 us (0.969)
  starting transfers between devices: 31.3 us -> 29.1 us
    ppermute x7, starting transfers between devices: 13.6 us -> 11.5 us  [per_device(): pieces[turn] = lax.ppermute(sent[turn], 'bins', partners)]
    pallas_call x7 -> x8, Pallas kernels: 33.4 us -> 32.9 us  [call(): pl.pallas_call(body, out_shape=out_shape, in_specs=ins, out_specs=outs, s...]
  transfers between devices with their start and end apart: 11 -> 12, of which waited for: 6 -> 5; matrix products, arithmetic and copies ran while one was open for 0% -> 0% of each run, Pallas kernels for 9% -> 10%
where the time goes in v6:
time: 96.3 us; the launch traced here: 96.1 us
  waiting for transfers between devices  33.2 us (34%)
  Pallas kernels  32.9 us (34%)
  starting transfers between devices  29.1 us (30%)
    pallas_call x8, Pallas kernels, call(): pl.pallas_call(body, out_shape=out_shape, in_specs=ins, out_specs=outs, s...  32.9 us
    ppermute x7, waiting for transfers between devices, per_device(): pieces[turn] = lax.ppermute(sent[turn], 'bins', partners)  18.8 us
    ppermute x7, starting transfers between devices, per_device(): pieces[turn] = lax.ppermute(sent[turn], 'bins', partners)  11.5 us
    all_to_all x1, starting transfers between devices, per_device(): lax.all_to_all(surface, both, split_axis=0, concat_axis=0, tiled=True)  11.1 us
    all_to_all x1, waiting for transfers between devices, per_device(): lax.all_to_all(routed.reshape(devices, 8, LANES), both, split_axis=0, con...  7.37 us
    all_to_all x1, waiting for transfers between devices, per_device(): lax.all_to_all(surface, both, split_axis=0, concat_axis=0, tiled=True)  6.98 us
    all_to_all x1, starting transfers between devices, per_device(): lax.all_to_all(routed.reshape(devices, 8, LANES), both, split_axis=0, con...  4.38 us
    ppermute x1, starting transfers between devices, per_device(): outer = lax.ppermute(outer, both, outward)  2.04 us
  transfers between devices with their start and end apart: 12, of which 5 were waited for; matrix products, arithmetic and copies ran while one was open for 0% of the time, Pallas kernels for 10%

profile of v6, /device:TPU:1, one launch (start us, length us, event | category | flops | bytes accessed | tf_op | source)
XLA Modules:
  0.0 96.1 jit_solution(3432122795974103649)
XLA Ops:
  0.6 0.1 pad_add_fusion.ids_ref
  0.7 0.0 copy-start
  0.7 0.0 copy-start.4
  0.7 0.0 copy-start.5
  0.7 0.0 copy-start.6
  0.7 3.4 %shard_map.107 = (bf16[7,144,128]{2,1,0:T(8,128)(2,1)S(1)}, bf16[6,144,128]{2,1,0:T(8,128)(2,1)}, bf16[7,144,128]{2,1,0:T(8,128)(2,1)}, bf16[6,144,128]{2,1,0:T(...) custom-call(s32[4]{0:T(128)S(1)} %pad_add_fusion.ids_ref, ...), custom_call_target="tpu_custom_call" | custom-call | flops 2000000 | bytes 4000000 | tf_op jit(solution)/shard_map/pallas_call | solution.py:53
  4.1 1.5 %collective-permute-start = (bf16[6,144,128]{2,1,0:T(8,128)(2,1)}, bf16[6,144,128]{2,1,0:T(8,128)(2,1)S(1)}, u32[]{:S(2)}, u32[]{:S(2)}) collective-permute-start(bf16[6,144,128]{2,1,0:T(8,128)(2,1)} %get-tuple-element.24), channel_id=1, source_target_pairs={{0,1},{1,0},{2,3},{3,2},{4,5},{5,4},{6,7},{7,6},{8,9},{9,8},{10,11... | collective-permute-start | bytes 663560 | tf_op jit(solution)/shard_map/ppermute | solution.py:652
  5.6 1.4 %collective-permute-start.2 = (bf16[6,144,128]{2,1,0:T(8,128)(2,1)}, bf16[6,144,128]{2,1,0:T(8,128)(2,1)S(1)}, u32[]{:S(2)}, u32[]{:S(2)}) collective-permute-start(bf16[6,144,128]{2,1,0:T(8,128)(2,1)} %get-tuple-element.26), channel_id=1, source_target_pairs={{0,3},{1,2},{2,1},{3,0},{4,7},{5,6},{6,5},{7,4},{8,11},{9,10},{10,... | collective-permute-start | bytes 663560 | tf_op jit(solution)/shard_map/ppermute | solution.py:652
  6.9 0.1 collective-permute-start.1
  7.0 3.0 %collective-permute-start.3 = (bf16[7,144,128]{2,1,0:T(8,128)(2,1)}, bf16[7,144,128]{2,1,0:T(8,128)(2,1)S(1)}, u32[]{:S(2)}, u32[]{:S(2)}) collective-permute-start(bf16[7,144,128]{2,1,0:T(8,128)(2,1)} %get-tuple-element.27), channel_id=1, source_target_pairs={{0,4},{1,5},{2,6},{3,7},{4,0},{5,1},{6,2},{7,3},{8,12},{9,13},{10,... | collective-permute-start | bytes 774152 | tf_op jit(solution)/shard_map/ppermute | solution.py:652
  10.0 0.8 collective-permute-start.5
  10.8 0.0 collective-permute-done.refs_1_
  10.8 2.6 %collective-permute-start.4 = (bf16[6,144,128]{2,1,0:T(8,128)(2,1)}, bf16[6,144,128]{2,1,0:T(8,128)(2,1)S(1)}, u32[]{:S(2)}, u32[]{:S(2)}) collective-permute-start(bf16[6,144,128]{2,1,0:T(8,128)(2,1)} %get-tuple-element.28), channel_id=1, source_target_pairs={{0,5},{1,4},{2,7},{3,6},{4,1},{5,0},{6,3},{7,2},{8,13},{9,12},{10,... | collective-permute-start | bytes 663560 | tf_op jit(solution)/shard_map/ppermute | solution.py:652
  13.4 0.1 collective-permute-done.2.refs_3_
  13.5 2.2 %collective-permute-start.6 = (bf16[6,144,128]{2,1,0:T(8,128)(2,1)}, bf16[6,144,128]{2,1,0:T(8,128)(2,1)S(1)}, u32[]{:S(2)}, u32[]{:S(2)}) collective-permute-start(bf16[6,144,128]{2,1,0:T(8,128)(2,1)} %get-tuple-element.30), channel_id=1, source_target_pairs={{0,7},{1,6},{2,5},{3,4},{4,3},{5,2},{6,1},{7,0},{8,15},{9,14},{10,... | collective-permute-start | bytes 663560 | tf_op jit(solution)/shard_map/ppermute | solution.py:652
  15.7 15.6 %collective-permute-done.4.refs_5_ = bf16[6,144,128]{2,1,0:T(8,128)(2,1)S(1)} collective-permute-done((bf16[6,144,128]{2,1,0:T(8,128)(2,1)}, bf16[6,144,128]{2,1,0:T(8,128)(2,1)S(1)}, u32[]{:S(2)}, u32[]{:S(2)}) %collective-permute-start.4) | collective-permute-done | bytes 221216 | tf_op jit(solution)/shard_map/ppermute | solution.py:652
  31.4 3.0 %collective-permute-done.6.refs_7_ = bf16[6,144,128]{2,1,0:T(8,128)(2,1)S(1)} collective-permute-done((bf16[6,144,128]{2,1,0:T(8,128)(2,1)}, bf16[6,144,128]{2,1,0:T(8,128)(2,1)S(1)}, u32[]{:S(2)}, u32[]{:S(2)}) %collective-permute-start.6) | collective-permute-done | bytes 221216 | tf_op jit(solution)/shard_map/ppermute | solution.py:652
  34.4 0.0 collective-permute-done.1.refs_2_
  34.4 0.0 collective-permute-done.3.refs_4_
  34.4 0.0 collective-permute-done.5.refs_6_
  34.4 0.9 shard_map.108
  35.3 0.0 copy-start.1
  35.3 0.0 copy-start.3
  35.3 0.0 collective-permute-start.7
  35.3 2.0 %collective-permute-start.8 = (bf16[8,2,144,128]{3,2,1,0:T(8,128)(2,1)S(1)}, bf16[8,2,144,128]{3,2,1,0:T(8,128)(2,1)}, u32[]{:S(2)}, u32[]{:S(2)}) collective-permute-start(bf16[8,2,144,128]{3,2,1,0:T(8,128)(2,1)S(1)} %get-tuple-element.32), channel_id=1, source_target_pairs={{1,2},{3,4},{5,6},{7,8},{9,10},{11,12},{13,14},{15,16},{17,18},{19... | collective-permute-start | bytes 1769480 | tf_op jit(solution)/shard_map/ppermute | solution.py:707
  37.4 0.1 collective-permute-start.9
  37.5 0.0 copy-done
  37.5 0.0 copy-done.4
  37.5 0.0 copy-done.5
  37.5 1.8 %shard_map.105 = f32[128,128]{1,0:T(8,128)} custom-call(s32[4]{0:T(128)S(1)} %pad_add_fusion.ids_ref, f32[2,384,128]{2,1,0:T(8,128)S(1)} %copy-done, s32[2,384]{1,0:T(2,128)S(1)} %copy-done.4, f32[2,144]{1,0:T(2,128)S(1)} %copy-done.5), custom_call_target="tpu_custom_call" | custom-call | flops 4000000 | bytes 500000 | tf_op jit(solution)/shard_map/pallas_call | solution.py:53
  39.3 11.1 %all-to-all-start = ((f32[128,1,128]{2,1,0:T(1,128)}), f32[128,1,128]{2,1,0:T(1,128)S(1)}, u32[]{:S(2)}, u32[]{:S(2)}) async-start(f32[128,1,128]{2,1,0:T(1,128)} %bitcast.7), calls=%async_computation | async-start | bytes 131072 | tf_op jit(solution)/shard_map/all_to_all | solution.py:664
  50.4 0.0 collective-permute-done.9.other_ref
  50.4 0.0 copy-done.6
  50.4 2.6 %shard_map.109 = (bf16[1024,128]{1,0:T(8,128)(2,1)}, f32[16,256]{1,0:T(8,128)S(1)}, bf16[32,1152]{1,0:T(8,128)(2,1)S(1)}) custom-call(s32[4]{0:T(128)S(1)} %pad_add_fusion.ids_ref, s32[1,128]{1,0:T(1,128)S(1)} %bitcast.18, bf16[4,144,128]{2,1,0:T(8,128)(2,1)S(1)} %collective-permute-done.9.other_ref, bf16[7,144,128]{2,1,0:T(8,128)(2,1)S(1)} %get-tuple-element.23.refs_0_, ...), custom_call_target="tpu_custom_call" | custom-call | flops 300000000 | bytes 2500000 | tf_op jit(solution)/shard_map/pallas_call | solution.py:53
  53.1 7.0 %all-to-all-done = f32[128,1,128]{2,1,0:T(1,128)S(1)} async-done(((f32[128,1,128]{2,1,0:T(1,128)}), f32[128,1,128]{2,1,0:T(1,128)S(1)}, u32[]{:S(2)}, u32[]{:S(2)}) %all-to-all-start) | async-done | bytes 65568 | tf_op jit(solution)/shard_map/all_to_all | solution.py:664
  60.0 4.4 %all-to-all-start.1 = ((bf16[128,8,128]{2,1,0:T(8,128)(2,1)}), bf16[128,8,128]{2,1,0:T(8,128)(2,1)S(1)}, u32[]{:S(2)}, u32[]{:S(2)}) async-start(bf16[128,8,128]{2,1,0:T(8,128)(2,1)} %bitcast.21), calls=%async_computation.1 | async-start | bytes 524288 | tf_op jit(solution)/shard_map/all_to_all | solution.py:731
  64.4 0.0 copy-start.2
  64.4 0.0 copy-done.1
  64.5 0.0 copy-done.3
  64.5 1.7 %shard_map.104 = (f32[4608,128]{1,0:T(8,128)}, s32[108,128]{1,0:T(8,128)S(1)}) custom-call(f32[36,128]{1,0:T(8,128)S(1)} %bitcast.17, s32[3,4608]{1,0:T(4,128)S(1)} %copy-done.1), custom_call_target="tpu_custom_call" | custom-call | flops 1000000 | bytes 2500000 | tf_op jit(solution)/shard_map/pallas_call | solution.py:53
  66.2 2.0 %shard_map.106 = (f32[32,256]{1,0:T(8,128)S(1)}, f32[2,1152,128]{2,1,0:T(8,128)}) custom-call(f32[128,128]{1,0:T(8,128)S(1)} %bitcast.15, s32[1,128]{1,0:T(1,128)S(1)} %bitcast.19), custom_call_target="tpu_custom_call" | custom-call | flops 600000000 | bytes 1300000 | tf_op jit(solution)/shard_map/pallas_call | solution.py:53
  68.2 7.4 %all-to-all-done.1 = bf16[128,8,128]{2,1,0:T(8,128)(2,1)S(1)} async-done(((bf16[128,8,128]{2,1,0:T(8,128)(2,1)}), bf16[128,8,128]{2,1,0:T(8,128)(2,1)S(1)}, u32[]{:S(2)}, u32[]{:S(2)}) %all-to-all-start.1) | async-done | bytes 262176 | tf_op jit(solution)/shard_map/all_to_all | solution.py:731
  75.5 1.4 %shard_map.111 = f32[2,384,128]{2,1,0:T(8,128)} custom-call(f32[2,384,128]{2,1,0:T(8,128)S(1)} %copy-done, bf16[1024,128]{1,0:T(8,128)(2,1)S(1)} %bitcast.14, s32[2,384]{1,0:T(2,128)S(1)} %copy-done.4), custom_call_target="tpu_custom_call" | custom-call | flops 4000000 | bytes 1500000 | tf_op jit(solution)/shard_map/pallas_call | solution.py:53
  76.9 0.0 collective-permute-done.7.inner_hbm
  76.9 0.0 collective-permute-done.8.outer_hbm
  76.9 0.0 copy-done.2
  76.9 19.2 %shard_map.110 = bf16[3,1152,256]{2,1,0:T(8,128)(2,1)} custom-call(s32[4]{0:T(128)S(1)} %pad_add_fusion.ids_ref, s32[13824]{0:T(1024)S(1)} %bitcast.16, f32[4608,128]{1,0:T(8,128)} %get-tuple-element.21.coef_hbm, f32[2,1152,128]{2,1,0:T(8,128)} %get-tuple-element.22.speeds_hbm, bf16[8,2,144,128]{3,2,1,0:T(8,128)(2,1)} %collective-permute-done.7.inner_hbm, ...), custom_call_target="tpu_custom_call" | custom-call | flops 40000000 | bytes 8000000 | tf_op jit(solution)/shard_map/pallas_call | solution.py:53
Async XLA Ops:
  0.7 36.8 %copy-start = (f32[2,384,128]{2,1,0:T(8,128)S(1)}, f32[2,384,128]{2,1,0:T(8,128)}, u32[]{:S(2)}) copy-start(f32[2,384,128]{2,1,0:T(8,128)} %currents_ref.3) | copy-start | bytes 1179652
  0.7 36.8 %copy-start.4 = (s32[2,384]{1,0:T(2,128)S(1)}, s32[2,384]{1,0:T(2,128)}, u32[]{:S(2)}) copy-start(s32[2,384]{1,0:T(2,128)} %wet_ref.5) | copy-start | bytes 9220
  0.7 36.8 %copy-start.5 = (f32[2,144]{1,0:T(2,128)S(1)}, f32[2,144]{1,0:T(2,128)}, u32[]{:S(2)}) copy-start(f32[2,144]{1,0:T(2,128)} %speed_ref.1) | copy-start | bytes 3460
  0.7 49.7 %copy-start.6 = (s32[128]{0:T(128)S(1)}, s32[128]{0:T(128)}, u32[]{:S(2)}) copy-start(s32[128]{0:T(128)} %param.15) | copy-start | bytes 1540
  4.1 6.7 %collective-permute-start = (bf16[6,144,128]{2,1,0:T(8,128)(2,1)}, bf16[6,144,128]{2,1,0:T(8,128)(2,1)S(1)}, u32[]{:S(2)}, u32[]{:S(2)}) collective-permute-start(bf16[6,144,128]{2,1,0:T(8,128)(2,1)} %get-tuple-element.24), channel_id=1, source_target_pairs={{0,1},{1,0},{2,3},{3,2},{4,5},{5,4},{6,7},{7,6},{8,9},{9,8},{10,11... | collective-permute-start | bytes 663560 | tf_op jit(solution)/shard_map/ppermute | solution.py:652
  5.6 7.9 %collective-permute-start.2 = (bf16[6,144,128]{2,1,0:T(8,128)(2,1)}, bf16[6,144,128]{2,1,0:T(8,128)(2,1)S(1)}, u32[]{:S(2)}, u32[]{:S(2)}) collective-permute-start(bf16[6,144,128]{2,1,0:T(8,128)(2,1)} %get-tuple-element.26), channel_id=1, source_target_pairs={{0,3},{1,2},{2,1},{3,0},{4,7},{5,6},{6,5},{7,4},{8,11},{9,10},{10,... | collective-permute-start | bytes 663560 | tf_op jit(solution)/shard_map/ppermute | solution.py:652
  6.9 27.5 %collective-permute-start.1 = (bf16[7,144,128]{2,1,0:T(8,128)(2,1)}, bf16[7,144,128]{2,1,0:T(8,128)(2,1)S(1)}, u32[]{:S(2)}, u32[]{:S(2)}) collective-permute-start(bf16[7,144,128]{2,1,0:T(8,128)(2,1)} %get-tuple-element.25), channel_id=1, source_target_pairs={{0,2},{1,3},{2,0},{3,1},{4,6},{5,7},{6,4},{7,5},{8,10},{9,11},{10,... | collective-permute-start | bytes 774152 | tf_op jit(solution)/shard_map/ppermute | solution.py:652
  7.0 27.4 %collective-permute-start.3 = (bf16[7,144,128]{2,1,0:T(8,128)(2,1)}, bf16[7,144,128]{2,1,0:T(8,128)(2,1)S(1)}, u32[]{:S(2)}, u32[]{:S(2)}) collective-permute-start(bf16[7,144,128]{2,1,0:T(8,128)(2,1)} %get-tuple-element.27), channel_id=1, source_target_pairs={{0,4},{1,5},{2,6},{3,7},{4,0},{5,1},{6,2},{7,3},{8,12},{9,13},{10,... | collective-permute-start | bytes 774152 | tf_op jit(solution)/shard_map/ppermute | solution.py:652
  10.0 24.4 %collective-permute-start.5 = (bf16[7,144,128]{2,1,0:T(8,128)(2,1)}, bf16[7,144,128]{2,1,0:T(8,128)(2,1)S(1)}, u32[]{:S(2)}, u32[]{:S(2)}) collective-permute-start(bf16[7,144,128]{2,1,0:T(8,128)(2,1)} %get-tuple-element.29), channel_id=1, source_target_pairs={{0,6},{1,7},{2,4},{3,5},{4,2},{5,3},{6,0},{7,1},{8,14},{9,15},{10,... | collective-permute-start | bytes 774152 | tf_op jit(solution)/shard_map/ppermute | solution.py:652
  10.8 20.6 %collective-permute-start.4 = (bf16[6,144,128]{2,1,0:T(8,128)(2,1)}, bf16[6,144,128]{2,1,0:T(8,128)(2,1)S(1)}, u32[]{:S(2)}, u32[]{:S(2)}) collective-permute-start(bf16[6,144,128]{2,1,0:T(8,128)(2,1)} %get-tuple-element.28), channel_id=1, source_target_pairs={{0,5},{1,4},{2,7},{3,6},{4,1},{5,0},{6,3},{7,2},{8,13},{9,12},{10,... | collective-permute-start | bytes 663560 | tf_op jit(solution)/shard_map/ppermute | solution.py:652
  13.5 20.9 %collective-permute-start.6 = (bf16[6,144,128]{2,1,0:T(8,128)(2,1)}, bf16[6,144,128]{2,1,0:T(8,128)(2,1)S(1)}, u32[]{:S(2)}, u32[]{:S(2)}) collective-permute-start(bf16[6,144,128]{2,1,0:T(8,128)(2,1)} %get-tuple-element.30), channel_id=1, source_target_pairs={{0,7},{1,6},{2,5},{3,4},{4,3},{5,2},{6,1},{7,0},{8,15},{9,14},{10,... | collective-permute-start | bytes 663560 | tf_op jit(solution)/shard_map/ppermute | solution.py:652
  35.3 29.1 %copy-start.1 = (s32[3,4608]{1,0:T(4,128)S(1)}, s32[3,4608]{1,0:T(4,128)}, u32[]{:S(2)}) copy-start(s32[3,4608]{1,0:T(4,128)} %pair_ref.1) | copy-start | bytes 165892
  35.3 29.1 %copy-start.3 = (f32[4608]{0:T(1024)S(1)}, f32[4608]{0:T(1024)}, u32[]{:S(2)}) copy-start(f32[4608]{0:T(1024)} %param.13) | copy-start | bytes 55300
  35.3 41.6 %collective-permute-start.7 = (bf16[8,2,144,128]{3,2,1,0:T(8,128)(2,1)}, bf16[8,2,144,128]{3,2,1,0:T(8,128)(2,1)}, u32[]{:S(2)}, u32[]{:S(2)}) collective-permute-start(bf16[8,2,144,128]{3,2,1,0:T(8,128)(2,1)} %get-tuple-element.31), channel_id=1, source_target_pairs={{0,1},{1,0},{2,3},{3,2},{4,5},{5,4},{6,7},{7,6},{8,9},{9,8},{10,11... | collective-permute-start | bytes 1769480 | tf_op jit(solution)/shard_map/ppermute | solution.py:709
  35.3 41.6 %collective-permute-start.8 = (bf16[8,2,144,128]{3,2,1,0:T(8,128)(2,1)S(1)}, bf16[8,2,144,128]{3,2,1,0:T(8,128)(2,1)}, u32[]{:S(2)}, u32[]{:S(2)}) collective-permute-start(bf16[8,2,144,128]{3,2,1,0:T(8,128)(2,1)S(1)} %get-tuple-element.32), channel_id=1, source_target_pairs={{1,2},{3,4},{5,6},{7,8},{9,10},{11,12},{13,14},{15,16},{17,18},{19... | collective-permute-start | bytes 1769480 | tf_op jit(solution)/shard_map/ppermute | solution.py:707
  37.4 13.0 %collective-permute-start.9 = (bf16[4,144,128]{2,1,0:T(8,128)(2,1)S(1)}, bf16[4,144,128]{2,1,0:T(8,128)(2,1)S(1)}, u32[]{:S(2)}, u32[]{:S(2)}) collective-permute-start(bf16[4,144,128]{2,1,0:T(8,128)(2,1)S(1)} %get-tuple-element.34), channel_id=1, source_target_pairs={{0,1},{1,0},{2,3},{3,2},{4,5},{5,4},{6,7},{7,6},{8,9},{9,8},{10,11... | collective-permute-start | bytes 442376 | tf_op jit(solution)/shard_map/ppermute | solution.py:710
  39.3 20.8 %all-to-all-start = ((f32[128,1,128]{2,1,0:T(1,128)}), f32[128,1,128]{2,1,0:T(1,128)S(1)}, u32[]{:S(2)}, u32[]{:S(2)}) async-start(f32[128,1,128]{2,1,0:T(1,128)} %bitcast.7), calls=%async_computation | async-start | bytes 131072 | tf_op jit(solution)/shard_map/all_to_all | solution.py:664
  60.0 15.5 %all-to-all-start.1 = ((bf16[128,8,128]{2,1,0:T(8,128)(2,1)}), bf16[128,8,128]{2,1,0:T(8,128)(2,1)S(1)}, u32[]{:S(2)}, u32[]{:S(2)}) async-start(bf16[128,8,128]{2,1,0:T(8,128)(2,1)} %bitcast.21), calls=%async_computation.1 | async-start | bytes 524288 | tf_op jit(solution)/shard_map/all_to_all | solution.py:731
  64.4 12.5 %copy-start.2 = (s32[24,256]{1,0:T(8,128)S(1)}, s32[24,256]{1,0:T(8,128)}, u32[]{:S(2)}) copy-start(s32[24,256]{1,0:T(8,128)} %wet_ref.4) | copy-start | bytes 73732

commit v7 on v6

--- a/solution.py
+++ b/solution.py
@@ -18,7 +18,7 @@
 ACCS = 3
 WAVE_LIMIT = 36
 CHUNKS = 7
-UNROLL = 48
+UNROLL = 144
 BLOCK = 16
 PITCH = 24
 ROW_GAP = 400
@@ -167,15 +167,16 @@
     index = lax.broadcasted_iota(jnp.int32, (local_bins, LANES), 0) - ids_ref[3] * piece
     place = lax.broadcasted_iota(jnp.int32, (local_bins, LANES), 1) - SPEED_LANE
     inside = (index >= 0) & (index < piece)
-    speeds = jnp.zeros((1, LANES), jnp.float32)
-    for part in range(2):
-        pick = (inside & (place == index + part * piece)).astype(jnp.float32)
-        speeds = speeds + jnp.dot(
-            speed_ref[part : part + 1, :],
-            pick,
-            precision=HIGHEST,
-            preferred_element_type=jnp.float32,
-        )
+    pick = inside & ((place == index) | (place == index + piece))
+    split = jnp.concatenate(thirds(speed_ref[...]), axis=0)
+    found = jnp.dot(
+        split,
+        pick.astype(jnp.float32).astype(jnp.bfloat16),
+        preferred_element_type=jnp.float32,
+    )
+    found = found[0:2] + found[2:4] + found[4:6]
+    spot = lax.broadcasted_iota(jnp.int32, (1, LANES), 1)
+    speeds = jnp.where(spot < SPEED_LANE + piece, found[0:1], found[1:2])
     total = jnp.broadcast_to(speeds, (LANES, LANES))
     for slot in range(2):
         for row in range(5):
@@ -514,7 +515,7 @@
                 )
         return carry
 
-    parts = 4
+    parts = 6
     out_copies = []
     for part in range(parts):
         span = pl.ds(part * (bins // parts), bins // parts)
@@ -574,7 +575,7 @@
             VMEM((8 * PITCH, LANES), f32),
             VMEM((rows, 4, bins, LANES), jnp.bfloat16),
             pltpu.SemaphoreType.DMA((5,)),
-            pltpu.SemaphoreType.DMA((12,)),
+            pltpu.SemaphoreType.DMA((18,)),
         ]
         + [VMEM((bins * 8, LANES), f32)] * ACCS,
         40_000_000,
@@ -619,7 +620,7 @@
     near_ids = [lax.rem(bins_at + step, bins_count) for step in (bins_count - 1, 1)]
     ids = jnp.stack([bins_at, *near_ids, space_at]).astype(jnp.int32)
 
-    order = (4, 5, 2, 6, 3, 7, 1, 0)
+    order = (4, 5, 3, 6, 2, 7, 1, 0)
     piece_shape = (CHUNKS, local_bins, LANES)
     sent = call(
         functools.partial(pack_kernel, order),

time: 96.3 us -> 96.1 us (level)
  no operation moved by 1% of the time
where the time goes in v7:
time: 96.1 us; the launch traced here: 95.9 us
  waiting for transfers between devices  33.2 us (35%)
  Pallas kernels  32.7 us (34%)
  starting transfers between devices  29.1 us (30%)
    pallas_call x8, Pallas kernels, call(): pl.pallas_call(body, out_shape=out_shape, in_specs=ins, out_specs=outs, s...  32.7 us
    ppermute x7, waiting for transfers between devices, per_device(): pieces[turn] = lax.ppermute(sent[turn], 'bins', partners)  18.8 us
    ppermute x7, starting transfers between devices, per_device(): pieces[turn] = lax.ppermute(sent[turn], 'bins', partners)  11.5 us
    all_to_all x1, starting transfers between devices, per_device(): lax.all_to_all(surface, both, split_axis=0, concat_axis=0, tiled=True)  11.1 us
    all_to_all x1, waiting for transfers between devices, per_device(): lax.all_to_all(routed.reshape(devices, 8, LANES), both, split_axis=0, con...  7.36 us
    all_to_all x1, waiting for transfers between devices, per_device(): lax.all_to_all(surface, both, split_axis=0, concat_axis=0, tiled=True)  6.98 us
    all_to_all x1, starting transfers between devices, per_device(): lax.all_to_all(routed.reshape(devices, 8, LANES), both, split_axis=0, con...  4.38 us
    ppermute x1, starting transfers between devices, per_device(): outer = lax.ppermute(outer, both, outward)  2.04 us
  transfers between devices with their start and end apart: 12, of which 5 were waited for; matrix products, arithmetic and copies ran while one was open for 0% of the time, Pallas kernels for 10%

profile of v7, /device:TPU:1, one launch (start us, length us, event | category | flops | bytes accessed | tf_op | source)
XLA Modules:
  0.0 95.9 jit_solution(1873396265769462799)
XLA Ops:
  0.6 0.1 pad_add_fusion.ids_ref
  0.7 0.0 copy-start
  0.7 0.0 copy-start.4
  0.7 0.0 copy-start.5
  0.7 0.0 copy-start.6
  0.7 3.4 %shard_map.107 = (bf16[7,144,128]{2,1,0:T(8,128)(2,1)S(1)}, bf16[6,144,128]{2,1,0:T(8,128)(2,1)}, bf16[7,144,128]{2,1,0:T(8,128)(2,1)}, bf16[6,144,128]{2,1,0:T(...) custom-call(s32[4]{0:T(128)S(1)} %pad_add_fusion.ids_ref, ...), custom_call_target="tpu_custom_call" | custom-call | flops 2000000 | bytes 4000000 | tf_op jit(solution)/shard_map/pallas_call | solution.py:53
  4.1 1.5 %collective-permute-start = (bf16[6,144,128]{2,1,0:T(8,128)(2,1)}, bf16[6,144,128]{2,1,0:T(8,128)(2,1)S(1)}, u32[]{:S(2)}, u32[]{:S(2)}) collective-permute-start(bf16[6,144,128]{2,1,0:T(8,128)(2,1)} %get-tuple-element.24), channel_id=1, source_target_pairs={{0,1},{1,0},{2,3},{3,2},{4,5},{5,4},{6,7},{7,6},{8,9},{9,8},{10,11... | collective-permute-start | bytes 663560 | tf_op jit(solution)/shard_map/ppermute | solution.py:653
  5.6 1.4 %collective-permute-start.2 = (bf16[6,144,128]{2,1,0:T(8,128)(2,1)}, bf16[6,144,128]{2,1,0:T(8,128)(2,1)S(1)}, u32[]{:S(2)}, u32[]{:S(2)}) collective-permute-start(bf16[6,144,128]{2,1,0:T(8,128)(2,1)} %get-tuple-element.26), channel_id=1, source_target_pairs={{0,3},{1,2},{2,1},{3,0},{4,7},{5,6},{6,5},{7,4},{8,11},{9,10},{10,... | collective-permute-start | bytes 663560 | tf_op jit(solution)/shard_map/ppermute | solution.py:653
  6.9 0.1 collective-permute-start.1
  7.0 3.0 %collective-permute-start.3 = (bf16[7,144,128]{2,1,0:T(8,128)(2,1)}, bf16[7,144,128]{2,1,0:T(8,128)(2,1)S(1)}, u32[]{:S(2)}, u32[]{:S(2)}) collective-permute-start(bf16[7,144,128]{2,1,0:T(8,128)(2,1)} %get-tuple-element.27), channel_id=1, source_target_pairs={{0,4},{1,5},{2,6},{3,7},{4,0},{5,1},{6,2},{7,3},{8,12},{9,13},{10,... | collective-permute-start | bytes 774152 | tf_op jit(solution)/shard_map/ppermute | solution.py:653
  10.0 0.8 collective-permute-start.5
  10.8 0.0 collective-permute-done.refs_1_
  10.8 2.6 %collective-permute-start.4 = (bf16[6,144,128]{2,1,0:T(8,128)(2,1)}, bf16[6,144,128]{2,1,0:T(8,128)(2,1)S(1)}, u32[]{:S(2)}, u32[]{:S(2)}) collective-permute-start(bf16[6,144,128]{2,1,0:T(8,128)(2,1)} %get-tuple-element.28), channel_id=1, source_target_pairs={{0,5},{1,4},{2,7},{3,6},{4,1},{5,0},{6,3},{7,2},{8,13},{9,12},{10,... | collective-permute-start | bytes 663560 | tf_op jit(solution)/shard_map/ppermute | solution.py:653
  13.4 0.1 collective-permute-done.2.refs_3_
  13.5 2.2 %collective-permute-start.6 = (bf16[6,144,128]{2,1,0:T(8,128)(2,1)}, bf16[6,144,128]{2,1,0:T(8,128)(2,1)S(1)}, u32[]{:S(2)}, u32[]{:S(2)}) collective-permute-start(bf16[6,144,128]{2,1,0:T(8,128)(2,1)} %get-tuple-element.30), channel_id=1, source_target_pairs={{0,7},{1,6},{2,5},{3,4},{4,3},{5,2},{6,1},{7,0},{8,15},{9,14},{10,... | collective-permute-start | bytes 663560 | tf_op jit(solution)/shard_map/ppermute | solution.py:653
  15.7 15.6 %collective-permute-done.4.refs_5_ = bf16[6,144,128]{2,1,0:T(8,128)(2,1)S(1)} collective-permute-done((bf16[6,144,128]{2,1,0:T(8,128)(2,1)}, bf16[6,144,128]{2,1,0:T(8,128)(2,1)S(1)}, u32[]{:S(2)}, u32[]{:S(2)}) %collective-permute-start.4) | collective-permute-done | bytes 221216 | tf_op jit(solution)/shard_map/ppermute | solution.py:653
  31.4 3.0 %collective-permute-done.6.refs_7_ = bf16[6,144,128]{2,1,0:T(8,128)(2,1)S(1)} collective-permute-done((bf16[6,144,128]{2,1,0:T(8,128)(2,1)}, bf16[6,144,128]{2,1,0:T(8,128)(2,1)S(1)}, u32[]{:S(2)}, u32[]{:S(2)}) %collective-permute-start.6) | collective-permute-done | bytes 221216 | tf_op jit(solution)/shard_map/ppermute | solution.py:653
  34.4 0.0 collective-permute-done.1.refs_2_
  34.4 0.0 collective-permute-done.3.refs_4_
  34.4 0.0 collective-permute-done.5.refs_6_
  34.4 0.9 shard_map.108
  35.3 0.0 copy-start.1
  35.3 0.0 copy-start.3
  35.3 0.0 collective-permute-start.7
  35.3 2.0 %collective-permute-start.8 = (bf16[8,2,144,128]{3,2,1,0:T(8,128)(2,1)S(1)}, bf16[8,2,144,128]{3,2,1,0:T(8,128)(2,1)}, u32[]{:S(2)}, u32[]{:S(2)}) collective-permute-start(bf16[8,2,144,128]{3,2,1,0:T(8,128)(2,1)S(1)} %get-tuple-element.32), channel_id=1, source_target_pairs={{1,2},{3,4},{5,6},{7,8},{9,10},{11,12},{13,14},{15,16},{17,18},{19... | collective-permute-start | bytes 1769480 | tf_op jit(solution)/shard_map/ppermute | solution.py:708
  37.4 0.1 collective-permute-start.9
  37.5 0.0 copy-done
  37.5 0.0 copy-done.4
  37.5 0.0 copy-done.5
  37.5 1.8 %shard_map.105 = f32[128,128]{1,0:T(8,128)} custom-call(s32[4]{0:T(128)S(1)} %pad_add_fusion.ids_ref, f32[2,384,128]{2,1,0:T(8,128)S(1)} %copy-done, s32[2,384]{1,0:T(2,128)S(1)} %copy-done.4, f32[2,144]{1,0:T(2,128)S(1)} %copy-done.5), custom_call_target="tpu_custom_call" | custom-call | flops 4000000 | bytes 500000 | tf_op jit(solution)/shard_map/pallas_call | solution.py:53
  39.3 11.1 %all-to-all-start = ((f32[128,1,128]{2,1,0:T(1,128)}), f32[128,1,128]{2,1,0:T(1,128)S(1)}, u32[]{:S(2)}, u32[]{:S(2)}) async-start(f32[128,1,128]{2,1,0:T(1,128)} %bitcast.7), calls=%async_computation | async-start | bytes 131072 | tf_op jit(solution)/shard_map/all_to_all | solution.py:665
  50.4 0.0 collective-permute-done.9.other_ref
  50.5 0.0 copy-done.6
  50.5 2.6 %shard_map.109 = (bf16[1024,128]{1,0:T(8,128)(2,1)}, f32[16,256]{1,0:T(8,128)S(1)}, bf16[32,1152]{1,0:T(8,128)(2,1)S(1)}) custom-call(s32[4]{0:T(128)S(1)} %pad_add_fusion.ids_ref, s32[1,128]{1,0:T(1,128)S(1)} %bitcast.18, bf16[4,144,128]{2,1,0:T(8,128)(2,1)S(1)} %collective-permute-done.9.other_ref, bf16[7,144,128]{2,1,0:T(8,128)(2,1)S(1)} %get-tuple-element.23.refs_0_, ...), custom_call_target="tpu_custom_call" | custom-call | flops 300000000 | bytes 2500000 | tf_op jit(solution)/shard_map/pallas_call | solution.py:53
  53.1 7.0 %all-to-all-done = f32[128,1,128]{2,1,0:T(1,128)S(1)} async-done(((f32[128,1,128]{2,1,0:T(1,128)}), f32[128,1,128]{2,1,0:T(1,128)S(1)}, u32[]{:S(2)}, u32[]{:S(2)}) %all-to-all-start) | async-done | bytes 65568 | tf_op jit(solution)/shard_map/all_to_all | solution.py:665
  60.1 4.4 %all-to-all-start.1 = ((bf16[128,8,128]{2,1,0:T(8,128)(2,1)}), bf16[128,8,128]{2,1,0:T(8,128)(2,1)S(1)}, u32[]{:S(2)}, u32[]{:S(2)}) async-start(bf16[128,8,128]{2,1,0:T(8,128)(2,1)} %bitcast.21), calls=%async_computation.1 | async-start | bytes 524288 | tf_op jit(solution)/shard_map/all_to_all | solution.py:732
  64.5 0.0 copy-start.2
  64.5 0.0 copy-done.1
  64.5 0.0 copy-done.3
  64.5 1.7 %shard_map.104 = (f32[4608,128]{1,0:T(8,128)}, s32[108,128]{1,0:T(8,128)S(1)}) custom-call(f32[36,128]{1,0:T(8,128)S(1)} %bitcast.17, s32[3,4608]{1,0:T(4,128)S(1)} %copy-done.1), custom_call_target="tpu_custom_call" | custom-call | flops 1000000 | bytes 2500000 | tf_op jit(solution)/shard_map/pallas_call | solution.py:53
  66.2 2.0 %shard_map.106 = (f32[32,256]{1,0:T(8,128)S(1)}, f32[2,1152,128]{2,1,0:T(8,128)}) custom-call(f32[128,128]{1,0:T(8,128)S(1)} %bitcast.15, s32[1,128]{1,0:T(1,128)S(1)} %bitcast.19), custom_call_target="tpu_custom_call" | custom-call | flops 600000000 | bytes 1300000 | tf_op jit(solution)/shard_map/pallas_call | solution.py:53
  68.2 7.4 %all-to-all-done.1 = bf16[128,8,128]{2,1,0:T(8,128)(2,1)S(1)} async-done(((bf16[128,8,128]{2,1,0:T(8,128)(2,1)}), bf16[128,8,128]{2,1,0:T(8,128)(2,1)S(1)}, u32[]{:S(2)}, u32[]{:S(2)}) %all-to-all-start.1) | async-done | bytes 262176 | tf_op jit(solution)/shard_map/all_to_all | solution.py:732
  75.6 1.4 %shard_map.111 = f32[2,384,128]{2,1,0:T(8,128)} custom-call(f32[2,384,128]{2,1,0:T(8,128)S(1)} %copy-done, bf16[1024,128]{1,0:T(8,128)(2,1)S(1)} %bitcast.14, s32[2,384]{1,0:T(2,128)S(1)} %copy-done.4), custom_call_target="tpu_custom_call" | custom-call | flops 4000000 | bytes 1500000 | tf_op jit(solution)/shard_map/pallas_call | solution.py:53
  77.0 0.0 collective-permute-done.7.inner_hbm
  77.0 0.0 collective-permute-done.8.outer_hbm
  77.0 0.0 copy-done.2
  77.0 18.9 %shard_map.110 = bf16[3,1152,256]{2,1,0:T(8,128)(2,1)} custom-call(s32[4]{0:T(128)S(1)} %pad_add_fusion.ids_ref, s32[13824]{0:T(1024)S(1)} %bitcast.16, f32[4608,128]{1,0:T(8,128)} %get-tuple-element.21.coef_hbm, f32[2,1152,128]{2,1,0:T(8,128)} %get-tuple-element.22.speeds_hbm, bf16[8,2,144,128]{3,2,1,0:T(8,128)(2,1)} %collective-permute-done.7.inner_hbm, ...), custom_call_target="tpu_custom_call" | custom-call | flops 40000000 | bytes 8000000 | tf_op jit(solution)/shard_map/pallas_call | solution.py:53
Async XLA Ops:
  0.7 36.8 %copy-start = (f32[2,384,128]{2,1,0:T(8,128)S(1)}, f32[2,384,128]{2,1,0:T(8,128)}, u32[]{:S(2)}) copy-start(f32[2,384,128]{2,1,0:T(8,128)} %currents_ref.3) | copy-start | bytes 1179652
  0.7 36.8 %copy-start.4 = (s32[2,384]{1,0:T(2,128)S(1)}, s32[2,384]{1,0:T(2,128)}, u32[]{:S(2)}) copy-start(s32[2,384]{1,0:T(2,128)} %wet_ref.5) | copy-start | bytes 9220
  0.7 36.8 %copy-start.5 = (f32[2,144]{1,0:T(2,128)S(1)}, f32[2,144]{1,0:T(2,128)}, u32[]{:S(2)}) copy-start(f32[2,144]{1,0:T(2,128)} %speed_ref.1) | copy-start | bytes 3460
  0.7 49.7 %copy-start.6 = (s32[128]{0:T(128)S(1)}, s32[128]{0:T(128)}, u32[]{:S(2)}) copy-start(s32[128]{0:T(128)} %param.15) | copy-start | bytes 1540
  4.1 6.7 %collective-permute-start = (bf16[6,144,128]{2,1,0:T(8,128)(2,1)}, bf16[6,144,128]{2,1,0:T(8,128)(2,1)S(1)}, u32[]{:S(2)}, u32[]{:S(2)}) collective-permute-start(bf16[6,144,128]{2,1,0:T(8,128)(2,1)} %get-tuple-element.24), channel_id=1, source_target_pairs={{0,1},{1,0},{2,3},{3,2},{4,5},{5,4},{6,7},{7,6},{8,9},{9,8},{10,11... | collective-permute-start | bytes 663560 | tf_op jit(solution)/shard_map/ppermute | solution.py:653
  5.6 7.9 %collective-permute-start.2 = (bf16[6,144,128]{2,1,0:T(8,128)(2,1)}, bf16[6,144,128]{2,1,0:T(8,128)(2,1)S(1)}, u32[]{:S(2)}, u32[]{:S(2)}) collective-permute-start(bf16[6,144,128]{2,1,0:T(8,128)(2,1)} %get-tuple-element.26), channel_id=1, source_target_pairs={{0,3},{1,2},{2,1},{3,0},{4,7},{5,6},{6,5},{7,4},{8,11},{9,10},{10,... | collective-permute-start | bytes 663560 | tf_op jit(solution)/shard_map/ppermute | solution.py:653
  6.9 27.5 %collective-permute-start.1 = (bf16[7,144,128]{2,1,0:T(8,128)(2,1)}, bf16[7,144,128]{2,1,0:T(8,128)(2,1)S(1)}, u32[]{:S(2)}, u32[]{:S(2)}) collective-permute-start(bf16[7,144,128]{2,1,0:T(8,128)(2,1)} %get-tuple-element.25), channel_id=1, source_target_pairs={{0,2},{1,3},{2,0},{3,1},{4,6},{5,7},{6,4},{7,5},{8,10},{9,11},{10,... | collective-permute-start | bytes 774152 | tf_op jit(solution)/shard_map/ppermute | solution.py:653
  7.0 27.4 %collective-permute-start.3 = (bf16[7,144,128]{2,1,0:T(8,128)(2,1)}, bf16[7,144,128]{2,1,0:T(8,128)(2,1)S(1)}, u32[]{:S(2)}, u32[]{:S(2)}) collective-permute-start(bf16[7,144,128]{2,1,0:T(8,128)(2,1)} %get-tuple-element.27), channel_id=1, source_target_pairs={{0,4},{1,5},{2,6},{3,7},{4,0},{5,1},{6,2},{7,3},{8,12},{9,13},{10,... | collective-permute-start | bytes 774152 | tf_op jit(solution)/shard_map/ppermute | solution.py:653
  10.0 24.4 %collective-permute-start.5 = (bf16[7,144,128]{2,1,0:T(8,128)(2,1)}, bf16[7,144,128]{2,1,0:T(8,128)(2,1)S(1)}, u32[]{:S(2)}, u32[]{:S(2)}) collective-permute-start(bf16[7,144,128]{2,1,0:T(8,128)(2,1)} %get-tuple-element.29), channel_id=1, source_target_pairs={{0,6},{1,7},{2,4},{3,5},{4,2},{5,3},{6,0},{7,1},{8,14},{9,15},{10,... | collective-permute-start | bytes 774152 | tf_op jit(solution)/shard_map/ppermute | solution.py:653
  10.8 20.6 %collective-permute-start.4 = (bf16[6,144,128]{2,1,0:T(8,128)(2,1)}, bf16[6,144,128]{2,1,0:T(8,128)(2,1)S(1)}, u32[]{:S(2)}, u32[]{:S(2)}) collective-permute-start(bf16[6,144,128]{2,1,0:T(8,128)(2,1)} %get-tuple-element.28), channel_id=1, source_target_pairs={{0,5},{1,4},{2,7},{3,6},{4,1},{5,0},{6,3},{7,2},{8,13},{9,12},{10,... | collective-permute-start | bytes 663560 | tf_op jit(solution)/shard_map/ppermute | solution.py:653
  13.5 20.9 %collective-permute-start.6 = (bf16[6,144,128]{2,1,0:T(8,128)(2,1)}, bf16[6,144,128]{2,1,0:T(8,128)(2,1)S(1)}, u32[]{:S(2)}, u32[]{:S(2)}) collective-permute-start(bf16[6,144,128]{2,1,0:T(8,128)(2,1)} %get-tuple-element.30), channel_id=1, source_target_pairs={{0,7},{1,6},{2,5},{3,4},{4,3},{5,2},{6,1},{7,0},{8,15},{9,14},{10,... | collective-permute-start | bytes 663560 | tf_op jit(solution)/shard_map/ppermute | solution.py:653
  35.3 29.2 %copy-start.1 = (s32[3,4608]{1,0:T(4,128)S(1)}, s32[3,4608]{1,0:T(4,128)}, u32[]{:S(2)}) copy-start(s32[3,4608]{1,0:T(4,128)} %pair_ref.1) | copy-start | bytes 165892
  35.3 29.2 %copy-start.3 = (f32[4608]{0:T(1024)S(1)}, f32[4608]{0:T(1024)}, u32[]{:S(2)}) copy-start(f32[4608]{0:T(1024)} %param.13) | copy-start | bytes 55300
  35.3 41.6 %collective-permute-start.7 = (bf16[8,2,144,128]{3,2,1,0:T(8,128)(2,1)}, bf16[8,2,144,128]{3,2,1,0:T(8,128)(2,1)}, u32[]{:S(2)}, u32[]{:S(2)}) collective-permute-start(bf16[8,2,144,128]{3,2,1,0:T(8,128)(2,1)} %get-tuple-element.31), channel_id=1, source_target_pairs={{0,1},{1,0},{2,3},{3,2},{4,5},{5,4},{6,7},{7,6},{8,9},{9,8},{10,11... | collective-permute-start | bytes 1769480 | tf_op jit(solution)/shard_map/ppermute | solution.py:710
  35.3 41.6 %collective-permute-start.8 = (bf16[8,2,144,128]{3,2,1,0:T(8,128)(2,1)S(1)}, bf16[8,2,144,128]{3,2,1,0:T(8,128)(2,1)}, u32[]{:S(2)}, u32[]{:S(2)}) collective-permute-start(bf16[8,2,144,128]{3,2,1,0:T(8,128)(2,1)S(1)} %get-tuple-element.32), channel_id=1, source_target_pairs={{1,2},{3,4},{5,6},{7,8},{9,10},{11,12},{13,14},{15,16},{17,18},{19... | collective-permute-start | bytes 1769480 | tf_op jit(solution)/shard_map/ppermute | solution.py:708
  37.4 13.1 %collective-permute-start.9 = (bf16[4,144,128]{2,1,0:T(8,128)(2,1)S(1)}, bf16[4,144,128]{2,1,0:T(8,128)(2,1)S(1)}, u32[]{:S(2)}, u32[]{:S(2)}) collective-permute-start(bf16[4,144,128]{2,1,0:T(8,128)(2,1)S(1)} %get-tuple-element.34), channel_id=1, source_target_pairs={{0,1},{1,0},{2,3},{3,2},{4,5},{5,4},{6,7},{7,6},{8,9},{9,8},{10,11... | collective-permute-start | bytes 442376 | tf_op jit(solution)/shard_map/ppermute | solution.py:711
  39.3 20.8 %all-to-all-start = ((f32[128,1,128]{2,1,0:T(1,128)}), f32[128,1,128]{2,1,0:T(1,128)S(1)}, u32[]{:S(2)}, u32[]{:S(2)}) async-start(f32[128,1,128]{2,1,0:T(1,128)} %bitcast.7), calls=%async_computation | async-start | bytes 131072 | tf_op jit(solution)/shard_map/all_to_all | solution.py:665
  60.1 15.5 %all-to-all-start.1 = ((bf16[128,8,128]{2,1,0:T(8,128)(2,1)}), bf16[128,8,128]{2,1,0:T(8,128)(2,1)S(1)}, u32[]{:S(2)}, u32[]{:S(2)}) async-start(bf16[128,8,128]{2,1,0:T(8,128)(2,1)} %bitcast.21), calls=%async_computation.1 | async-start | bytes 524288 | tf_op jit(solution)/shard_map/all_to_all | solution.py:732
  64.5 12.5 %copy-start.2 = (s32[24,256]{1,0:T(8,128)S(1)}, s32[24,256]{1,0:T(8,128)}, u32[]{:S(2)}) copy-start(s32[24,256]{1,0:T(8,128)} %wet_ref.4) | copy-start | bytes 73732

commit v8 on v7

--- a/solution.py
+++ b/solution.py
@@ -16,7 +16,7 @@
 
 LANES = 128
 ACCS = 3
-WAVE_LIMIT = 36
+WAVE_LIMIT = 42
 CHUNKS = 7
 UNROLL = 144
 BLOCK = 16
@@ -376,9 +376,7 @@
         )
         beside = jnp.dot(cells, narrow_pick, preferred_element_type=jnp.float32)
         for part in range(4):
-            beside_ref[row, part] = beside[:, part * LANES : (part + 1) * LANES].astype(
-                jnp.bfloat16
-            )
+            beside_ref[row, part] = beside[:, part * LANES : (part + 1) * LANES]
 
     loads[0].wait()
     loads[1].wait()
@@ -458,8 +456,8 @@
                 def side(at, cells, row=row, lanes=lanes):
                     return (speed_y + cur_ref[at + 1 + row : at + 2 + row, lanes]) * cells
 
-                left = side(40, beside_ref[at_row, half, spot, :].astype(jnp.float32))
-                right = side(48, beside_ref[at_row, 2 + half, spot, :].astype(jnp.float32))
+                left = side(40, beside_ref[at_row, half, spot, :])
+                right = side(48, beside_ref[at_row, 2 + half, spot, :])
                 wet = cur_ref[16 + row : 17 + row, lanes]
                 moved = value - jnp.abs(side(8, old))
                 result = wet * (moved + jnp.maximum(left, 0.0) - jnp.minimum(right, 0.0))
@@ -573,7 +571,7 @@
             VMEM((bins * 8, LANES), f32),
             VMEM((56, columns), f32),
             VMEM((8 * PITCH, LANES), f32),
-            VMEM((rows, 4, bins, LANES), jnp.bfloat16),
+            VMEM((rows, 4, bins, LANES), f32),
             pltpu.SemaphoreType.DMA((5,)),
             pltpu.SemaphoreType.DMA((18,)),
         ]

time: 96.1 us -> 95.9 us (level)
  no operation moved by 1% of the time
where the time goes in v8:
time: 95.9 us; the launch traced here: 95.6 us
  waiting for transfers between devices  33.2 us (35%)
  Pallas kernels  32.5 us (34%)
  starting transfers between devices  29.1 us (30%)
    pallas_call x8, Pallas kernels, call(): pl.pallas_call(body, out_shape=out_shape, in_specs=ins, out_specs=outs, s...  32.5 us
    ppermute x7, waiting for transfers between devices, per_device(): pieces[turn] = lax.ppermute(sent[turn], 'bins', partners)  18.8 us
    ppermute x7, starting transfers between devices, per_device(): pieces[turn] = lax.ppermute(sent[turn], 'bins', partners)  11.5 us
    all_to_all x1, starting transfers between devices, per_device(): lax.all_to_all(surface, both, split_axis=0, concat_axis=0, tiled=True)  11.1 us
    all_to_all x1, waiting for transfers between devices, per_device(): lax.all_to_all(routed.reshape(devices, 8, LANES), both, split_axis=0, con...  7.36 us
    all_to_all x1, waiting for transfers between devices, per_device(): lax.all_to_all(surface, both, split_axis=0, concat_axis=0, tiled=True)  6.98 us
    all_to_all x1, starting transfers between devices, per_device(): lax.all_to_all(routed.reshape(devices, 8, LANES), both, split_axis=0, con...  4.38 us
    ppermute x1, starting transfers between devices, per_device(): outer = lax.ppermute(outer, both, outward)  2.04 us
  transfers between devices with their start and end apart: 12, of which 5 were waited for; matrix products, arithmetic and copies ran while one was open for 0% of the time, Pallas kernels for 10%

profile of v8, /device:TPU:1, one launch (start us, length us, event | category | flops | bytes accessed | tf_op | source)
XLA Modules:
  0.0 95.6 jit_solution(3903381701163190962)
XLA Ops:
  0.6 0.1 pad_add_fusion.ids_ref
  0.7 0.0 copy-start
  0.7 0.0 copy-start.4
  0.7 0.0 copy-start.5
  0.7 0.0 copy-start.6
  0.7 3.4 %shard_map.107 = (bf16[7,144,128]{2,1,0:T(8,128)(2,1)S(1)}, bf16[6,144,128]{2,1,0:T(8,128)(2,1)}, bf16[7,144,128]{2,1,0:T(8,128)(2,1)}, bf16[6,144,128]{2,1,0:T(...) custom-call(s32[4]{0:T(128)S(1)} %pad_add_fusion.ids_ref, ...), custom_call_target="tpu_custom_call" | custom-call | flops 2000000 | bytes 4000000 | tf_op jit(solution)/shard_map/pallas_call | solution.py:53
  4.1 1.5 %collective-permute-start = (bf16[6,144,128]{2,1,0:T(8,128)(2,1)}, bf16[6,144,128]{2,1,0:T(8,128)(2,1)S(1)}, u32[]{:S(2)}, u32[]{:S(2)}) collective-permute-start(bf16[6,144,128]{2,1,0:T(8,128)(2,1)} %get-tuple-element.24), channel_id=1, source_target_pairs={{0,1},{1,0},{2,3},{3,2},{4,5},{5,4},{6,7},{7,6},{8,9},{9,8},{10,11... | collective-permute-start | bytes 663560 | tf_op jit(solution)/shard_map/ppermute | solution.py:651
  5.6 1.4 %collective-permute-start.2 = (bf16[6,144,128]{2,1,0:T(8,128)(2,1)}, bf16[6,144,128]{2,1,0:T(8,128)(2,1)S(1)}, u32[]{:S(2)}, u32[]{:S(2)}) collective-permute-start(bf16[6,144,128]{2,1,0:T(8,128)(2,1)} %get-tuple-element.26), channel_id=1, source_target_pairs={{0,3},{1,2},{2,1},{3,0},{4,7},{5,6},{6,5},{7,4},{8,11},{9,10},{10,... | collective-permute-start | bytes 663560 | tf_op jit(solution)/shard_map/ppermute | solution.py:651
  6.9 0.1 collective-permute-start.1
  7.0 3.0 %collective-permute-start.3 = (bf16[7,144,128]{2,1,0:T(8,128)(2,1)}, bf16[7,144,128]{2,1,0:T(8,128)(2,1)S(1)}, u32[]{:S(2)}, u32[]{:S(2)}) collective-permute-start(bf16[7,144,128]{2,1,0:T(8,128)(2,1)} %get-tuple-element.27), channel_id=1, source_target_pairs={{0,4},{1,5},{2,6},{3,7},{4,0},{5,1},{6,2},{7,3},{8,12},{9,13},{10,... | collective-permute-start | bytes 774152 | tf_op jit(solution)/shard_map/ppermute | solution.py:651
  10.0 0.8 collective-permute-start.5
  10.8 0.0 collective-permute-done.refs_1_
  10.8 2.6 %collective-permute-start.4 = (bf16[6,144,128]{2,1,0:T(8,128)(2,1)}, bf16[6,144,128]{2,1,0:T(8,128)(2,1)S(1)}, u32[]{:S(2)}, u32[]{:S(2)}) collective-permute-start(bf16[6,144,128]{2,1,0:T(8,128)(2,1)} %get-tuple-element.28), channel_id=1, source_target_pairs={{0,5},{1,4},{2,7},{3,6},{4,1},{5,0},{6,3},{7,2},{8,13},{9,12},{10,... | collective-permute-start | bytes 663560 | tf_op jit(solution)/shard_map/ppermute | solution.py:651
  13.4 0.1 collective-permute-done.2.refs_3_
  13.5 2.2 %collective-permute-start.6 = (bf16[6,144,128]{2,1,0:T(8,128)(2,1)}, bf16[6,144,128]{2,1,0:T(8,128)(2,1)S(1)}, u32[]{:S(2)}, u32[]{:S(2)}) collective-permute-start(bf16[6,144,128]{2,1,0:T(8,128)(2,1)} %get-tuple-element.30), channel_id=1, source_target_pairs={{0,7},{1,6},{2,5},{3,4},{4,3},{5,2},{6,1},{7,0},{8,15},{9,14},{10,... | collective-permute-start | bytes 663560 | tf_op jit(solution)/shard_map/ppermute | solution.py:651
  15.7 15.6 %collective-permute-done.4.refs_5_ = bf16[6,144,128]{2,1,0:T(8,128)(2,1)S(1)} collective-permute-done((bf16[6,144,128]{2,1,0:T(8,128)(2,1)}, bf16[6,144,128]{2,1,0:T(8,128)(2,1)S(1)}, u32[]{:S(2)}, u32[]{:S(2)}) %collective-permute-start.4) | collective-permute-done | bytes 221216 | tf_op jit(solution)/shard_map/ppermute | solution.py:651
  31.4 3.0 %collective-permute-done.6.refs_7_ = bf16[6,144,128]{2,1,0:T(8,128)(2,1)S(1)} collective-permute-done((bf16[6,144,128]{2,1,0:T(8,128)(2,1)}, bf16[6,144,128]{2,1,0:T(8,128)(2,1)S(1)}, u32[]{:S(2)}, u32[]{:S(2)}) %collective-permute-start.6) | collective-permute-done | bytes 221216 | tf_op jit(solution)/shard_map/ppermute | solution.py:651
  34.4 0.0 collective-permute-done.1.refs_2_
  34.4 0.0 collective-permute-done.3.refs_4_
  34.4 0.0 collective-permute-done.5.refs_6_
  34.4 0.9 shard_map.108
  35.3 0.0 copy-start.1
  35.3 0.0 copy-start.3
  35.3 0.0 collective-permute-start.7
  35.3 2.0 %collective-permute-start.8 = (bf16[8,2,144,128]{3,2,1,0:T(8,128)(2,1)S(1)}, bf16[8,2,144,128]{3,2,1,0:T(8,128)(2,1)}, u32[]{:S(2)}, u32[]{:S(2)}) collective-permute-start(bf16[8,2,144,128]{3,2,1,0:T(8,128)(2,1)S(1)} %get-tuple-element.32), channel_id=1, source_target_pairs={{1,2},{3,4},{5,6},{7,8},{9,10},{11,12},{13,14},{15,16},{17,18},{19... | collective-permute-start | bytes 1769480 | tf_op jit(solution)/shard_map/ppermute | solution.py:706
  37.4 0.1 collective-permute-start.9
  37.5 0.0 copy-done
  37.5 0.0 copy-done.4
  37.5 0.0 copy-done.5
  37.5 1.8 %shard_map.105 = f32[128,128]{1,0:T(8,128)} custom-call(s32[4]{0:T(128)S(1)} %pad_add_fusion.ids_ref, f32[2,384,128]{2,1,0:T(8,128)S(1)} %copy-done, s32[2,384]{1,0:T(2,128)S(1)} %copy-done.4, f32[2,144]{1,0:T(2,128)S(1)} %copy-done.5), custom_call_target="tpu_custom_call" | custom-call | flops 4000000 | bytes 500000 | tf_op jit(solution)/shard_map/pallas_call | solution.py:53
  39.3 11.1 %all-to-all-start = ((f32[128,1,128]{2,1,0:T(1,128)}), f32[128,1,128]{2,1,0:T(1,128)S(1)}, u32[]{:S(2)}, u32[]{:S(2)}) async-start(f32[128,1,128]{2,1,0:T(1,128)} %bitcast.7), calls=%async_computation | async-start | bytes 131072 | tf_op jit(solution)/shard_map/all_to_all | solution.py:663
  50.4 0.0 collective-permute-done.9.other_ref
  50.5 0.0 copy-done.6
  50.5 2.6 %shard_map.109 = (bf16[1024,128]{1,0:T(8,128)(2,1)}, f32[16,256]{1,0:T(8,128)S(1)}, bf16[32,1152]{1,0:T(8,128)(2,1)S(1)}) custom-call(s32[4]{0:T(128)S(1)} %pad_add_fusion.ids_ref, s32[1,128]{1,0:T(1,128)S(1)} %bitcast.18, bf16[4,144,128]{2,1,0:T(8,128)(2,1)S(1)} %collective-permute-done.9.other_ref, bf16[7,144,128]{2,1,0:T(8,128)(2,1)S(1)} %get-tuple-element.23.refs_0_, ...), custom_call_target="tpu_custom_call" | custom-call | flops 300000000 | bytes 2500000 | tf_op jit(solution)/shard_map/pallas_call | solution.py:53
  53.1 7.0 %all-to-all-done = f32[128,1,128]{2,1,0:T(1,128)S(1)} async-done(((f32[128,1,128]{2,1,0:T(1,128)}), f32[128,1,128]{2,1,0:T(1,128)S(1)}, u32[]{:S(2)}, u32[]{:S(2)}) %all-to-all-start) | async-done | bytes 65568 | tf_op jit(solution)/shard_map/all_to_all | solution.py:663
  60.1 4.4 %all-to-all-start.1 = ((bf16[128,8,128]{2,1,0:T(8,128)(2,1)}), bf16[128,8,128]{2,1,0:T(8,128)(2,1)S(1)}, u32[]{:S(2)}, u32[]{:S(2)}) async-start(bf16[128,8,128]{2,1,0:T(8,128)(2,1)} %bitcast.21), calls=%async_computation.1 | async-start | bytes 524288 | tf_op jit(solution)/shard_map/all_to_all | solution.py:730
  64.5 0.0 copy-start.2
  64.5 0.0 copy-done.1
  64.5 0.0 copy-done.3
  64.5 1.7 %shard_map.104 = (f32[4608,128]{1,0:T(8,128)}, s32[108,128]{1,0:T(8,128)S(1)}) custom-call(f32[36,128]{1,0:T(8,128)S(1)} %bitcast.17, s32[3,4608]{1,0:T(4,128)S(1)} %copy-done.1), custom_call_target="tpu_custom_call" | custom-call | flops 1000000 | bytes 2500000 | tf_op jit(solution)/shard_map/pallas_call | solution.py:53
  66.2 2.0 %shard_map.106 = (f32[32,256]{1,0:T(8,128)S(1)}, f32[2,1152,128]{2,1,0:T(8,128)}) custom-call(f32[128,128]{1,0:T(8,128)S(1)} %bitcast.15, s32[1,128]{1,0:T(1,128)S(1)} %bitcast.19), custom_call_target="tpu_custom_call" | custom-call | flops 600000000 | bytes 1300000 | tf_op jit(solution)/shard_map/pallas_call | solution.py:53
  68.2 7.4 %all-to-all-done.1 = bf16[128,8,128]{2,1,0:T(8,128)(2,1)S(1)} async-done(((bf16[128,8,128]{2,1,0:T(8,128)(2,1)}), bf16[128,8,128]{2,1,0:T(8,128)(2,1)S(1)}, u32[]{:S(2)}, u32[]{:S(2)}) %all-to-all-start.1) | async-done | bytes 262176 | tf_op jit(solution)/shard_map/all_to_all | solution.py:730
  75.6 1.4 %shard_map.111 = f32[2,384,128]{2,1,0:T(8,128)} custom-call(f32[2,384,128]{2,1,0:T(8,128)S(1)} %copy-done, bf16[1024,128]{1,0:T(8,128)(2,1)S(1)} %bitcast.14, s32[2,384]{1,0:T(2,128)S(1)} %copy-done.4), custom_call_target="tpu_custom_call" | custom-call | flops 4000000 | bytes 1500000 | tf_op jit(solution)/shard_map/pallas_call | solution.py:53
  77.0 0.0 collective-permute-done.7.inner_hbm
  77.0 0.0 collective-permute-done.8.outer_hbm
  77.0 0.0 copy-done.2
  77.0 18.7 %shard_map.110 = bf16[3,1152,256]{2,1,0:T(8,128)(2,1)} custom-call(s32[4]{0:T(128)S(1)} %pad_add_fusion.ids_ref, s32[13824]{0:T(1024)S(1)} %bitcast.16, f32[4608,128]{1,0:T(8,128)} %get-tuple-element.21.coef_hbm, f32[2,1152,128]{2,1,0:T(8,128)} %get-tuple-element.22.speeds_hbm, bf16[8,2,144,128]{3,2,1,0:T(8,128)(2,1)} %collective-permute-done.7.inner_hbm, ...), custom_call_target="tpu_custom_call" | custom-call | flops 40000000 | bytes 8000000 | tf_op jit(solution)/shard_map/pallas_call | solution.py:53
Async XLA Ops:
  0.7 36.8 %copy-start = (f32[2,384,128]{2,1,0:T(8,128)S(1)}, f32[2,384,128]{2,1,0:T(8,128)}, u32[]{:S(2)}) copy-start(f32[2,384,128]{2,1,0:T(8,128)} %currents_ref.3) | copy-start | bytes 1179652
  0.7 36.8 %copy-start.4 = (s32[2,384]{1,0:T(2,128)S(1)}, s32[2,384]{1,0:T(2,128)}, u32[]{:S(2)}) copy-start(s32[2,384]{1,0:T(2,128)} %wet_ref.5) | copy-start | bytes 9220
  0.7 36.8 %copy-start.5 = (f32[2,144]{1,0:T(2,128)S(1)}, f32[2,144]{1,0:T(2,128)}, u32[]{:S(2)}) copy-start(f32[2,144]{1,0:T(2,128)} %speed_ref.1) | copy-start | bytes 3460
  0.7 49.7 %copy-start.6 = (s32[128]{0:T(128)S(1)}, s32[128]{0:T(128)}, u32[]{:S(2)}) copy-start(s32[128]{0:T(128)} %param.15) | copy-start | bytes 1540
  4.1 6.7 %collective-permute-start = (bf16[6,144,128]{2,1,0:T(8,128)(2,1)}, bf16[6,144,128]{2,1,0:T(8,128)(2,1)S(1)}, u32[]{:S(2)}, u32[]{:S(2)}) collective-permute-start(bf16[6,144,128]{2,1,0:T(8,128)(2,1)} %get-tuple-element.24), channel_id=1, source_target_pairs={{0,1},{1,0},{2,3},{3,2},{4,5},{5,4},{6,7},{7,6},{8,9},{9,8},{10,11... | collective-permute-start | bytes 663560 | tf_op jit(solution)/shard_map/ppermute | solution.py:651
  5.6 7.9 %collective-permute-start.2 = (bf16[6,144,128]{2,1,0:T(8,128)(2,1)}, bf16[6,144,128]{2,1,0:T(8,128)(2,1)S(1)}, u32[]{:S(2)}, u32[]{:S(2)}) collective-permute-start(bf16[6,144,128]{2,1,0:T(8,128)(2,1)} %get-tuple-element.26), channel_id=1, source_target_pairs={{0,3},{1,2},{2,1},{3,0},{4,7},{5,6},{6,5},{7,4},{8,11},{9,10},{10,... | collective-permute-start | bytes 663560 | tf_op jit(solution)/shard_map/ppermute | solution.py:651
  6.9 27.5 %collective-permute-start.1 = (bf16[7,144,128]{2,1,0:T(8,128)(2,1)}, bf16[7,144,128]{2,1,0:T(8,128)(2,1)S(1)}, u32[]{:S(2)}, u32[]{:S(2)}) collective-permute-start(bf16[7,144,128]{2,1,0:T(8,128)(2,1)} %get-tuple-element.25), channel_id=1, source_target_pairs={{0,2},{1,3},{2,0},{3,1},{4,6},{5,7},{6,4},{7,5},{8,10},{9,11},{10,... | collective-permute-start | bytes 774152 | tf_op jit(solution)/shard_map/ppermute | solution.py:651
  7.0 27.4 %collective-permute-start.3 = (bf16[7,144,128]{2,1,0:T(8,128)(2,1)}, bf16[7,144,128]{2,1,0:T(8,128)(2,1)S(1)}, u32[]{:S(2)}, u32[]{:S(2)}) collective-permute-start(bf16[7,144,128]{2,1,0:T(8,128)(2,1)} %get-tuple-element.27), channel_id=1, source_target_pairs={{0,4},{1,5},{2,6},{3,7},{4,0},{5,1},{6,2},{7,3},{8,12},{9,13},{10,... | collective-permute-start | bytes 774152 | tf_op jit(solution)/shard_map/ppermute | solution.py:651
  10.0 24.4 %collective-permute-start.5 = (bf16[7,144,128]{2,1,0:T(8,128)(2,1)}, bf16[7,144,128]{2,1,0:T(8,128)(2,1)S(1)}, u32[]{:S(2)}, u32[]{:S(2)}) collective-permute-start(bf16[7,144,128]{2,1,0:T(8,128)(2,1)} %get-tuple-element.29), channel_id=1, source_target_pairs={{0,6},{1,7},{2,4},{3,5},{4,2},{5,3},{6,0},{7,1},{8,14},{9,15},{10,... | collective-permute-start | bytes 774152 | tf_op jit(solution)/shard_map/ppermute | solution.py:651
  10.8 20.6 %collective-permute-start.4 = (bf16[6,144,128]{2,1,0:T(8,128)(2,1)}, bf16[6,144,128]{2,1,0:T(8,128)(2,1)S(1)}, u32[]{:S(2)}, u32[]{:S(2)}) collective-permute-start(bf16[6,144,128]{2,1,0:T(8,128)(2,1)} %get-tuple-element.28), channel_id=1, source_target_pairs={{0,5},{1,4},{2,7},{3,6},{4,1},{5,0},{6,3},{7,2},{8,13},{9,12},{10,... | collective-permute-start | bytes 663560 | tf_op jit(solution)/shard_map/ppermute | solution.py:651
  13.5 20.9 %collective-permute-start.6 = (bf16[6,144,128]{2,1,0:T(8,128)(2,1)}, bf16[6,144,128]{2,1,0:T(8,128)(2,1)S(1)}, u32[]{:S(2)}, u32[]{:S(2)}) collective-permute-start(bf16[6,144,128]{2,1,0:T(8,128)(2,1)} %get-tuple-element.30), channel_id=1, source_target_pairs={{0,7},{1,6},{2,5},{3,4},{4,3},{5,2},{6,1},{7,0},{8,15},{9,14},{10,... | collective-permute-start | bytes 663560 | tf_op jit(solution)/shard_map/ppermute | solution.py:651
  35.3 29.2 %copy-start.1 = (s32[3,4608]{1,0:T(4,128)S(1)}, s32[3,4608]{1,0:T(4,128)}, u32[]{:S(2)}) copy-start(s32[3,4608]{1,0:T(4,128)} %pair_ref.1) | copy-start | bytes 165892
  35.3 29.2 %copy-start.3 = (f32[4608]{0:T(1024)S(1)}, f32[4608]{0:T(1024)}, u32[]{:S(2)}) copy-start(f32[4608]{0:T(1024)} %param.13) | copy-start | bytes 55300
  35.3 41.6 %collective-permute-start.7 = (bf16[8,2,144,128]{3,2,1,0:T(8,128)(2,1)}, bf16[8,2,144,128]{3,2,1,0:T(8,128)(2,1)}, u32[]{:S(2)}, u32[]{:S(2)}) collective-permute-start(bf16[8,2,144,128]{3,2,1,0:T(8,128)(2,1)} %get-tuple-element.31), channel_id=1, source_target_pairs={{0,1},{1,0},{2,3},{3,2},{4,5},{5,4},{6,7},{7,6},{8,9},{9,8},{10,11... | collective-permute-start | bytes 1769480 | tf_op jit(solution)/shard_map/ppermute | solution.py:708
  35.3 41.6 %collective-permute-start.8 = (bf16[8,2,144,128]{3,2,1,0:T(8,128)(2,1)S(1)}, bf16[8,2,144,128]{3,2,1,0:T(8,128)(2,1)}, u32[]{:S(2)}, u32[]{:S(2)}) collective-permute-start(bf16[8,2,144,128]{3,2,1,0:T(8,128)(2,1)S(1)} %get-tuple-element.32), channel_id=1, source_target_pairs={{1,2},{3,4},{5,6},{7,8},{9,10},{11,12},{13,14},{15,16},{17,18},{19... | collective-permute-start | bytes 1769480 | tf_op jit(solution)/shard_map/ppermute | solution.py:706
  37.4 13.1 %collective-permute-start.9 = (bf16[4,144,128]{2,1,0:T(8,128)(2,1)S(1)}, bf16[4,144,128]{2,1,0:T(8,128)(2,1)S(1)}, u32[]{:S(2)}, u32[]{:S(2)}) collective-permute-start(bf16[4,144,128]{2,1,0:T(8,128)(2,1)S(1)} %get-tuple-element.34), channel_id=1, source_target_pairs={{0,1},{1,0},{2,3},{3,2},{4,5},{5,4},{6,7},{7,6},{8,9},{9,8},{10,11... | collective-permute-start | bytes 442376 | tf_op jit(solution)/shard_map/ppermute | solution.py:709
  39.3 20.8 %all-to-all-start = ((f32[128,1,128]{2,1,0:T(1,128)}), f32[128,1,128]{2,1,0:T(1,128)S(1)}, u32[]{:S(2)}, u32[]{:S(2)}) async-start(f32[128,1,128]{2,1,0:T(1,128)} %bitcast.7), calls=%async_computation | async-start | bytes 131072 | tf_op jit(solution)/shard_map/all_to_all | solution.py:663
  60.1 15.5 %all-to-all-start.1 = ((bf16[128,8,128]{2,1,0:T(8,128)(2,1)}), bf16[128,8,128]{2,1,0:T(8,128)(2,1)S(1)}, u32[]{:S(2)}, u32[]{:S(2)}) async-start(bf16[128,8,128]{2,1,0:T(8,128)(2,1)} %bitcast.21), calls=%async_computation.1 | async-start | bytes 524288 | tf_op jit(solution)/shard_map/all_to_all | solution.py:730
  64.5 12.5 %copy-start.2 = (s32[24,256]{1,0:T(8,128)S(1)}, s32[24,256]{1,0:T(8,128)}, u32[]{:S(2)}) copy-start(s32[24,256]{1,0:T(8,128)} %wet_ref.4) | copy-start | bytes 73732

commit v9 on v8

--- a/solution.py
+++ b/solution.py
@@ -238,14 +238,13 @@
     own = ((index >= first) & (index < first + 9)).astype(jnp.float32).astype(bf16)
     rows = [jnp.dot(own, part, preferred_element_type=jnp.float32) for part in parts]
     place = index - ((index * 7282) >> 16) * 9
-    ones = jnp.ones((LANES, LANES), bf16)
+    ones = jnp.ones((3 * LANES, LANES), bf16)
     for part in range(2):
         mine = lane == place + (SPEED_LANE + 9 * part)
-        total = jnp.zeros((bins, LANES), jnp.float32)
-        for value in rows:
-            kept = jnp.where(mine, value, 0.0).astype(bf16)
-            total = total + jnp.dot(kept, ones, preferred_element_type=jnp.float32)
-        speeds_ref[part] = total
+        kept = [jnp.where(mine, value, 0.0).astype(bf16) for value in rows]
+        speeds_ref[part] = jnp.dot(
+            jnp.concatenate(kept, axis=1), ones, preferred_element_type=jnp.float32
+        )
         copies.append(
             pltpu.make_async_copy(speeds_ref.at[part], speeds_hbm.at[part], sems.at[part])
         )
@@ -513,7 +512,7 @@
                 )
         return carry
 
-    parts = 6
+    parts = 9
     out_copies = []
     for part in range(parts):
         span = pl.ds(part * (bins // parts), bins // parts)
@@ -573,7 +572,7 @@
             VMEM((8 * PITCH, LANES), f32),
             VMEM((rows, 4, bins, LANES), f32),
             pltpu.SemaphoreType.DMA((5,)),
-            pltpu.SemaphoreType.DMA((18,)),
+            pltpu.SemaphoreType.DMA((27,)),
         ]
         + [VMEM((bins * 8, LANES), f32)] * ACCS,
         40_000_000,

time: 95.9 us -> 95.9 us (level)
  no operation moved by 1% of the time
where the time goes in v9:
time: 95.9 us; the launch traced here: 95.7 us
  waiting for transfers between devices  33.4 us (35%)
  Pallas kernels  32.3 us (34%)
  starting transfers between devices  29.1 us (30%)
    pallas_call x8, Pallas kernels, call(): pl.pallas_call(body, out_shape=out_shape, in_specs=ins, out_specs=outs, s...  32.3 us
    ppermute x7, waiting for transfers between devices, per_device(): pieces[turn] = lax.ppermute(sent[turn], 'bins', partners)  18.8 us
    ppermute x7, starting transfers between devices, per_device(): pieces[turn] = lax.ppermute(sent[turn], 'bins', partners)  11.5 us
    all_to_all x1, starting transfers between devices, per_device(): lax.all_to_all(surface, both, split_axis=0, concat_axis=0, tiled=True)  11.1 us
    all_to_all x1, waiting for transfers between devices, per_device(): lax.all_to_all(routed.reshape(devices, 8, LANES), both, split_axis=0, con...  7.54 us
    all_to_all x1, waiting for transfers between devices, per_device(): lax.all_to_all(surface, both, split_axis=0, concat_axis=0, tiled=True)  6.98 us
    all_to_all x1, starting transfers between devices, per_device(): lax.all_to_all(routed.reshape(devices, 8, LANES), both, split_axis=0, con...  4.38 us
    ppermute x1, starting transfers between devices, per_device(): outer = lax.ppermute(outer, both, outward)  2.04 us
  transfers between devices with their start and end apart: 12, of which 5 were waited for; matrix products, arithmetic and copies ran while one was open for 0% of the time, Pallas kernels for 10%

profile of v9, /device:TPU:1, one launch (start us, length us, event | category | flops | bytes accessed | tf_op | source)
XLA Modules:
  0.0 95.7 jit_solution(14637883936119870771)
XLA Ops:
  0.6 0.1 pad_add_fusion.ids_ref
  0.7 0.0 copy-start
  0.7 0.0 copy-start.4
  0.7 0.0 copy-start.5
  0.7 0.0 copy-start.6
  0.7 3.4 %shard_map.107 = (bf16[7,144,128]{2,1,0:T(8,128)(2,1)S(1)}, bf16[6,144,128]{2,1,0:T(8,128)(2,1)}, bf16[7,144,128]{2,1,0:T(8,128)(2,1)}, bf16[6,144,128]{2,1,0:T(...) custom-call(s32[4]{0:T(128)S(1)} %pad_add_fusion.ids_ref, ...), custom_call_target="tpu_custom_call" | custom-call | flops 2000000 | bytes 4000000 | tf_op jit(solution)/shard_map/pallas_call | solution.py:53
  4.1 1.5 %collective-permute-start = (bf16[6,144,128]{2,1,0:T(8,128)(2,1)}, bf16[6,144,128]{2,1,0:T(8,128)(2,1)S(1)}, u32[]{:S(2)}, u32[]{:S(2)}) collective-permute-start(bf16[6,144,128]{2,1,0:T(8,128)(2,1)} %get-tuple-element.24), channel_id=1, source_target_pairs={{0,1},{1,0},{2,3},{3,2},{4,5},{5,4},{6,7},{7,6},{8,9},{9,8},{10,11... | collective-permute-start | bytes 663560 | tf_op jit(solution)/shard_map/ppermute | solution.py:650
  5.6 1.4 %collective-permute-start.2 = (bf16[6,144,128]{2,1,0:T(8,128)(2,1)}, bf16[6,144,128]{2,1,0:T(8,128)(2,1)S(1)}, u32[]{:S(2)}, u32[]{:S(2)}) collective-permute-start(bf16[6,144,128]{2,1,0:T(8,128)(2,1)} %get-tuple-element.26), channel_id=1, source_target_pairs={{0,3},{1,2},{2,1},{3,0},{4,7},{5,6},{6,5},{7,4},{8,11},{9,10},{10,... | collective-permute-start | bytes 663560 | tf_op jit(solution)/shard_map/ppermute | solution.py:650
  6.9 0.1 collective-permute-start.1
  7.0 3.0 %collective-permute-start.3 = (bf16[7,144,128]{2,1,0:T(8,128)(2,1)}, bf16[7,144,128]{2,1,0:T(8,128)(2,1)S(1)}, u32[]{:S(2)}, u32[]{:S(2)}) collective-permute-start(bf16[7,144,128]{2,1,0:T(8,128)(2,1)} %get-tuple-element.27), channel_id=1, source_target_pairs={{0,4},{1,5},{2,6},{3,7},{4,0},{5,1},{6,2},{7,3},{8,12},{9,13},{10,... | collective-permute-start | bytes 774152 | tf_op jit(solution)/shard_map/ppermute | solution.py:650
  10.0 0.8 collective-permute-start.5
  10.8 0.0 collective-permute-done.refs_1_
  10.8 2.6 %collective-permute-start.4 = (bf16[6,144,128]{2,1,0:T(8,128)(2,1)}, bf16[6,144,128]{2,1,0:T(8,128)(2,1)S(1)}, u32[]{:S(2)}, u32[]{:S(2)}) collective-permute-start(bf16[6,144,128]{2,1,0:T(8,128)(2,1)} %get-tuple-element.28), channel_id=1, source_target_pairs={{0,5},{1,4},{2,7},{3,6},{4,1},{5,0},{6,3},{7,2},{8,13},{9,12},{10,... | collective-permute-start | bytes 663560 | tf_op jit(solution)/shard_map/ppermute | solution.py:650
  13.4 0.1 collective-permute-done.2.refs_3_
  13.5 2.2 %collective-permute-start.6 = (bf16[6,144,128]{2,1,0:T(8,128)(2,1)}, bf16[6,144,128]{2,1,0:T(8,128)(2,1)S(1)}, u32[]{:S(2)}, u32[]{:S(2)}) collective-permute-start(bf16[6,144,128]{2,1,0:T(8,128)(2,1)} %get-tuple-element.30), channel_id=1, source_target_pairs={{0,7},{1,6},{2,5},{3,4},{4,3},{5,2},{6,1},{7,0},{8,15},{9,14},{10,... | collective-permute-start | bytes 663560 | tf_op jit(solution)/shard_map/ppermute | solution.py:650
  15.7 15.6 %collective-permute-done.4.refs_5_ = bf16[6,144,128]{2,1,0:T(8,128)(2,1)S(1)} collective-permute-done((bf16[6,144,128]{2,1,0:T(8,128)(2,1)}, bf16[6,144,128]{2,1,0:T(8,128)(2,1)S(1)}, u32[]{:S(2)}, u32[]{:S(2)}) %collective-permute-start.4) | collective-permute-done | bytes 221216 | tf_op jit(solution)/shard_map/ppermute | solution.py:650
  31.4 3.0 %collective-permute-done.6.refs_7_ = bf16[6,144,128]{2,1,0:T(8,128)(2,1)S(1)} collective-permute-done((bf16[6,144,128]{2,1,0:T(8,128)(2,1)}, bf16[6,144,128]{2,1,0:T(8,128)(2,1)S(1)}, u32[]{:S(2)}, u32[]{:S(2)}) %collective-permute-start.6) | collective-permute-done | bytes 221216 | tf_op jit(solution)/shard_map/ppermute | solution.py:650
  34.4 0.0 collective-permute-done.1.refs_2_
  34.4 0.0 collective-permute-done.3.refs_4_
  34.4 0.0 collective-permute-done.5.refs_6_
  34.4 0.9 shard_map.108
  35.3 0.0 copy-start.1
  35.3 0.0 copy-start.3
  35.3 0.0 collective-permute-start.7
  35.3 2.0 %collective-permute-start.8 = (bf16[8,2,144,128]{3,2,1,0:T(8,128)(2,1)S(1)}, bf16[8,2,144,128]{3,2,1,0:T(8,128)(2,1)}, u32[]{:S(2)}, u32[]{:S(2)}) collective-permute-start(bf16[8,2,144,128]{3,2,1,0:T(8,128)(2,1)S(1)} %get-tuple-element.32), channel_id=1, source_target_pairs={{1,2},{3,4},{5,6},{7,8},{9,10},{11,12},{13,14},{15,16},{17,18},{19... | collective-permute-start | bytes 1769480 | tf_op jit(solution)/shard_map/ppermute | solution.py:705
  37.4 0.1 collective-permute-start.9
  37.5 0.0 copy-done
  37.5 0.0 copy-done.4
  37.5 0.0 copy-done.5
  37.5 1.8 %shard_map.105 = f32[128,128]{1,0:T(8,128)} custom-call(s32[4]{0:T(128)S(1)} %pad_add_fusion.ids_ref, f32[2,384,128]{2,1,0:T(8,128)S(1)} %copy-done, s32[2,384]{1,0:T(2,128)S(1)} %copy-done.4, f32[2,144]{1,0:T(2,128)S(1)} %copy-done.5), custom_call_target="tpu_custom_call" | custom-call | flops 4000000 | bytes 500000 | tf_op jit(solution)/shard_map/pallas_call | solution.py:53
  39.3 11.1 %all-to-all-start = ((f32[128,1,128]{2,1,0:T(1,128)}), f32[128,1,128]{2,1,0:T(1,128)S(1)}, u32[]{:S(2)}, u32[]{:S(2)}) async-start(f32[128,1,128]{2,1,0:T(1,128)} %bitcast.7), calls=%async_computation | async-start | bytes 131072 | tf_op jit(solution)/shard_map/all_to_all | solution.py:662
  50.4 0.0 collective-permute-done.9.other_ref
  50.5 0.0 copy-done.6
  50.5 2.6 %shard_map.109 = (bf16[1024,128]{1,0:T(8,128)(2,1)}, f32[16,256]{1,0:T(8,128)S(1)}, bf16[32,1152]{1,0:T(8,128)(2,1)S(1)}) custom-call(s32[4]{0:T(128)S(1)} %pad_add_fusion.ids_ref, s32[1,128]{1,0:T(1,128)S(1)} %bitcast.18, bf16[4,144,128]{2,1,0:T(8,128)(2,1)S(1)} %collective-permute-done.9.other_ref, bf16[7,144,128]{2,1,0:T(8,128)(2,1)S(1)} %get-tuple-element.23.refs_0_, ...), custom_call_target="tpu_custom_call" | custom-call | flops 300000000 | bytes 2500000 | tf_op jit(solution)/shard_map/pallas_call | solution.py:53
  53.1 7.0 %all-to-all-done = f32[128,1,128]{2,1,0:T(1,128)S(1)} async-done(((f32[128,1,128]{2,1,0:T(1,128)}), f32[128,1,128]{2,1,0:T(1,128)S(1)}, u32[]{:S(2)}, u32[]{:S(2)}) %all-to-all-start) | async-done | bytes 65568 | tf_op jit(solution)/shard_map/all_to_all | solution.py:662
  60.1 4.4 %all-to-all-start.1 = ((bf16[128,8,128]{2,1,0:T(8,128)(2,1)}), bf16[128,8,128]{2,1,0:T(8,128)(2,1)S(1)}, u32[]{:S(2)}, u32[]{:S(2)}) async-start(bf16[128,8,128]{2,1,0:T(8,128)(2,1)} %bitcast.21), calls=%async_computation.1 | async-start | bytes 524288 | tf_op jit(solution)/shard_map/all_to_all | solution.py:729
  64.5 0.0 copy-start.2
  64.5 0.0 copy-done.1
  64.5 0.0 copy-done.3
  64.5 1.7 %shard_map.104 = (f32[4608,128]{1,0:T(8,128)}, s32[108,128]{1,0:T(8,128)S(1)}) custom-call(f32[36,128]{1,0:T(8,128)S(1)} %bitcast.17, s32[3,4608]{1,0:T(4,128)S(1)} %copy-done.1), custom_call_target="tpu_custom_call" | custom-call | flops 1000000 | bytes 2500000 | tf_op jit(solution)/shard_map/pallas_call | solution.py:53
  66.2 1.8 %shard_map.106 = (f32[32,256]{1,0:T(8,128)S(1)}, f32[2,1152,128]{2,1,0:T(8,128)}) custom-call(f32[128,128]{1,0:T(8,128)S(1)} %bitcast.15, s32[1,128]{1,0:T(1,128)S(1)} %bitcast.19), custom_call_target="tpu_custom_call" | custom-call | flops 600000000 | bytes 1300000 | tf_op jit(solution)/shard_map/pallas_call | solution.py:53
  68.0 7.5 %all-to-all-done.1 = bf16[128,8,128]{2,1,0:T(8,128)(2,1)S(1)} async-done(((bf16[128,8,128]{2,1,0:T(8,128)(2,1)}), bf16[128,8,128]{2,1,0:T(8,128)(2,1)S(1)}, u32[]{:S(2)}, u32[]{:S(2)}) %all-to-all-start.1) | async-done | bytes 262176 | tf_op jit(solution)/shard_map/all_to_all | solution.py:729
  75.6 1.4 %shard_map.111 = f32[2,384,128]{2,1,0:T(8,128)} custom-call(f32[2,384,128]{2,1,0:T(8,128)S(1)} %copy-done, bf16[1024,128]{1,0:T(8,128)(2,1)S(1)} %bitcast.14, s32[2,384]{1,0:T(2,128)S(1)} %copy-done.4), custom_call_target="tpu_custom_call" | custom-call | flops 4000000 | bytes 1500000 | tf_op jit(solution)/shard_map/pallas_call | solution.py:53
  77.0 0.0 collective-permute-done.7.inner_hbm
  77.0 0.0 collective-permute-done.8.outer_hbm
  77.0 0.0 copy-done.2
  77.0 18.7 %shard_map.110 = bf16[3,1152,256]{2,1,0:T(8,128)(2,1)} custom-call(s32[4]{0:T(128)S(1)} %pad_add_fusion.ids_ref, s32[13824]{0:T(1024)S(1)} %bitcast.16, f32[4608,128]{1,0:T(8,128)} %get-tuple-element.21.coef_hbm, f32[2,1152,128]{2,1,0:T(8,128)} %get-tuple-element.22.speeds_hbm, bf16[8,2,144,128]{3,2,1,0:T(8,128)(2,1)} %collective-permute-done.7.inner_hbm, ...), custom_call_target="tpu_custom_call" | custom-call | flops 40000000 | bytes 8000000 | tf_op jit(solution)/shard_map/pallas_call | solution.py:53
Async XLA Ops:
  0.7 36.8 %copy-start = (f32[2,384,128]{2,1,0:T(8,128)S(1)}, f32[2,384,128]{2,1,0:T(8,128)}, u32[]{:S(2)}) copy-start(f32[2,384,128]{2,1,0:T(8,128)} %currents_ref.3) | copy-start | bytes 1179652
  0.7 36.8 %copy-start.4 = (s32[2,384]{1,0:T(2,128)S(1)}, s32[2,384]{1,0:T(2,128)}, u32[]{:S(2)}) copy-start(s32[2,384]{1,0:T(2,128)} %wet_ref.5) | copy-start | bytes 9220
  0.7 36.8 %copy-start.5 = (f32[2,144]{1,0:T(2,128)S(1)}, f32[2,144]{1,0:T(2,128)}, u32[]{:S(2)}) copy-start(f32[2,144]{1,0:T(2,128)} %speed_ref.1) | copy-start | bytes 3460
  0.7 49.7 %copy-start.6 = (s32[128]{0:T(128)S(1)}, s32[128]{0:T(128)}, u32[]{:S(2)}) copy-start(s32[128]{0:T(128)} %param.15) | copy-start | bytes 1540
  4.1 6.7 %collective-permute-start = (bf16[6,144,128]{2,1,0:T(8,128)(2,1)}, bf16[6,144,128]{2,1,0:T(8,128)(2,1)S(1)}, u32[]{:S(2)}, u32[]{:S(2)}) collective-permute-start(bf16[6,144,128]{2,1,0:T(8,128)(2,1)} %get-tuple-element.24), channel_id=1, source_target_pairs={{0,1},{1,0},{2,3},{3,2},{4,5},{5,4},{6,7},{7,6},{8,9},{9,8},{10,11... | collective-permute-start | bytes 663560 | tf_op jit(solution)/shard_map/ppermute | solution.py:650
  5.6 7.9 %collective-permute-start.2 = (bf16[6,144,128]{2,1,0:T(8,128)(2,1)}, bf16[6,144,128]{2,1,0:T(8,128)(2,1)S(1)}, u32[]{:S(2)}, u32[]{:S(2)}) collective-permute-start(bf16[6,144,128]{2,1,0:T(8,128)(2,1)} %get-tuple-element.26), channel_id=1, source_target_pairs={{0,3},{1,2},{2,1},{3,0},{4,7},{5,6},{6,5},{7,4},{8,11},{9,10},{10,... | collective-permute-start | bytes 663560 | tf_op jit(solution)/shard_map/ppermute | solution.py:650
  6.9 27.5 %collective-permute-start.1 = (bf16[7,144,128]{2,1,0:T(8,128)(2,1)}, bf16[7,144,128]{2,1,0:T(8,128)(2,1)S(1)}, u32[]{:S(2)}, u32[]{:S(2)}) collective-permute-start(bf16[7,144,128]{2,1,0:T(8,128)(2,1)} %get-tuple-element.25), channel_id=1, source_target_pairs={{0,2},{1,3},{2,0},{3,1},{4,6},{5,7},{6,4},{7,5},{8,10},{9,11},{10,... | collective-permute-start | bytes 774152 | tf_op jit(solution)/shard_map/ppermute | solution.py:650
  7.0 27.4 %collective-permute-start.3 = (bf16[7,144,128]{2,1,0:T(8,128)(2,1)}, bf16[7,144,128]{2,1,0:T(8,128)(2,1)S(1)}, u32[]{:S(2)}, u32[]{:S(2)}) collective-permute-start(bf16[7,144,128]{2,1,0:T(8,128)(2,1)} %get-tuple-element.27), channel_id=1, source_target_pairs={{0,4},{1,5},{2,6},{3,7},{4,0},{5,1},{6,2},{7,3},{8,12},{9,13},{10,... | collective-permute-start | bytes 774152 | tf_op jit(solution)/shard_map/ppermute | solution.py:650
  10.0 24.4 %collective-permute-start.5 = (bf16[7,144,128]{2,1,0:T(8,128)(2,1)}, bf16[7,144,128]{2,1,0:T(8,128)(2,1)S(1)}, u32[]{:S(2)}, u32[]{:S(2)}) collective-permute-start(bf16[7,144,128]{2,1,0:T(8,128)(2,1)} %get-tuple-element.29), channel_id=1, source_target_pairs={{0,6},{1,7},{2,4},{3,5},{4,2},{5,3},{6,0},{7,1},{8,14},{9,15},{10,... | collective-permute-start | bytes 774152 | tf_op jit(solution)/shard_map/ppermute | solution.py:650
  10.8 20.6 %collective-permute-start.4 = (bf16[6,144,128]{2,1,0:T(8,128)(2,1)}, bf16[6,144,128]{2,1,0:T(8,128)(2,1)S(1)}, u32[]{:S(2)}, u32[]{:S(2)}) collective-permute-start(bf16[6,144,128]{2,1,0:T(8,128)(2,1)} %get-tuple-element.28), channel_id=1, source_target_pairs={{0,5},{1,4},{2,7},{3,6},{4,1},{5,0},{6,3},{7,2},{8,13},{9,12},{10,... | collective-permute-start | bytes 663560 | tf_op jit(solution)/shard_map/ppermute | solution.py:650
  13.5 20.9 %collective-permute-start.6 = (bf16[6,144,128]{2,1,0:T(8,128)(2,1)}, bf16[6,144,128]{2,1,0:T(8,128)(2,1)S(1)}, u32[]{:S(2)}, u32[]{:S(2)}) collective-permute-start(bf16[6,144,128]{2,1,0:T(8,128)(2,1)} %get-tuple-element.30), channel_id=1, source_target_pairs={{0,7},{1,6},{2,5},{3,4},{4,3},{5,2},{6,1},{7,0},{8,15},{9,14},{10,... | collective-permute-start | bytes 663560 | tf_op jit(solution)/shard_map/ppermute | solution.py:650
  35.3 29.2 %copy-start.1 = (s32[3,4608]{1,0:T(4,128)S(1)}, s32[3,4608]{1,0:T(4,128)}, u32[]{:S(2)}) copy-start(s32[3,4608]{1,0:T(4,128)} %pair_ref.1) | copy-start | bytes 165892
  35.3 29.2 %copy-start.3 = (f32[4608]{0:T(1024)S(1)}, f32[4608]{0:T(1024)}, u32[]{:S(2)}) copy-start(f32[4608]{0:T(1024)} %param.13) | copy-start | bytes 55300
  35.3 41.6 %collective-permute-start.7 = (bf16[8,2,144,128]{3,2,1,0:T(8,128)(2,1)}, bf16[8,2,144,128]{3,2,1,0:T(8,128)(2,1)}, u32[]{:S(2)}, u32[]{:S(2)}) collective-permute-start(bf16[8,2,144,128]{3,2,1,0:T(8,128)(2,1)} %get-tuple-element.31), channel_id=1, source_target_pairs={{0,1},{1,0},{2,3},{3,2},{4,5},{5,4},{6,7},{7,6},{8,9},{9,8},{10,11... | collective-permute-start | bytes 1769480 | tf_op jit(solution)/shard_map/ppermute | solution.py:707
  35.3 41.6 %collective-permute-start.8 = (bf16[8,2,144,128]{3,2,1,0:T(8,128)(2,1)S(1)}, bf16[8,2,144,128]{3,2,1,0:T(8,128)(2,1)}, u32[]{:S(2)}, u32[]{:S(2)}) collective-permute-start(bf16[8,2,144,128]{3,2,1,0:T(8,128)(2,1)S(1)} %get-tuple-element.32), channel_id=1, source_target_pairs={{1,2},{3,4},{5,6},{7,8},{9,10},{11,12},{13,14},{15,16},{17,18},{19... | collective-permute-start | bytes 1769480 | tf_op jit(solution)/shard_map/ppermute | solution.py:705
  37.4 13.1 %collective-permute-start.9 = (bf16[4,144,128]{2,1,0:T(8,128)(2,1)S(1)}, bf16[4,144,128]{2,1,0:T(8,128)(2,1)S(1)}, u32[]{:S(2)}, u32[]{:S(2)}) collective-permute-start(bf16[4,144,128]{2,1,0:T(8,128)(2,1)S(1)} %get-tuple-element.34), channel_id=1, source_target_pairs={{0,1},{1,0},{2,3},{3,2},{4,5},{5,4},{6,7},{7,6},{8,9},{9,8},{10,11... | collective-permute-start | bytes 442376 | tf_op jit(solution)/shard_map/ppermute | solution.py:708
  39.3 20.8 %all-to-all-start = ((f32[128,1,128]{2,1,0:T(1,128)}), f32[128,1,128]{2,1,0:T(1,128)S(1)}, u32[]{:S(2)}, u32[]{:S(2)}) async-start(f32[128,1,128]{2,1,0:T(1,128)} %bitcast.7), calls=%async_computation | async-start | bytes 131072 | tf_op jit(solution)/shard_map/all_to_all | solution.py:662
  60.1 15.5 %all-to-all-start.1 = ((bf16[128,8,128]{2,1,0:T(8,128)(2,1)}), bf16[128,8,128]{2,1,0:T(8,128)(2,1)S(1)}, u32[]{:S(2)}, u32[]{:S(2)}) async-start(bf16[128,8,128]{2,1,0:T(8,128)(2,1)} %bitcast.21), calls=%async_computation.1 | async-start | bytes 524288 | tf_op jit(solution)/shard_map/all_to_all | solution.py:729
  64.5 12.5 %copy-start.2 = (s32[24,256]{1,0:T(8,128)S(1)}, s32[24,256]{1,0:T(8,128)}, u32[]{:S(2)}) copy-start(s32[24,256]{1,0:T(8,128)} %wet_ref.4) | copy-start | bytes 73732
